TPU v7x, 32 devices: a whole 2x2x4 slice. The times are simulated.
32 devices in a mesh: section: 4 (over z), dp: 8 (over y, x, core).
Axes of the slice: x: 2, y: 2, z: 4, core: 2. Of those that a mesh axis runs over, the one named last changes fastest.
Arguments:
- held: bfloat16 [4, 2, 1024, 2048], P('section', None, 'dp'), may hold values from -70 to 70
- norm_gain: float32 [4, 2048], P('section'), may hold values from 0.3 to 3
- w_qkv: bfloat16 [4, 2048, 2560], P('section', None, 'dp'), may hold values from -1 to 1
- q_gain: float32 [4, 128], P('section'), may hold values from 0.5 to 7
- k_gain: float32 [4, 128], P('section'), may hold values from 0.5 to 7
- w_out: bfloat16 [4, 2048, 2048], P('section', None, 'dp'), may hold values from -0.125 to 0.125
- lengths: int32 [4, 2, 8], P('section'), may hold values from 1 to 512, 1024 in all within a row
Outputs:
- handed: bfloat16 [4, 2, 1024, 2048], P('section', None, 'dp')
Inputs may be any that keep to these rules, and one draw needn't show every extreme that they name: Each row lists the 8 document lengths of one packed micro-batch in order; they sum to 1024 and the longest is exactly 512.
All inputs are finite; a program needn't handle non-finite values.
Results may differ from a plain program's by a relative error of at most 0.0086.
Values may be sent and summed in bfloat16 or wider, within the bound.
No kernel may reach another device: no remote copies, remote signals or barrier semaphores. Data moves between devices by JAX's collectives and lax.ppermute only.
A program may use at most 128 MiB of HBM per device.

v0:
```python
import math

import jax
import jax.numpy as jnp
from jax import lax
from jax.sharding import PartitionSpec as P

HEADS = 16
KV_HEADS = 2
HEAD = 128
GROUP = 8


EPSILON = 1e-06
THETA = 1000000.0
NEGATIVE = -1e30


def from_behind(value, axis, steps):
    count = lax.axis_size(axis)
    pairs = [(source, (source + steps) % count) for source in range(count)]
    return lax.ppermute(value, axis, pairs)


def rms_scale(values, gain):
    return values * lax.rsqrt(jnp.mean(values * values, axis=-1, keepdims=True) + EPSILON) * gain


def rotary(values, places):
    width = values.shape[-1]
    middle = width // 2
    spacing = jnp.exp(jnp.arange(middle, dtype=jnp.float32) * (-2.0 * math.log(THETA) / width))
    angle = places.astype(jnp.float32)[..., None] * spacing
    cosine = jnp.cos(angle)[..., None, :]
    sine = jnp.sin(angle)[..., None, :]
    former = values[..., :middle]
    latter = values[..., middle:]
    return jnp.concatenate(
        [former * cosine - latter * sine, latter * cosine + former * sine], axis=-1
    )


def locate(positions, doc_lengths):
    ends = jnp.cumsum(doc_lengths, axis=-1)
    before = (ends[:, None, :] <= positions[None, :, None]).astype(jnp.int32)
    return (jnp.sum(before, axis=-1), jnp.sum(before * doc_lengths[:, None, :], axis=-1))


def attend_rows(query_rows, key_rows, value_rows, allowed):
    scores = jnp.einsum(
        "kqd,nkd->kqn", query_rows, key_rows, preferred_element_type=jnp.float32
    ) / math.sqrt(HEAD)
    highest = jnp.max(jnp.where(allowed[None], scores, NEGATIVE), axis=-1)
    weights = jnp.where(allowed[None], jnp.exp(scores - highest[..., None]), 0.0).astype(
        jnp.bfloat16
    )
    total = jnp.sum(weights.astype(jnp.float32), axis=-1)
    summed = jnp.einsum("kqn,nkd->kqd", weights, value_rows, preferred_element_type=jnp.float32)
    return summed / total[..., None]


def on_device(held, norm_gain, w_qkv, q_gain, k_gain, w_out, lengths):
    micro = held.shape[1]
    rows = held.shape[2]
    width = held.shape[3]
    inner = HEADS * HEAD
    key_width = KV_HEADS * HEAD
    middle = rows // 2
    devices = lax.axis_size("dp")
    here = lax.axis_index("dp")
    total_tokens = rows * devices
    doc_most = min(4096, total_tokens // 2)
    reach = min(total_tokens, doc_most + middle)
    doc_lengths = lengths[0]
    resident = held[0].astype(jnp.float32).reshape(micro * rows, width)
    normed = rms_scale(resident, norm_gain[0]).astype(jnp.bfloat16)
    projected = jnp.dot(
        normed,
        lax.all_gather(w_qkv[0], "dp", axis=1, tiled=True),
        preferred_element_type=jnp.float32,
    ).reshape(micro, rows, inner + 2 * key_width)
    own_index = here * rows + jnp.arange(rows, dtype=jnp.int32)
    own_start = locate(own_index, doc_lengths)[1]
    places = own_index[None, :] - own_start
    queries = rotary(
        rms_scale(projected[..., :inner].reshape(micro, rows, HEADS, HEAD), q_gain[0]), places
    ).astype(jnp.bfloat16)
    keys = rotary(
        rms_scale(
            projected[..., inner : inner + key_width].reshape(micro, rows, KV_HEADS, HEAD),
            k_gain[0],
        ),
        places,
    ).astype(jnp.bfloat16)
    values = projected[..., inner + key_width :].astype(jnp.bfloat16)
    packed = jnp.concatenate([keys.reshape(micro, rows, key_width), values], axis=-1)
    gathered = lax.all_gather(packed, "dp", axis=1, tiled=True)
    latter_queries = queries[:, middle:]
    latter_index = own_index[middle:]
    group_index = jnp.stack([own_index[:middle], latter_index])
    group_doc = locate(group_index.reshape(-1), doc_lengths)[0].reshape(micro, 2, middle)
    arranged = jnp.stack([queries[:, :middle], latter_queries], axis=1)
    arranged = arranged.reshape(micro, 2, middle, KV_HEADS, GROUP, HEAD).transpose(0, 1, 3, 4, 2, 5)
    arranged = arranged.reshape(micro, 2, KV_HEADS, GROUP * middle, HEAD)
    row_index = jnp.tile(group_index, (1, GROUP))
    row_doc = jnp.tile(group_doc, (1, 1, GROUP))
    finished = []
    for which_micro in range(micro):
        for which_half in range(2):
            first = group_index[which_half, 0]
            key_first = jnp.clip(first + middle - reach, 0, total_tokens - reach)
            window = lax.dynamic_slice_in_dim(gathered[which_micro], key_first, reach, 0)
            key_index = key_first + jnp.arange(reach, dtype=jnp.int32)
            key_doc = locate(key_index, doc_lengths[which_micro : which_micro + 1])[0][0]
            key_part = window[:, :key_width].reshape(reach, KV_HEADS, HEAD)
            value_part = window[:, key_width:].reshape(reach, KV_HEADS, HEAD)
            allowed = (row_doc[which_micro, which_half][:, None] == key_doc[None, :]) & (
                row_index[which_half][:, None] >= key_index[None, :]
            )
            ratio = attend_rows(
                arranged[which_micro, which_half], key_part, value_part, allowed
            ).astype(jnp.bfloat16)
            finished.append(
                ratio.reshape(KV_HEADS, GROUP, middle, HEAD)
                .transpose(2, 0, 1, 3)
                .reshape(middle, inner)
            )
    former_part = jnp.stack(finished[0::2])
    latter_part = jnp.stack(finished[1::2])
    attended = jnp.concatenate([former_part, latter_part], axis=1).reshape(micro * rows, inner)
    mixed = jnp.dot(
        attended,
        lax.all_gather(w_out[0], "dp", axis=1, tiled=True),
        preferred_element_type=jnp.float32,
    )
    result = (resident + mixed).astype(jnp.bfloat16).reshape(1, micro, rows, width)
    return from_behind(result, "section", 1)


def solution(mesh):
    in_specs = (
        P("section", None, "dp", None),
        P("section", None),
        P("section", None, "dp"),
        P("section", None),
        P("section", None),
        P("section", None, "dp"),
        P("section", None, None),
    )
    out_specs = P("section", None, "dp", None)
    return jax.shard_map(
        on_device, mesh=mesh, in_specs=in_specs, out_specs=out_specs, check_vma=False
    )
```

profile of v0, /device:TPU:0, one launch (start us, length us, event | category | flops | bytes accessed | tf_op | source)
XLA Modules:
  0.0 210.5 jit_solution(9987172462694645910)
XLA Ops:
  6.5 0.7 all-gather.8.cloned.1.call-update
  7.9 0.9 reduce_window_sum.26
  8.8 0.8 convert_reduce_fusion.8
  9.5 1.5 multiply_reduce_fusion
  11.1 0.5 multiply_cosine_fusion
  11.6 63.5 %all-gather.8.cloned.1.call-done = bf16[1,2048,2560]{1,2,0:T(8,128)(2,1)} async-done(((bf16[1,2048,320]{1,2,0:T(8,128)(2,1)}), bf16[1,2048,2560]{1,2,0:T(8,128)(2,1)}) %all-gather.8.cloned.1.call-update) | async-done | bytes 10485776 | tf_op jit(solution)/shard_map/all_gather | solution.py:79
  75.1 6.0 %fusion.4 = f32[2,128,2560]{2,1,0:T(8,128)S(1)} fusion(bf16[1,2048,2560]{1,2,0:T(8,128)(2,1)} %all-gather.8.cloned.1.call-done, bf16[1,2,128,2048]{3,2,1,0:T(8,128)(2,1)} %param.7, f32[2048]{0:T(1024)S(1)} %bitcast.185, f32[2,128]{1,0:T(2,128)S(1)} %add_rsqrt_fusion.2), kind=kOutput, calls=%fused_computation.4 | convolution fusion | flops 2686451712 | bytes 14164992 | tf_op jit(solution)/shard_map/dot_general | solution.py:77
  81.7 1.0 multiply_multiply_fusion
  82.7 0.5 subtract_convert_fusion.1
  83.6 0.7 pad_maximum_fusion.2
  84.4 0.7 all-gather.10.cloned.1.call-update
  86.0 2.1 %compare_and_fusion.1 = (pred[512,576]{0,1:T(8,128)(4,1)}, pred[512,576]{0,1:T(8,128)(4,1)S(1)}, pred[512,576]{0,1:T(8,128)(4,1)}, pred[512,576]{0,1:T(8,128)(4,1)}) fusion(s32[512]{0:T(512)S(1)} %ge.62, s32[512]{0:T(512)S(1)} %bitcast.176, s32[576]{0:T(1024)S(1)} %iota_add_fusion, s32[576]{0:T(1024)S(1)} %get-tuple-element.7, s32[576]{0:T(1024)S(1)} %get-tuple-element.8, ...), kind=kLoop, calls=%fused_computation.41 | loop fusion | flops 2949120 | bytes 1205760 | tf_op jit(solution)/shard_map/and | solution.py:117
  88.7 0.6 fusion.18
  89.5 0.9 fusion.19
  90.4 0.8 subtract_convert_fusion
  91.2 0.6 fusion.55
  92.2 20.1 %all-gather.6.cloned.1.call-done = bf16[2,1024,512]{2,1,0:T(8,128)(2,1)} async-done(((bf16[2,128,512]{2,1,0:T(8,128)(2,1)}), bf16[2,1024,512]{2,1,0:T(8,128)(2,1)}) %all-gather.6.cloned.1.call-update) | async-done | bytes 2097168 | tf_op jit(solution)/shard_map/all_gather | solution.py:97
  112.3 1.7 fusion.85
  114.0 0.6 dynamic-slice_bitcast_fusion.2
  115.2 1.3 convert_reduce_fusion
  116.5 0.7 fusion.37
  118.4 1.3 convert_reduce_fusion.1
  119.8 0.7 fusion.36
  121.6 1.3 convert_reduce_fusion.2
  123.0 0.7 fusion.35
  124.8 1.5 convert_reduce_fusion.3
  126.4 0.7 fusion.34
  127.5 42.6 %all-gather.10.cloned.1.call-done = bf16[1,2048,2048]{2,1,0:T(8,128)(2,1)} async-done(((bf16[1,2048,256]{2,1,0:T(8,128)(2,1)}), bf16[1,2048,2048]{2,1,0:T(8,128)(2,1)}) %all-gather.10.cloned.1.call-update) | async-done | bytes 8388624 | tf_op jit(solution)/shard_map/all_gather | solution.py:133
  170.1 5.7 %fusion.11 = bf16[256,2048]{1,0:T(8,128)(2,1)S(1)} fusion(bf16[256,2048]{1,0:T(8,128)(2,1)S(1)} %bitcast.163, bf16[1,2048,2048]{2,1,0:T(8,128)(2,1)} %all-gather.10.cloned.1.call-done, bf16[256,2048]{1,0:T(8,128)(2,1)S(1)} %bitcast.162), kind=kOutput, calls=%fused_computation.9 | convolution fusion | flops 2149056512 | bytes 11534336 | tf_op jit(solution)/shard_map/dot_general | solution.py:131
  175.8 1.5 collective-permute-start
  177.4 25.6 %collective-permute-done = bf16[1,2,128,2048]{3,2,1,0:T(8,128)(2,1)S(1)} collective-permute-done((bf16[1,2,128,2048]{3,2,1,0:T(8,128)(2,1)S(1)}, bf16[1,2,128,2048]{3,2,1,0:T(8,128)(2,1)S(1)}, u32[]{:S(2)}, u32[]{:S(2)}) %collective-permute-start) | collective-permute-done | bytes 1048608 | tf_op jit(solution)/shard_map/ppermute | solution.py:22
  203.0 1.0 copy.143
  (75 shorter events, 8.1 us)
Async XLA Ops:
  6.5 68.6 %copy-start.8 = (f32[1,2048]{1,0:T(1,128)S(1)}, f32[1,2048]{1,0:T(1,128)}, u32[]{:S(2)}) copy-start(f32[1,2048]{1,0:T(1,128)} %param.8) | copy-start | bytes 24580
  6.5 68.6 %all-gather.8.cloned.1.call-start = ((), (), s32[]{:S(2)}) async-start(), calls=%async_computation.1 | async-start | bytes 11796480 | tf_op jit(solution)/shard_map/all_gather | solution.py:79
  7.3 105.1 %all-gather.6.cloned.1.call-start = ((), (), s32[]{:S(2)}) async-start(), calls=%async_computation | async-start | bytes 2359296 | tf_op jit(solution)/shard_map/all_gather | solution.py:97
  7.4 0.5 copy-start.5
  81.3 3.8 %copy-start.6 = (s32[1,64]{1,0:T(1,128)S(1)}, s32[1,64]{1,0:T(1,128)}, u32[]{:S(2)}) copy-start(s32[1,64]{1,0:T(1,128)} %copy-done.5) | copy-start | bytes 772
  81.6 3.8 %copy-start.4 = (s32[1,2,8]{2,1,0:T(2,128)S(1)}, s32[1,2,8]{2,1,0:T(2,128)}, u32[]{:S(2)}) copy-start(s32[1,2,8]{2,1,0:T(2,128)} %param.13) | copy-start | bytes 196
  84.4 85.7 %all-gather.10.cloned.1.call-start = ((), (), s32[]{:S(2)}) async-start(), calls=%async_computation.2 | async-start | bytes 9437184 | tf_op jit(solution)/shard_map/all_gather | solution.py:133
  88.3 1.2 copy-start.7
  117.5 1.0 copy-start.3
  120.6 1.0 copy-start.2
  123.8 1.0 copy-start.1
  127.1 43.1 %copy-start = (bf16[1,2,128,2048]{3,2,1,0:T(8,128)(2,1)S(1)}, bf16[1,2,128,2048]{3,2,1,0:T(8,128)(2,1)}, u32[]{:S(2)}) copy-start(bf16[1,2,128,2048]{3,2,1,0:T(8,128)(2,1)} %param.7) | copy-start | bytes 3145732
  175.8 27.2 %collective-permute-start = (bf16[1,2,128,2048]{3,2,1,0:T(8,128)(2,1)S(1)}, bf16[1,2,128,2048]{3,2,1,0:T(8,128)(2,1)S(1)}, u32[]{:S(2)}, u32[]{:S(2)}) collective-permute-start(bf16[1,2,128,2048]{3,2,1,0:T(8,128)(2,1)S(1)} %bitcast.184), channel_id=1, source_target_pairs={{0,8},{8,16},{16,24},{24,0},{1,9},{9,17},{17,25},{25,1},{2,10},{10... | collective-permute-start | bytes 3145736 | tf_op jit(solution)/shard_map/ppermute | solution.py:22
Sparse Core Ops, SparseCore 0:
  9.2 65.8 all-gather.7
  84.5 27.8 all-gather.5
  114.2 55.8 all-gather.9
where the time goes:
time: 211 us; the launch traced here: 210 us
  waiting for transfers between devices  153 us (73%)
  other arithmetic  17.7 us (8%)
  matrix products  16.3 us (8%)
  between operations  13.6 us (6%)
  local copies, waits for them, and re-layouts  7.9 us (4%)
    all_gather x1, waiting for transfers between devices, on_device(): lax.all_gather(w_qkv[0], 'dp', axis=1, tiled=True)  63.5 us
    all_gather x1, waiting for transfers between devices, on_device(): lax.all_gather(w_out[0], 'dp', axis=1, tiled=True)  42.6 us
    ppermute x1, waiting for transfers between devices, from_behind(): return lax.ppermute(value, axis, pairs)  25.6 us
    all_gather x1, waiting for transfers between devices, on_device(): gathered = lax.all_gather(packed, 'dp', axis=1, tiled=True)  20.1 us
    dot_general x1, matrix products, on_device(): jnp.dot(normed, lax.all_gather(w_qkv[0], 'dp', axis=1, tiled=True), prefe...  5.95 us
    dot_general x1, matrix products, on_device(): jnp.dot(attended, lax.all_gather(w_out[0], 'dp', axis=1, tiled=True), pre...  5.71 us
    sub x4, other arithmetic, attend_rows(): scores - highest[..., None]  5.49 us
  transfers between devices with their start and end apart: 4, of which 4 were waited for; matrix products, arithmetic and copies ran while one was open for 12% of the time, Pallas kernels for 0%

commit v1 on v0

--- a/solution.py
+++ b/solution.py
@@ -1,8 +1,11 @@
+import functools
 import math
 
 import jax
 import jax.numpy as jnp
 from jax import lax
+from jax.experimental import pallas as pl
+from jax.experimental.pallas import tpu as pltpu
 from jax.sharding import PartitionSpec as P
 
 HEADS = 16
@@ -137,7 +140,570 @@
     return from_behind(result, "section", 1)
 
 
+MIB = 1 << 20
+VMEM = pl.BlockSpec(memory_space=pltpu.VMEM)
+SMEM = pl.BlockSpec(memory_space=pltpu.SMEM)
+
+
+def local_kernel(body, outs, inputs, scratch=(), flops=0, grant=24, scalars=1):
+    moved = sum(math.prod(s.shape) * s.dtype.itemsize for s in (*outs, *inputs))
+    return pl.pallas_call(
+        body,
+        out_shape=tuple(outs),
+        in_specs=[SMEM] * scalars + [VMEM] * (len(inputs) - scalars),
+        out_specs=tuple(VMEM for _ in outs),
+        scratch_shapes=list(scratch),
+        compiler_params=pltpu.CompilerParams(vmem_limit_bytes=grant * MIB),
+        cost_estimate=pl.CostEstimate(flops=flops, bytes_accessed=moved, transcendentals=0),
+    )(*inputs)
+
+
+def prepare_kernel(
+    here_ref,
+    lengths_ref,
+    spacing_ref,
+    w_ref,
+    place_ref,
+    bias_ref,
+    cos_ref,
+    sin_ref,
+    here_out,
+    there_out,
+):
+    here = here_ref[0]
+    line, column, core = here >> 2, (here >> 1) & 1, here & 1
+    chip = here >> 1
+    half = here_out.shape[0]
+    here_out[...] = w_ref[pl.ds(pl.multiple_of(line * half, half), half), :]
+    there_out[...] = w_ref[pl.ds(pl.multiple_of((1 - line) * half, half), half), :]
+    documents = lengths_ref.shape[1]
+    sizes = [lengths_ref[core, j] for j in range(documents)]
+    ends = [sizes[0]]
+    for size in sizes[1:]:
+        ends.append(ends[-1] + size)
+
+    def locate_in(index):
+        number = jnp.zeros_like(index)
+        start = jnp.zeros_like(index)
+        for end, size in zip(ends, sizes):
+            past = (end <= index).astype(jnp.int32)
+            number = number + past
+            start = start + past * size
+        return number, start
+
+    rows = cos_ref.shape[0] // 4
+    lane = lax.broadcasted_iota(jnp.int32, (1, rows), 1)
+    keys = []
+    for bits in (0, 1, 4, 5, 2, 3, 6, 7):
+        index = (here ^ bits) * rows + lane
+        keys.append((index, locate_in(index)[0]))
+    first_half = lax.broadcasted_iota(jnp.int32, (rows, HEAD), 1) < HEAD // 2
+    for block, bits in enumerate((0, 1, 4, 5)):
+        span = slice(block * rows, (block + 1) * rows)
+        index = (here ^ bits) * rows + lax.broadcasted_iota(jnp.int32, (rows, HEAD), 0)
+        number, start = locate_in(index)
+        angle = (index - start).astype(jnp.float32) * spacing_ref[...]
+        sine = jnp.sin(angle)
+        cos_ref[span, :] = jnp.cos(angle)
+        sin_ref[span, :] = jnp.where(first_half, -sine, sine)
+        for other, (key_index, key_number) in enumerate(keys):
+            allowed = (number[:, :1] == key_number) & (index[:, :1] >= key_index)
+            bias_ref[span, other * rows : (other + 1) * rows] = jnp.where(
+                allowed, 0.0, NEGATIVE
+            ).astype(jnp.float32)
+
+    def number_at(index):
+        number = jnp.int32(0)
+        for end in ends:
+            number = number + jnp.where(end <= index, 1, 0)
+        return number
+
+    place_ref[0] = line
+    place_ref[1] = column
+    place_ref[2] = core
+    for row, row_bits in enumerate((0, 2)):
+        row_chip = chip ^ row_bits
+        for key, key_bits in enumerate((0, 2, 1, 3)):
+            key_chip = chip ^ key_bits
+            shares = number_at(key_chip * 2 * rows + 2 * rows - 1) >= number_at(row_chip * 2 * rows)
+            meets = (key_chip == row_chip) | ((key_chip < row_chip) & shares)
+            place_ref[3 + 4 * row + key] = jnp.where(meets, 1, 0)
+
+
+def project_block(projected, head, cosine, sine, gains_ref):
+    is_value = head >= HEADS + KV_HEADS
+    is_query = head < HEADS
+    gain = jnp.where(is_query, gains_ref[0][...], gains_ref[1][...])
+    scale = lax.rsqrt(jnp.mean(projected * projected, axis=-1, keepdims=True) + EPSILON)
+    v = projected * scale * gain
+    turned = v * cosine + pltpu.roll(v, HEAD // 2, 1) * sine
+    return jnp.where(is_value, projected, turned).astype(jnp.bfloat16)
+
+
+def project_with(normed, w_own, w_partner, middle, core, write):
+    part = w_own.shape[0]
+    whole = part // HEAD
+    rest = part - whole * HEAD
+    spread = whole + 1 if rest else whole
+    for piece, turn in ((w_own, core), (w_partner, 1 - core)):
+        start = pl.multiple_of(turn * rest, rest) if rest else 0
+        projected = lax.dot_general(
+            normed,
+            piece[pl.ds(start, whole * HEAD), :],
+            (((1,), (1,)), ((), ())),
+            preferred_element_type=jnp.float32,
+        )
+        for block in range(whole):
+            write(turn * spread + block, projected[:, block * HEAD : (block + 1) * HEAD])
+    if rest:
+        projected = lax.dot_general(
+            normed, middle[...], (((1,), (1,)), ((), ())), preferred_element_type=jnp.float32
+        )
+        write(whole, projected)
+
+
+def join_middle(core, middle, w_own, w_partner):
+    part = w_own.shape[0]
+    rest = part % HEAD
+    if rest:
+        for piece, turn in ((w_own, core), (w_partner, 1 - core)):
+            there = pl.multiple_of(turn * rest, rest)
+            here = pl.multiple_of((1 - turn) * (part - rest), rest)
+            middle[pl.ds(there, rest), :] = piece[pl.ds(here, rest), :]
+
+
+def project_own_kernel(
+    offset,
+    place_ref,
+    x0_ref,
+    x1_ref,
+    gain_ref,
+    w_own,
+    w_partner,
+    cos_ref,
+    sin_ref,
+    q_gain_ref,
+    k_gain_ref,
+    out_ref,
+    normed_ref,
+    middle,
+):
+    line, column, core = place_ref[0], place_ref[1], place_ref[2]
+    rows = x0_ref.shape[1]
+    join_middle(core, middle, w_own, w_partner)
+    for number, x_ref in enumerate((x0_ref, x1_ref)):
+        x = x_ref[core].astype(jnp.float32)
+        scale = lax.rsqrt(jnp.mean(x * x, axis=-1, keepdims=True) + EPSILON)
+        normed_ref[number * rows : (number + 1) * rows, :] = (x * scale * gain_ref[...]).astype(
+            jnp.bfloat16
+        )
+    blocks = out_ref.shape[1] // HEAD
+    span = slice(offset, offset + 2 * rows)
+
+    def write(block, projected):
+        head = (line * 2 + column) * blocks + block
+        out_ref[:, pl.ds(pl.multiple_of(block * HEAD, HEAD), HEAD)] = project_block(
+            projected, head, cos_ref[span, :], sin_ref[span, :], (q_gain_ref, k_gain_ref)
+        )
+
+    project_with(normed_ref[...], w_own, w_partner, middle, core, write)
+
+
+def project_far_kernel(
+    place_ref,
+    normed0_ref,
+    normed1_ref,
+    w_own,
+    w_partner,
+    cos_ref,
+    sin_ref,
+    q_gain_ref,
+    k_gain_ref,
+    near0_ref,
+    near1_ref,
+    full,
+    swap_a_ref,
+    swap_b_ref,
+    kv_a_ref,
+    kv_b_ref,
+    middle,
+):
+    line, column, core = place_ref[0], place_ref[1], place_ref[2]
+    join_middle(core, middle, w_own, w_partner)
+    chip_width = near0_ref.shape[1]
+    blocks = chip_width // HEAD
+    which = 1 - column
+    step = normed0_ref.shape[0]
+    own = pl.multiple_of(column * chip_width, HEAD)
+    for number, (normed_ref, near_ref) in enumerate(
+        ((normed0_ref, near0_ref), (normed1_ref, near1_ref))
+    ):
+        span = slice(number * step, (number + 1) * step)
+        full[span, pl.ds(own, chip_width)] = near_ref[...]
+
+        def write(block, projected, span=span):
+            head = (line * 2 + which) * blocks + block
+            start = pl.multiple_of((which * blocks + block) * HEAD, HEAD)
+            full[span, pl.ds(start, HEAD)] = project_block(
+                projected, head, cos_ref[span, :], sin_ref[span, :], (q_gain_ref, k_gain_ref)
+            )
+
+        project_with(normed_ref[...], w_own, w_partner, middle, core, write)
+    inner = HEADS // 2 * HEAD
+    pair = swap_a_ref.shape[1]
+    half = pair // 2
+    left = inner - pair
+    first = pl.ds(pl.multiple_of(column * step, step), step)
+    second = pl.ds(pl.multiple_of((1 - column) * step, step), step)
+
+    @pl.when(line == 0)
+    def _():
+        swap_a_ref[...] = full[first, inner : inner + pair]
+        swap_b_ref[...] = full[second, inner : inner + pair]
+        kv_a_ref[...] = jnp.zeros_like(kv_a_ref)
+        kv_b_ref[...] = jnp.zeros_like(kv_b_ref)
+
+    @pl.when(line == 1)
+    def _():
+        for out, rows, skip in (
+            (swap_a_ref, first, 0),
+            (swap_b_ref, second, 0),
+            (kv_a_ref, second, half),
+            (kv_b_ref, first, half),
+        ):
+            out[:, :half] = full[rows, left + skip : left + skip + half]
+            out[:, half:] = full[rows, left + skip + pair : left + skip + pair + half]
+
+
+SHRINK = math.log2(math.e) / math.sqrt(HEAD)
+
+
+def with_ones(values):
+    return jnp.concatenate([values, jnp.ones_like(values)], axis=1)
+
+
+def query_of(head, part, place_ref, full_ref, swap_a_ref, swap_b_ref):
+    line, column = place_ref[0], place_ref[1]
+    rows = swap_a_ref.shape[0]
+    span = slice(part * rows, (part + 1) * rows)
+    moved = swap_a_ref.shape[1] // HEAD
+    lanes = slice(head * HEAD, (head + 1) * HEAD)
+    if head < moved:
+        came = jnp.where(column == 1 - part, swap_a_ref[:, lanes], swap_b_ref[:, lanes])
+        return jnp.where(line == 1, came, full_ref[span, lanes])
+    start = pl.multiple_of((head - moved * line) * HEAD, HEAD)
+    return full_ref[span, pl.ds(start, HEAD)]
+
+
+def scores_of(q, keys, bias):
+    return (
+        lax.dot_general(q, keys, (((1,), (1,)), ((), ())), preferred_element_type=jnp.float32)
+        + bias
+    )
+
+
+def attend_near_kernel(
+    part,
+    place_ref,
+    full_ref,
+    swap_a_ref,
+    swap_b_ref,
+    kv_a_ref,
+    kv_b_ref,
+    bias_ref,
+    sum_ref,
+    top_ref,
+    near,
+):
+    line, column = place_ref[0], place_ref[1]
+    rows = sum_ref.shape[0]
+    half = kv_a_ref.shape[1] // 2
+    heads = top_ref.shape[1] // HEAD
+    span = slice(part * rows, (part + 1) * rows)
+    for turn, swap_ref, kv_ref in ((1 - column, swap_a_ref, kv_a_ref), (column, swap_b_ref, kv_b_ref)):
+        start = pl.multiple_of(turn * rows, rows)
+        near[pl.ds(start, rows), :] = jnp.where(line == 0, swap_ref[...], kv_ref[...])
+
+    def attend(block):
+        keys = near[block, :half]
+        values = with_ones(near[block, half:])
+        bias = bias_ref[span, block]
+        for head in range(heads):
+            q = query_of(head, part, place_ref, full_ref, swap_a_ref, swap_b_ref)
+            s = scores_of(q, keys, bias)
+            top = jnp.max(s, axis=-1, keepdims=True)
+            weight = jnp.exp2((s - top) * SHRINK).astype(jnp.bfloat16)
+            sum_ref[:, 2 * head * HEAD : 2 * (head + 1) * HEAD] = jnp.dot(
+                weight, values, preferred_element_type=jnp.float32
+            )
+            top_ref[:, head * HEAD : (head + 1) * HEAD] = jnp.broadcast_to(top, (rows, HEAD))
+
+    both = place_ref[3 + part * 4 + 1 - part] == 1
+
+    @pl.when(both)
+    def _():
+        attend(slice(0, 2 * rows))
+
+    @pl.when(jnp.logical_not(both))
+    def _():
+        attend(span)
+
+
+def attend_far_kernel(
+    part,
+    place_ref,
+    full_ref,
+    swap_a_ref,
+    swap_b_ref,
+    far0_ref,
+    far1_ref,
+    bias_ref,
+    sum_ref,
+    top_ref,
+    out_ref,
+):
+    line, column = place_ref[0], place_ref[1]
+    rows = out_ref.shape[0]
+    half = far0_ref.shape[1] // 2
+    heads = top_ref.shape[1] // HEAD
+    span = slice(part * rows, (part + 1) * rows)
+    block = 2 + column if part == 1 else 3 - column
+    meets = place_ref[3 + part * 4 + block] == 1
+
+    def finish(head, summed):
+        out_ref[:, head * HEAD : (head + 1) * HEAD] = (
+            summed[:, :HEAD] / summed[:, HEAD:]
+        ).astype(jnp.bfloat16)
+
+    @pl.when(jnp.logical_not(meets))
+    def _():
+        for head in range(heads):
+            finish(head, sum_ref[:, 2 * head * HEAD : 2 * (head + 1) * HEAD])
+
+    @pl.when(meets)
+    def _():
+        far = jnp.where(line == 0, far0_ref[...], far1_ref[...])
+        keys = far[:, :half]
+        values = with_ones(far[:, half:])
+        bias = bias_ref[span, pl.ds(pl.multiple_of(block * rows, rows), rows)]
+        for head in range(heads):
+            q = query_of(head, part, place_ref, full_ref, swap_a_ref, swap_b_ref)
+            s = scores_of(q, keys, bias)
+            before = top_ref[:, head * HEAD : (head + 1) * HEAD]
+            top = jnp.maximum(before, jnp.max(s, axis=-1, keepdims=True))
+            wide = jnp.concatenate([top] * (rows // HEAD), axis=1)
+            weight = jnp.exp2((s - wide) * SHRINK).astype(jnp.bfloat16)
+            kept = jnp.exp2((before - top) * SHRINK)
+            kept = jnp.concatenate([kept, kept], axis=1)
+            summed = sum_ref[:, 2 * head * HEAD : 2 * (head + 1) * HEAD] * kept + jnp.dot(
+                weight, values, preferred_element_type=jnp.float32
+            )
+            finish(head, summed)
+
+
+def share_kernel(place_ref, a_ref, w0_ref, w1_ref, out_ref):
+    core = place_ref[2]
+    width = w0_ref.shape[1]
+    for turn, w_ref in enumerate((w0_ref, w1_ref)):
+        start = pl.multiple_of((core ^ turn) * width, HEAD)
+        out_ref[:, pl.ds(start, width)] = jnp.dot(
+            a_ref[...], w_ref[...], preferred_element_type=jnp.float32
+        ).astype(jnp.bfloat16)
+
+
+def finish_kernel(
+    relative, place_ref, a_ref, w0_ref, w1_ref, came_ref, x0_ref, x1_ref, own_ref, pair_ref
+):
+    chip = place_ref[0] * 2 + place_ref[1]
+    core = place_ref[2]
+    width = w0_ref.shape[1]
+    rows = own_ref.shape[0]
+    for turn, w_ref in enumerate((w0_ref, w1_ref)):
+        start = pl.multiple_of((core ^ turn) * width, HEAD)
+        mixed = jnp.dot(
+            a_ref[...], w_ref[...], preferred_element_type=jnp.float32
+        ) + came_ref[:, pl.ds(start, width)].astype(jnp.float32)
+        where = pl.multiple_of((chip ^ relative) * 2 * width + start, HEAD)
+        for number, (x_ref, out_ref) in enumerate(((x0_ref, own_ref), (x1_ref, pair_ref))):
+            out_ref[:, pl.ds(start, width)] = (
+                x_ref[core, :, pl.ds(where, width)].astype(jnp.float32)
+                + mixed[number * rows : (number + 1) * rows, :]
+            ).astype(jnp.bfloat16)
+
+
+def gather_kernel(place_ref, *refs):
+    out_ref = refs[-1]
+    chip = place_ref[0] * 2 + place_ref[1]
+    core = place_ref[2]
+    for turn in range(2):
+        for relative in range(4):
+            piece = refs[turn * 4 + relative]
+            width = piece.shape[1]
+            start = pl.multiple_of((chip ^ relative) * width, HEAD)
+            out_ref[core ^ turn, :, pl.ds(start, width)] = piece[...]
+
+
+def on_chip_grid(held, norm_gain, w_qkv, q_gain, k_gain, w_out, lengths):
+    micro, rows, width = held.shape[1:]
+    devices = lax.axis_size("dp")
+    sections = lax.axis_size("section")
+    here = lax.axis_index("dp")
+    inner = w_out.shape[1]
+    pair = KV_HEADS * HEAD
+
+    def swap(value, bits, among=range(8)):
+        return lax.ppermute(value, "dp", [(i, i ^ bits) for i in among])
+
+    def after(value, *others):
+        return lax.optimization_barrier((value, *others))[0]
+
+    kept = held[0]
+    w_in = w_qkv[0].T
+    w_across = swap(w_in, 2)
+    x_y = swap(kept, 4)
+    x_c = swap(kept, 1)
+    w_c = swap(w_in, 1)
+
+    w_o = w_out[0]
+    half = inner // 2
+    own_rows = micro * 2 * rows
+    spread = [-2.0 * math.log(THETA) / HEAD * (lane % (HEAD // 2)) for lane in range(HEAD)]
+    spacing = jnp.asarray([[math.exp(value) for value in spread]], jnp.float32)
+    f32, bf16 = jnp.float32, jnp.bfloat16
+    shape = jax.ShapeDtypeStruct
+    place, bias, cosine, sine, o_here, o_there = pl.pallas_call(
+        prepare_kernel,
+        out_shape=(
+            shape((11,), jnp.int32),
+            shape((own_rows, 2 * own_rows), f32),
+            shape((own_rows, HEAD), f32),
+            shape((own_rows, HEAD), f32),
+            shape((half, w_o.shape[1]), bf16),
+            shape((half, w_o.shape[1]), bf16),
+        ),
+        in_specs=[SMEM, SMEM, VMEM, VMEM],
+        out_specs=(SMEM, VMEM, VMEM, VMEM, VMEM, VMEM),
+        compiler_params=pltpu.CompilerParams(vmem_limit_bytes=12 * MIB),
+    )(here[None], lengths[0], spacing, w_o)
+    o_here_c = swap(o_here, 1)
+
+    part = w_in.shape[0]
+    flops = 2 * own_rows * width * 2 * part
+    chip_rows = own_rows // 2
+
+    def project_own(offset, gain, first, second):
+        return local_kernel(
+            functools.partial(project_own_kernel, offset),
+            [shape((chip_rows, 2 * part), bf16), shape((chip_rows, width), bf16)],
+            [place, first, second, gain, w_in, w_c, cosine, sine, q_gain, k_gain],
+            [pltpu.VMEM((HEAD, width), bf16)],
+            flops // 2,
+        )
+
+    near0, normed0 = project_own(0, norm_gain, kept, x_c)
+    x_y, near0 = lax.optimization_barrier((x_y, near0))
+    x_yc = swap(x_y, 1)
+    near1, normed1 = project_own(chip_rows, norm_gain, x_y, x_yc)
+    o_y = swap(o_there, 4)
+    w_across_c = swap(after(w_across, x_yc), 1)
+    full, swapping_a, swapping_b, kv_a, kv_b = local_kernel(
+        project_far_kernel,
+        [shape((own_rows, 4 * part), bf16)] + [shape((chip_rows, pair), bf16)] * 4,
+        [place, normed0, normed1, w_across, w_across_c, cosine, sine, q_gain, k_gain, near0, near1],
+        [pltpu.VMEM((HEAD, width), bf16)],
+        flops,
+    )
+    swap_a = swap(swapping_a, 4)
+    swap_b = swap(swapping_b, 4)
+    far1_a = swap(kv_a, 2, range(4, 8))
+    far1_b = swap(kv_b, 2, range(4, 8))
+    far0_a = swap(swap_a, 2, range(4))
+    far0_b = swap(swap_b, 2, range(4))
+    o_x = swap(after(o_here, w_across), 2)
+    o_x_c = swap(after(o_x, swap_a), 1)
+    o_xy = swap(after(o_y, far0_b, far1_b), 2)
+    o_y_c = swap(after(o_y, kv_a), 1)
+
+    def attend_near(part):
+        return local_kernel(
+            functools.partial(attend_near_kernel, part),
+            [shape((chip_rows, 2 * half), f32), shape((chip_rows, half), f32)],
+            [place, full, swap_a, swap_b, kv_a, kv_b, bias],
+            [pltpu.VMEM((own_rows, pair), bf16)],
+            flops=2 * own_rows * own_rows * half,
+        )
+
+    def attend_far(part, before, far0, far1, *others):
+        return local_kernel(
+            functools.partial(attend_far_kernel, part),
+            [shape((chip_rows, half), bf16)],
+            [place, full, swap_a, swap_b, far0, far1, after(bias, *others), *before],
+            flops=own_rows * own_rows * half,
+        )[0]
+
+    sums_there = attend_near(1)
+    sums_here = attend_near(0)
+    attended_there = attend_far(1, sums_there, far0_a, far1_a)
+
+    chunk = 2 * w_o.shape[1]
+    came = {}
+
+    def share(relative, rows_there, *pieces):
+        (value,) = local_kernel(
+            share_kernel,
+            [shape((own_rows // 2, chunk), bf16)],
+            [place, rows_there, *pieces],
+            flops=own_rows * half * chunk,
+        )
+        came[relative ^ 2] = swap(value, 4)
+        return value
+
+    ring = [
+        (s * devices + i, (s + 1) % sections * devices + i)
+        for s in range(sections)
+        for i in range(devices)
+    ]
+    cross = [(source, target ^ 1) for source, target in ring]
+    arrived = {}
+
+    def finish(relative, *pieces):
+        own, other = local_kernel(
+            functools.partial(finish_kernel, relative),
+            [shape((rows, chunk), bf16)] * 2,
+            [place, attended_here, *pieces, came[relative], kept, x_c],
+            flops=own_rows * half * chunk,
+        )
+        arrived[0, relative] = lax.ppermute(own, ("section", "dp"), ring)
+        arrived[1, relative] = lax.ppermute(other, ("section", "dp"), cross)
+        return own
+
+    last = share(0, attended_there, o_here, o_here_c)
+    last = share(2, after(attended_there, last), o_y, o_y_c)
+    last = share(1, after(attended_there, last), o_x, o_x_c)
+    attended_here = attend_far(0, sums_here, far0_b, far1_b, last)
+    last = finish(2, o_y, o_y_c)
+    o_xy_c = swap(after(o_xy, last), 1)
+    share(3, attended_there, o_xy, o_xy_c)
+    finish(0, o_here, o_here_c)
+    finish(3, o_xy, o_xy_c)
+    finish(1, o_x, o_x_c)
+    (result,) = local_kernel(
+        gather_kernel,
+        [shape((micro, rows, width), bf16)],
+        [place, *[arrived[turn, relative] for turn in range(2) for relative in range(4)]],
+    )
+    return result[None]
+
+
 def solution(mesh):
+    devices = mesh.shape["dp"]
+
+    def body(held, norm_gain, w_qkv, q_gain, k_gain, w_out, lengths):
+        paired = KV_HEADS == 2 and HEADS == KV_HEADS * GROUP and held.shape[1] == 2
+        whole_heads = (2 * w_qkv.shape[2]) % HEAD == 0
+        form = on_chip_grid if devices == 8 and paired and whole_heads else on_device
+        return form(held, norm_gain, w_qkv, q_gain, k_gain, w_out, lengths)
+
     in_specs = (
         P("section", None, "dp", None),
         P("section", None),
@@ -149,5 +715,5 @@
     )
     out_specs = P("section", None, "dp", None)
     return jax.shard_map(
-        on_device, mesh=mesh, in_specs=in_specs, out_specs=out_specs, check_vma=False
+        body, mesh=mesh, in_specs=in_specs, out_specs=out_specs, check_vma=False
     )

time: 211 us -> 121 us (0.57)
  waiting for transfers between devices: 153 us -> 57.8 us
  starting transfers between devices: 1.62 us -> 30.3 us
  Pallas kernels: 0 us -> 26.5 us
  other arithmetic: 17.7 us -> 0 us
  matrix products: 16.3 us -> 0 us
  between operations: 13.6 us -> 0.3 us
    all_gather x3 -> x0, waiting for transfers between devices: 126 us -> none  [the longest x1 63.5 us: on_device(): lax.all_gather(w_qkv[0], 'dp', axis=1, tiled=True)]
    ppermute x1 -> x31, waiting for transfers between devices: 25.6 us -> 57.8 us  [the longest x23 48 us: swap(): return lax.ppermute(value, 'dp', [(i, i ^ bits) for i in among])]
    ppermute x1 -> x31, starting transfers between devices: 1.54 us -> 30.3 us  [the longest x23 21.5 us: swap(): return lax.ppermute(value, 'dp', [(i, i ^ bits) for i in among])]
    pallas_call x0 -> x17, Pallas kernels: none -> 26.5 us  [the longest x16 23.8 us: local_kernel(): pl.pallas_call(body, out_shape=tuple(outs), in_specs=[SMEM] * scalars + [...]
    dot_general x10 -> x0, matrix products: 16.3 us -> none  [the longest x1 5.95 us: on_device(): jnp.dot(normed, lax.all_gather(w_qkv[0], 'dp', axis=1, tiled=True), prefe...]
    sub x4 -> x0, other arithmetic: 5.49 us -> none  [attend_rows(): scores - highest[..., None]]
    reduce_sum x5 -> x0, other arithmetic: 3.33 us -> none  [the longest x3 2.47 us: rms_scale(): jnp.mean(values * values, axis=-1, keepdims=True) + EPSILON]
    another operation x8 -> x0, other arithmetic: 3.16 us -> none
  transfers between devices with their start and end apart: 4 -> 31, of which waited for: 4 -> 14; matrix products, arithmetic and copies ran while one was open for 12% -> 0% of each run, Pallas kernels for 0% -> 21%
where the time goes in v1:
time: 121 us
  waiting for transfers between devices  57.8 us (48%)
  starting transfers between devices  30.3 us (25%)
  Pallas kernels  26.5 us (22%)
  local copies, waits for them, and re-layouts  5.88 us (5%)
    ppermute x23, waiting for transfers between devices, swap(): return lax.ppermute(value, 'dp', [(i, i ^ bits) for i in among])  48 us
    pallas_call x16, Pallas kernels, local_kernel(): pl.pallas_call(body, out_shape=tuple(outs), in_specs=[SMEM] * scalars + [...  23.8 us
    ppermute x23, starting transfers between devices, swap(): return lax.ppermute(value, 'dp', [(i, i ^ bits) for i in among])  21.5 us
    ppermute x4, starting transfers between devices, finish(): arrived[0, relative] = lax.ppermute(own, ('section', 'dp'), ring)  7.16 us
    ppermute x4, waiting for transfers between devices, finish(): arrived[1, relative] = lax.ppermute(other, ('section', 'dp'), cross)  6.75 us
    unnamed x18, local copies, waits for them, and re-layouts  5.88 us
    ppermute x4, waiting for transfers between devices, finish(): arrived[0, relative] = lax.ppermute(own, ('section', 'dp'), ring)  3 us
    pallas_call x1, Pallas kernels, on_chip_grid(): pl.pallas_call(prepare_kernel, out_shape=(shape((11,), jnp.int32), shape(...  2.78 us
  transfers between devices with their start and end apart: 31, of which 14 were waited for; matrix products, arithmetic and copies ran while one was open for 0% of the time, Pallas kernels for 21%

profile of v1, /device:TPU:0, one launch (start us, length us, event | category | flops | bytes accessed | tf_op | source)
XLA Modules:
  0.0 120.8 jit_solution(12270338930543518504)
XLA Ops:
  0.6 2.9 %collective-permute-start.2 = (bf16[2,128,2048]{2,1,0:T(8,128)(2,1)}, bf16[2,128,2048]{2,1,0:T(8,128)(2,1)}, u32[]{:S(2)}, u32[]{:S(2)}) collective-permute-start(bf16[2,128,2048]{2,1,0:T(8,128)(2,1)} %bitcast.9), channel_id=1, source_target_pairs={{0,4},{1,5},{2,6},{3,7},{4,0},{5,1},{6,2},{7,3},{8,12},{9,13},{10,... | collective-permute-start | bytes 3145736 | tf_op jit(solution)/shard_map/ppermute | solution.py:555
  3.5 1.5 %collective-permute-start.4 = (bf16[320,2048]{1,0:T(8,128)(2,1)}, bf16[320,2048]{1,0:T(8,128)(2,1)}, u32[]{:S(2)}, u32[]{:S(2)}) collective-permute-start(bf16[320,2048]{1,0:T(8,128)(2,1)} %bitcast.16), channel_id=1, source_target_pairs={{0,2},{1,3},{2,0},{3,1},{4,6},{5,7},{6,4},{7,5},{8,10},{9,11},{10,... | collective-permute-start | bytes 3932168 | tf_op jit(solution)/shard_map/ppermute | solution.py:555
  7.6 2.8 %shard_map.82 = (s32[11]{0:T(128)S(1)}, f32[512,1024]{1,0:T(8,128)S(1)}, f32[512,128]{1,0:T(8,128)S(1)}, f32[512,128]{1,0:T(8,128)S(1)}, bf16[1024,256]{1,0:T(8,128)(2,1)S(1)}, /*index=5*/bf16[1024,256]{1,0:T(8,128)(2,1)S(1)}) custom-call(s32[1]{0:T(128)} %bitcast.here_ref, s32[2,8]{1,0:T(2,128)S(1)} %bitcast.20, f32[1,128]{1,0:T(1,128)S(1)} %copy-done.8, ...), custom_call_target="tpu_custom_call" | custom-call | tf_op jit(solution)/shard_map/pallas_call | solution.py:574
  13.7 2.1 %shard_map.83 = (bf16[256,640]{1,0:T(8,128)(2,1)S(1)}, bf16[256,2048]{1,0:T(8,128)(2,1)S(1)}) custom-call(s32[11]{0:T(128)S(1)} %get-tuple-element.43.place_ref, bf16[2,128,2048]{2,1,0:T(8,128)(2,1)S(1)} %bitcast.10, bf16[2,128,2048]{2,1,0:T(8,128)(2,1)S(1)} %collective-permute-done.x1_ref, f32[1,2048]{1,0:T(1,128)S(1)} %copy-done.4, ...), custom_call_target="tpu_custom_call" | custom-call | flops 671088640 | bytes 6628396 | tf_op jit(solution)/shard_map/pallas_call | solution.py:150
  15.8 11.4 %collective-permute-done.2.x0_ref = bf16[2,128,2048]{2,1,0:T(8,128)(2,1)} collective-permute-done((bf16[2,128,2048]{2,1,0:T(8,128)(2,1)}, bf16[2,128,2048]{2,1,0:T(8,128)(2,1)}, u32[]{:S(2)}, u32[]{:S(2)}) %collective-permute-start.2) | collective-permute-done | bytes 1048608 | tf_op jit(solution)/shard_map/ppermute | solution.py:555
  27.2 7.1 %collective-permute-done.4.w_own = bf16[320,2048]{1,0:T(8,128)(2,1)} collective-permute-done((bf16[320,2048]{1,0:T(8,128)(2,1)}, bf16[320,2048]{1,0:T(8,128)(2,1)}, u32[]{:S(2)}, u32[]{:S(2)}) %collective-permute-start.4) | collective-permute-done | bytes 1310752 | tf_op jit(solution)/shard_map/ppermute | solution.py:555
  34.6 1.7 %collective-permute-start.15 = (bf16[1024,256]{1,0:T(8,128)(2,1)S(1)}, bf16[1024,256]{1,0:T(8,128)(2,1)S(1)}, u32[]{:S(2)}, u32[]{:S(2)}) collective-permute-start(bf16[1024,256]{1,0:T(8,128)(2,1)S(1)} %get-tuple-element.66.w0_ref), channel_id=1, source_target_pairs={{0,2},{1,3},{2,0},{3,1},{4,6},{5,7},{6,4},{7,5},{8,10},{9,11},{10,... | collective-permute-start | bytes 1572872 | tf_op jit(solution)/shard_map/ppermute | solution.py:555
  36.3 2.8 %shard_map.84 = (bf16[256,640]{1,0:T(8,128)(2,1)S(1)}, bf16[256,2048]{1,0:T(8,128)(2,1)S(1)}) custom-call(s32[11]{0:T(128)S(1)} %get-tuple-element.43.place_ref, bf16[2,128,2048]{2,1,0:T(8,128)(2,1)} %collective-permute-done.2.x0_ref, bf16[2,128,2048]{2,1,0:T(8,128)(2,1)S(1)} %collective-permute-done.3.x1_ref, f32[1,2048]{1,0:T(1,128)S(1)} %copy-done.4, ...), custom_call_target="tpu_custom_call" | custom-call | flops 671088640 | bytes 6628396 | tf_op jit(solution)/shard_map/pallas_call | solution.py:150
  39.1 3.7 %shard_map.85 = (bf16[512,1280]{1,0:T(8,128)(2,1)S(1)}, bf16[256,256]{1,0:T(8,128)(2,1)S(1)}, bf16[256,256]{1,0:T(8,128)(2,1)S(1)}, bf16[256,256]{1,0:T(8,128)(2,1)S(1)}, bf16[256,256]{1,0:T(8,128)(2,1)S(1)}) custom-call(s32[11]{0:T(128)S(1)} %get-tuple-element.43.place_ref, bf16[256,2048]{1,0:T(8,128)(2,1)S(1)} %get-tuple-element.46.normed0_ref, ...), custom_call_target="tpu_custom_call" | custom-call | flops 1342177280 | bytes 7734316 | tf_op jit(solution)/shard_map/pallas_call | solution.py:150
  42.8 1.6 %collective-permute-start.7 = (bf16[256,256]{1,0:T(8,128)(2,1)S(1)}, bf16[256,256]{1,0:T(8,128)(2,1)S(1)}, u32[]{:S(2)}, u32[]{:S(2)}) collective-permute-start(bf16[256,256]{1,0:T(8,128)(2,1)S(1)} %get-tuple-element.55), channel_id=1, source_target_pairs={{0,4},{1,5},{2,6},{3,7},{4,0},{5,1},{6,2},{7,3},{8,12},{9,13},{10,... | collective-permute-start | bytes 393224 | tf_op jit(solution)/shard_map/ppermute | solution.py:555
  44.9 4.2 %collective-permute-done.13.w0_ref = bf16[1024,256]{1,0:T(8,128)(2,1)S(1)} collective-permute-done((bf16[1024,256]{1,0:T(8,128)(2,1)S(1)}, bf16[1024,256]{1,0:T(8,128)(2,1)S(1)}, u32[]{:S(2)}, u32[]{:S(2)}) %collective-permute-start.13) | collective-permute-done | bytes 524320 | tf_op jit(solution)/shard_map/ppermute | solution.py:555
  49.8 2.1 %collective-permute-done.7.swap_b_ref = bf16[256,256]{1,0:T(8,128)(2,1)S(1)} collective-permute-done((bf16[256,256]{1,0:T(8,128)(2,1)S(1)}, bf16[256,256]{1,0:T(8,128)(2,1)S(1)}, u32[]{:S(2)}, u32[]{:S(2)}) %collective-permute-start.7) | collective-permute-done | bytes 131104 | tf_op jit(solution)/shard_map/ppermute | solution.py:555
  51.9 3.4 %collective-permute-start.8 = (bf16[256,256]{1,0:T(8,128)(2,1)S(1)}, bf16[256,256]{1,0:T(8,128)(2,1)S(1)}, u32[]{:S(2)}, u32[]{:S(2)}) collective-permute-start(bf16[256,256]{1,0:T(8,128)(2,1)S(1)} %collective-permute-done.7.swap_b_ref), channel_id=1, source_target_pairs={{0,2},{1,3},{2,0},{3,1},{8,10},{9,11},{10,8},{11,9},{16,18},{17,19... | collective-permute-start | bytes 393224 | tf_op jit(solution)/shard_map/ppermute | solution.py:555
  56.6 2.2 %collective-permute-done.8.far0_ref = bf16[256,256]{1,0:T(8,128)(2,1)S(1)} collective-permute-done((bf16[256,256]{1,0:T(8,128)(2,1)S(1)}, bf16[256,256]{1,0:T(8,128)(2,1)S(1)}, u32[]{:S(2)}, u32[]{:S(2)}) %collective-permute-start.8) | collective-permute-done | bytes 131104 | tf_op jit(solution)/shard_map/ppermute | solution.py:555
  58.8 1.5 %collective-permute-start.19 = (bf16[1024,256]{1,0:T(8,128)(2,1)S(1)}, bf16[1024,256]{1,0:T(8,128)(2,1)S(1)}, u32[]{:S(2)}, u32[]{:S(2)}) collective-permute-start(bf16[1024,256]{1,0:T(8,128)(2,1)S(1)} %collective-permute-done.13.w0_ref), channel_id=1, source_target_pairs={{0,2},{1,3},{2,0},{3,1},{4,6},{5,7},{6,4},{7,5},{8,10},{9,11},{10,... | collective-permute-start | bytes 1572872 | tf_op jit(solution)/shard_map/ppermute | solution.py:555
  60.2 2.4 %collective-permute-start.10 = (bf16[256,256]{1,0:T(8,128)(2,1)S(1)}, bf16[256,256]{1,0:T(8,128)(2,1)S(1)}, u32[]{:S(2)}, u32[]{:S(2)}) collective-permute-start(bf16[256,256]{1,0:T(8,128)(2,1)S(1)} %collective-permute-done.6.swap_a_ref), channel_id=1, source_target_pairs={{0,2},{1,3},{2,0},{3,1},{8,10},{9,11},{10,8},{11,9},{16,18},{17,19... | collective-permute-start | bytes 393224 | tf_op jit(solution)/shard_map/ppermute | solution.py:555
  62.7 1.5 %shard_map.86 = (f32[256,2048]{1,0:T(8,128)S(1)}, f32[256,1024]{1,0:T(8,128)S(1)}) custom-call(s32[11]{0:T(128)S(1)} %get-tuple-element.43.place_ref, bf16[512,1280]{1,0:T(8,128)(2,1)S(1)} %get-tuple-element.53.full_ref, bf16[256,256]{1,0:T(8,128)(2,1)S(1)} %collective-permute-done.6.swap_a_ref, bf16[256,256]{1,0:T(8,128)(2,1)S(1)} %collective-permute-done.7.swap_b_ref, ...), custom_call_target="tpu_custom_call" | custom-call | flops 536870912 | bytes 7077932 | tf_op jit(solution)/shard_map/pallas_call | solution.py:150
  64.2 9.2 %collective-permute-done.10.far0_ref = bf16[256,256]{1,0:T(8,128)(2,1)S(1)} collective-permute-done((bf16[256,256]{1,0:T(8,128)(2,1)S(1)}, bf16[256,256]{1,0:T(8,128)(2,1)S(1)}, u32[]{:S(2)}, u32[]{:S(2)}) %collective-permute-start.10) | collective-permute-done | bytes 131104 | tf_op jit(solution)/shard_map/ppermute | solution.py:555
  73.4 1.9 %shard_map.87.a_ref = bf16[256,1024]{1,0:T(8,128)(2,1)S(1)} custom-call(s32[11]{0:T(128)S(1)} %get-tuple-element.43.place_ref, bf16[512,1280]{1,0:T(8,128)(2,1)S(1)} %get-tuple-element.53.full_ref, bf16[256,256]{1,0:T(8,128)(2,1)S(1)} %collective-permute-done.6.swap_a_ref, bf16[256,256]{1,0:T(8,128)(2,1)S(1)} %collective-permute-done.7.swap_b_ref, ...), custom_call_target="tpu_custom_call" | custom-call | flops 268435456 | bytes 7602220 | tf_op jit(solution)/shard_map/pallas_call | solution.py:150
  76.5 1.5 %shard_map.91 = (f32[256,2048]{1,0:T(8,128)S(1)}, f32[256,1024]{1,0:T(8,128)S(1)}) custom-call(s32[11]{0:T(128)S(1)} %get-tuple-element.43.place_ref, bf16[512,1280]{1,0:T(8,128)(2,1)S(1)} %get-tuple-element.53.full_ref, bf16[256,256]{1,0:T(8,128)(2,1)S(1)} %collective-permute-done.6.swap_a_ref, bf16[256,256]{1,0:T(8,128)(2,1)S(1)} %collective-permute-done.7.swap_b_ref, ...), custom_call_target="tpu_custom_call" | custom-call | flops 536870912 | bytes 7077932 | tf_op jit(solution)/shard_map/pallas_call | solution.py:150
  80.7 2.1 %collective-permute-done.20.came_ref = bf16[256,512]{1,0:T(8,128)(2,1)S(1)} collective-permute-done((bf16[256,512]{1,0:T(8,128)(2,1)S(1)}, bf16[256,512]{1,0:T(8,128)(2,1)S(1)}, u32[]{:S(2)}, u32[]{:S(2)}) %collective-permute-start.20) | collective-permute-done | bytes 262176 | tf_op jit(solution)/shard_map/ppermute | solution.py:555
  88.0 2.4 %collective-permute-start.24 = (bf16[128,512]{1,0:T(8,128)(2,1)S(1)}, bf16[128,512]{1,0:T(8,128)(2,1)S(1)}, u32[]{:S(2)}, u32[]{:S(2)}) collective-permute-start(bf16[128,512]{1,0:T(8,128)(2,1)S(1)} %get-tuple-element.73), channel_id=1, source_target_pairs={{0,8},{1,9},{2,10},{3,11},{4,12},{5,13},{6,14},{7,15},{8,16},{9,17... | collective-permute-start | bytes 393224 | tf_op jit(solution)/shard_map/ppermute | solution.py:676
  90.4 2.8 %collective-permute-done.17.came_ref = bf16[256,512]{1,0:T(8,128)(2,1)S(1)} collective-permute-done((bf16[256,512]{1,0:T(8,128)(2,1)S(1)}, bf16[256,512]{1,0:T(8,128)(2,1)S(1)}, u32[]{:S(2)}, u32[]{:S(2)}) %collective-permute-start.17) | collective-permute-done | bytes 262176 | tf_op jit(solution)/shard_map/ppermute | solution.py:555
  94.2 1.6 %collective-permute-start.18 = (bf16[128,512]{1,0:T(8,128)(2,1)S(1)}, bf16[128,512]{1,0:T(8,128)(2,1)S(1)}, u32[]{:S(2)}, u32[]{:S(2)}) collective-permute-start(bf16[128,512]{1,0:T(8,128)(2,1)S(1)} %get-tuple-element.71), channel_id=1, source_target_pairs={{0,8},{1,9},{2,10},{3,11},{4,12},{5,13},{6,14},{7,15},{8,16},{9,17... | collective-permute-start | bytes 393224 | tf_op jit(solution)/shard_map/ppermute | solution.py:676
  95.8 3.0 %collective-permute-done.25.came_ref = bf16[256,512]{1,0:T(8,128)(2,1)S(1)} collective-permute-done((bf16[256,512]{1,0:T(8,128)(2,1)S(1)}, bf16[256,512]{1,0:T(8,128)(2,1)S(1)}, u32[]{:S(2)}, u32[]{:S(2)}) %collective-permute-start.25) | collective-permute-done | bytes 262176 | tf_op jit(solution)/shard_map/ppermute | solution.py:555
  100.0 3.9 %collective-permute-done.22.came_ref = bf16[256,512]{1,0:T(8,128)(2,1)S(1)} collective-permute-done((bf16[256,512]{1,0:T(8,128)(2,1)S(1)}, bf16[256,512]{1,0:T(8,128)(2,1)S(1)}, u32[]{:S(2)}, u32[]{:S(2)}) %collective-permute-start.22) | collective-permute-done | bytes 262176 | tf_op jit(solution)/shard_map/ppermute | solution.py:555
  103.8 1.6 %collective-permute-start.26 = (bf16[128,512]{1,0:T(8,128)(2,1)S(1)}, bf16[128,512]{1,0:T(8,128)(2,1)S(1)}, u32[]{:S(2)}, u32[]{:S(2)}) collective-permute-start(bf16[128,512]{1,0:T(8,128)(2,1)S(1)} %get-tuple-element.76), channel_id=1, source_target_pairs={{0,8},{1,9},{2,10},{3,11},{4,12},{5,13},{6,14},{7,15},{8,16},{9,17... | collective-permute-start | bytes 393224 | tf_op jit(solution)/shard_map/ppermute | solution.py:676
  107.0 1.6 %collective-permute-start.23 = (bf16[128,512]{1,0:T(8,128)(2,1)S(1)}, bf16[128,512]{1,0:T(8,128)(2,1)S(1)}, u32[]{:S(2)}, u32[]{:S(2)}) collective-permute-start(bf16[128,512]{1,0:T(8,128)(2,1)S(1)} %get-tuple-element.75), channel_id=1, source_target_pairs={{0,8},{1,9},{2,10},{3,11},{4,12},{5,13},{6,14},{7,15},{8,16},{9,17... | collective-permute-start | bytes 393224 | tf_op jit(solution)/shard_map/ppermute | solution.py:676
  110.7 3.4 %collective-permute-done.30.refs_7_ = bf16[128,512]{1,0:T(8,128)(2,1)S(1)} collective-permute-done((bf16[128,512]{1,0:T(8,128)(2,1)S(1)}, bf16[128,512]{1,0:T(8,128)(2,1)S(1)}, u32[]{:S(2)}, u32[]{:S(2)}) %collective-permute-start.30) | collective-permute-done | bytes 131104 | tf_op jit(solution)/shard_map/ppermute | solution.py:677
  114.1 1.7 %collective-permute-done.23.refs_1_ = bf16[128,512]{1,0:T(8,128)(2,1)S(1)} collective-permute-done((bf16[128,512]{1,0:T(8,128)(2,1)S(1)}, bf16[128,512]{1,0:T(8,128)(2,1)S(1)}, u32[]{:S(2)}, u32[]{:S(2)}) %collective-permute-start.23) | collective-permute-done | bytes 131104 | tf_op jit(solution)/shard_map/ppermute | solution.py:676
  115.8 3.3 %collective-permute-done.28.refs_5_ = bf16[128,512]{1,0:T(8,128)(2,1)S(1)} collective-permute-done((bf16[128,512]{1,0:T(8,128)(2,1)S(1)}, bf16[128,512]{1,0:T(8,128)(2,1)S(1)}, u32[]{:S(2)}, u32[]{:S(2)}) %collective-permute-start.28) | collective-permute-done | bytes 131104 | tf_op jit(solution)/shard_map/ppermute | solution.py:677
  119.2 1.6 %shard_map.98 = bf16[2,128,2048]{2,1,0:T(8,128)(2,1)} custom-call(s32[11]{0:T(128)S(1)} %get-tuple-element.43.place_ref, bf16[128,512]{1,0:T(8,128)(2,1)S(1)} %collective-permute-done.18.refs_0_, bf16[128,512]{1,0:T(8,128)(2,1)S(1)} %collective-permute-done.23.refs_1_, bf16[128,512]{1,0:T(8,128)(2,1)S(1)} %collective-permute-done.24.refs_2_, ...), custom_call_target="tpu_custom_call" | custom-call | bytes 2097196 | tf_op jit(solution)/shard_map/pallas_call | solution.py:150
  (65 shorter events, 23.9 us)
Async XLA Ops:
  0.0 10.4 %collective-permute-start.1 = (bf16[320,2048]{1,0:T(8,128)(2,1)}, bf16[320,2048]{1,0:T(8,128)(2,1)S(1)}, u32[]{:S(2)}, u32[]{:S(2)}) collective-permute-start(bf16[320,2048]{1,0:T(8,128)(2,1)} %bitcast.15), channel_id=1, source_target_pairs={{0,1},{1,0},{2,3},{3,2},{4,5},{5,4},{6,7},{7,6},{8,9},{9,8},{10,11... | collective-permute-start | bytes 3932168 | tf_op jit(solution)/shard_map/ppermute | solution.py:555
  0.5 9.9 %collective-permute-start = (bf16[2,128,2048]{2,1,0:T(8,128)(2,1)}, bf16[2,128,2048]{2,1,0:T(8,128)(2,1)S(1)}, u32[]{:S(2)}, u32[]{:S(2)}) collective-permute-start(bf16[2,128,2048]{2,1,0:T(8,128)(2,1)} %bitcast.8), channel_id=1, source_target_pairs={{0,1},{1,0},{2,3},{3,2},{4,5},{5,4},{6,7},{7,6},{8,9},{9,8},{10,11... | collective-permute-start | bytes 3145736 | tf_op jit(solution)/shard_map/ppermute | solution.py:555
  0.6 26.6 %collective-permute-start.2 = (bf16[2,128,2048]{2,1,0:T(8,128)(2,1)}, bf16[2,128,2048]{2,1,0:T(8,128)(2,1)}, u32[]{:S(2)}, u32[]{:S(2)}) collective-permute-start(bf16[2,128,2048]{2,1,0:T(8,128)(2,1)} %bitcast.9), channel_id=1, source_target_pairs={{0,4},{1,5},{2,6},{3,7},{4,0},{5,1},{6,2},{7,3},{8,12},{9,13},{10,... | collective-permute-start | bytes 3145736 | tf_op jit(solution)/shard_map/ppermute | solution.py:555
  3.5 30.8 %collective-permute-start.4 = (bf16[320,2048]{1,0:T(8,128)(2,1)}, bf16[320,2048]{1,0:T(8,128)(2,1)}, u32[]{:S(2)}, u32[]{:S(2)}) collective-permute-start(bf16[320,2048]{1,0:T(8,128)(2,1)} %bitcast.16), channel_id=1, source_target_pairs={{0,2},{1,3},{2,0},{3,1},{4,6},{5,7},{6,4},{7,5},{8,10},{9,11},{10,... | collective-permute-start | bytes 3932168 | tf_op jit(solution)/shard_map/ppermute | solution.py:555
  13.7 22.6 %copy-start.2 = (bf16[1,2048,320]{1,2,0:T(8,128)(2,1)S(1)}, bf16[1,2048,320]{1,2,0:T(8,128)(2,1)}, u32[]{:S(2)}) copy-start(bf16[1,2048,320]{1,2,0:T(8,128)(2,1)} %param.10) | copy-start | bytes 3932164
  27.2 7.1 %collective-permute-start.3 = (bf16[2,128,2048]{2,1,0:T(8,128)(2,1)}, bf16[2,128,2048]{2,1,0:T(8,128)(2,1)S(1)}, u32[]{:S(2)}, u32[]{:S(2)}) collective-permute-start(bf16[2,128,2048]{2,1,0:T(8,128)(2,1)} %collective-permute-done.2.x0_ref), channel_id=1, source_target_pairs={{0,1},{1,0},{2,3},{3,2},{4,5},{5,4},{6,7},{7,6},{8,9},{9,8},{10,11... | collective-permute-start | bytes 3145736 | tf_op jit(solution)/shard_map/ppermute | solution.py:555
  34.3 4.8 %collective-permute-start.5 = (bf16[320,2048]{1,0:T(8,128)(2,1)}, bf16[320,2048]{1,0:T(8,128)(2,1)S(1)}, u32[]{:S(2)}, u32[]{:S(2)}) collective-permute-start(bf16[320,2048]{1,0:T(8,128)(2,1)} %collective-permute-done.4.w_own), channel_id=1, source_target_pairs={{0,1},{1,0},{2,3},{3,2},{4,5},{5,4},{6,7},{7,6},{8,9},{9,8},{10,11... | collective-permute-start | bytes 3932168 | tf_op jit(solution)/shard_map/ppermute | solution.py:555
  34.3 14.8 %collective-permute-start.13 = (bf16[1024,256]{1,0:T(8,128)(2,1)S(1)}, bf16[1024,256]{1,0:T(8,128)(2,1)S(1)}, u32[]{:S(2)}, u32[]{:S(2)}) collective-permute-start(bf16[1024,256]{1,0:T(8,128)(2,1)S(1)} %get-tuple-element.63), channel_id=1, source_target_pairs={{0,4},{1,5},{2,6},{3,7},{4,0},{5,1},{6,2},{7,3},{8,12},{9,13},{10,... | collective-permute-start | bytes 1572872 | tf_op jit(solution)/shard_map/ppermute | solution.py:555
  34.6 20.7 %collective-permute-start.15 = (bf16[1024,256]{1,0:T(8,128)(2,1)S(1)}, bf16[1024,256]{1,0:T(8,128)(2,1)S(1)}, u32[]{:S(2)}, u32[]{:S(2)}) collective-permute-start(bf16[1024,256]{1,0:T(8,128)(2,1)S(1)} %get-tuple-element.66.w0_ref), channel_id=1, source_target_pairs={{0,2},{1,3},{2,0},{3,1},{4,6},{5,7},{6,4},{7,5},{8,10},{9,11},{10,... | collective-permute-start | bytes 1572872 | tf_op jit(solution)/shard_map/ppermute | solution.py:555
  36.3 39.1 %collective-permute-start.12 = (bf16[1024,256]{1,0:T(8,128)(2,1)S(1)}, bf16[1024,256]{1,0:T(8,128)(2,1)S(1)}, u32[]{:S(2)}, u32[]{:S(2)}) collective-permute-start(bf16[1024,256]{1,0:T(8,128)(2,1)S(1)} %get-tuple-element.66.w0_ref), channel_id=1, source_target_pairs={{0,1},{1,0},{2,3},{3,2},{4,5},{5,4},{6,7},{7,6},{8,9},{9,8},{10,11... | collective-permute-start | bytes 1572872 | tf_op jit(solution)/shard_map/ppermute | solution.py:555
  42.8 9.1 %collective-permute-start.7 = (bf16[256,256]{1,0:T(8,128)(2,1)S(1)}, bf16[256,256]{1,0:T(8,128)(2,1)S(1)}, u32[]{:S(2)}, u32[]{:S(2)}) collective-permute-start(bf16[256,256]{1,0:T(8,128)(2,1)S(1)} %get-tuple-element.55), channel_id=1, source_target_pairs={{0,4},{1,5},{2,6},{3,7},{4,0},{5,1},{6,2},{7,3},{8,12},{9,13},{10,... | collective-permute-start | bytes 393224 | tf_op jit(solution)/shard_map/ppermute | solution.py:555
  44.4 11.0 %collective-permute-start.6 = (bf16[256,256]{1,0:T(8,128)(2,1)S(1)}, bf16[256,256]{1,0:T(8,128)(2,1)S(1)}, u32[]{:S(2)}, u32[]{:S(2)}) collective-permute-start(bf16[256,256]{1,0:T(8,128)(2,1)S(1)} %get-tuple-element.54), channel_id=1, source_target_pairs={{0,4},{1,5},{2,6},{3,7},{4,0},{5,1},{6,2},{7,3},{8,12},{9,13},{10,... | collective-permute-start | bytes 393224 | tf_op jit(solution)/shard_map/ppermute | solution.py:555
  49.1 6.8 %collective-permute-start.9 = (bf16[256,256]{1,0:T(8,128)(2,1)S(1)}, bf16[256,256]{1,0:T(8,128)(2,1)S(1)}, u32[]{:S(2)}, u32[]{:S(2)}) collective-permute-start(bf16[256,256]{1,0:T(8,128)(2,1)S(1)} %get-tuple-element.56.kv_b_ref), channel_id=1, source_target_pairs={{4,6},{5,7},{6,4},{7,5},{12,14},{13,15},{14,12},{15,13},{20,22},{2... | collective-permute-start | bytes 393224 | tf_op jit(solution)/shard_map/ppermute | solution.py:555
  51.9 6.8 %collective-permute-start.8 = (bf16[256,256]{1,0:T(8,128)(2,1)S(1)}, bf16[256,256]{1,0:T(8,128)(2,1)S(1)}, u32[]{:S(2)}, u32[]{:S(2)}) collective-permute-start(bf16[256,256]{1,0:T(8,128)(2,1)S(1)} %collective-permute-done.7.swap_b_ref), channel_id=1, source_target_pairs={{0,2},{1,3},{2,0},{3,1},{8,10},{9,11},{10,8},{11,9},{16,18},{17,19... | collective-permute-start | bytes 393224 | tf_op jit(solution)/shard_map/ppermute | solution.py:555
  55.3 22.7 %collective-permute-start.14 = (bf16[1024,256]{1,0:T(8,128)(2,1)S(1)}, bf16[1024,256]{1,0:T(8,128)(2,1)S(1)}, u32[]{:S(2)}, u32[]{:S(2)}) collective-permute-start(bf16[1024,256]{1,0:T(8,128)(2,1)S(1)} %collective-permute-done.13.w0_ref), channel_id=1, source_target_pairs={{0,1},{1,0},{2,3},{3,2},{4,5},{5,4},{6,7},{7,6},{8,9},{9,8},{10,11... | collective-permute-start | bytes 1572872 | tf_op jit(solution)/shard_map/ppermute | solution.py:555
  55.4 23.6 %collective-permute-start.16 = (bf16[1024,256]{1,0:T(8,128)(2,1)S(1)}, bf16[1024,256]{1,0:T(8,128)(2,1)S(1)}, u32[]{:S(2)}, u32[]{:S(2)}) collective-permute-start(bf16[1024,256]{1,0:T(8,128)(2,1)S(1)} %collective-permute-done.15.w0_ref), channel_id=1, source_target_pairs={{0,1},{1,0},{2,3},{3,2},{4,5},{5,4},{6,7},{7,6},{8,9},{9,8},{10,11... | collective-permute-start | bytes 1572872 | tf_op jit(solution)/shard_map/ppermute | solution.py:555
  55.9 4.4 %collective-permute-start.11 = (bf16[256,256]{1,0:T(8,128)(2,1)S(1)}, bf16[256,256]{1,0:T(8,128)(2,1)S(1)}, u32[]{:S(2)}, u32[]{:S(2)}) collective-permute-start(bf16[256,256]{1,0:T(8,128)(2,1)S(1)} %get-tuple-element.58.kv_a_ref), channel_id=1, source_target_pairs={{4,6},{5,7},{6,4},{7,5},{12,14},{13,15},{14,12},{15,13},{20,22},{2... | collective-permute-start | bytes 393224 | tf_op jit(solution)/shard_map/ppermute | solution.py:555
  58.8 25.1 %collective-permute-start.19 = (bf16[1024,256]{1,0:T(8,128)(2,1)S(1)}, bf16[1024,256]{1,0:T(8,128)(2,1)S(1)}, u32[]{:S(2)}, u32[]{:S(2)}) collective-permute-start(bf16[1024,256]{1,0:T(8,128)(2,1)S(1)} %collective-permute-done.13.w0_ref), channel_id=1, source_target_pairs={{0,2},{1,3},{2,0},{3,1},{4,6},{5,7},{6,4},{7,5},{8,10},{9,11},{10,... | collective-permute-start | bytes 1572872 | tf_op jit(solution)/shard_map/ppermute | solution.py:555
  60.2 13.2 %collective-permute-start.10 = (bf16[256,256]{1,0:T(8,128)(2,1)S(1)}, bf16[256,256]{1,0:T(8,128)(2,1)S(1)}, u32[]{:S(2)}, u32[]{:S(2)}) collective-permute-start(bf16[256,256]{1,0:T(8,128)(2,1)S(1)} %collective-permute-done.6.swap_a_ref), channel_id=1, source_target_pairs={{0,2},{1,3},{2,0},{3,1},{8,10},{9,11},{10,8},{11,9},{16,18},{17,19... | collective-permute-start | bytes 393224 | tf_op jit(solution)/shard_map/ppermute | solution.py:555
  76.4 6.4 %collective-permute-start.20 = (bf16[256,512]{1,0:T(8,128)(2,1)S(1)}, bf16[256,512]{1,0:T(8,128)(2,1)S(1)}, u32[]{:S(2)}, u32[]{:S(2)}) collective-permute-start(bf16[256,512]{1,0:T(8,128)(2,1)S(1)} %shard_map.88), channel_id=1, source_target_pairs={{0,4},{1,5},{2,6},{3,7},{4,0},{5,1},{6,2},{7,3},{8,12},{9,13},{10,... | collective-permute-start | bytes 786440 | tf_op jit(solution)/shard_map/ppermute | solution.py:555
  83.8 2.2 %collective-permute-start.21 = (bf16[1024,256]{1,0:T(8,128)(2,1)S(1)}, bf16[1024,256]{1,0:T(8,128)(2,1)S(1)}, u32[]{:S(2)}, u32[]{:S(2)}) collective-permute-start(bf16[1024,256]{1,0:T(8,128)(2,1)S(1)} %collective-permute-done.19.w0_ref), channel_id=1, source_target_pairs={{0,1},{1,0},{2,3},{3,2},{4,5},{5,4},{6,7},{7,6},{8,9},{9,8},{10,11... | collective-permute-start | bytes 1572872 | tf_op jit(solution)/shard_map/ppermute | solution.py:555
  83.9 9.2 %collective-permute-start.17 = (bf16[256,512]{1,0:T(8,128)(2,1)S(1)}, bf16[256,512]{1,0:T(8,128)(2,1)S(1)}, u32[]{:S(2)}, u32[]{:S(2)}) collective-permute-start(bf16[256,512]{1,0:T(8,128)(2,1)S(1)} %shard_map.89), channel_id=1, source_target_pairs={{0,4},{1,5},{2,6},{3,7},{4,0},{5,1},{6,2},{7,3},{8,12},{9,13},{10,... | collective-permute-start | bytes 786440 | tf_op jit(solution)/shard_map/ppermute | solution.py:555
  84.9 13.9 %collective-permute-start.25 = (bf16[256,512]{1,0:T(8,128)(2,1)S(1)}, bf16[256,512]{1,0:T(8,128)(2,1)S(1)}, u32[]{:S(2)}, u32[]{:S(2)}) collective-permute-start(bf16[256,512]{1,0:T(8,128)(2,1)S(1)} %shard_map.90), channel_id=1, source_target_pairs={{0,4},{1,5},{2,6},{3,7},{4,0},{5,1},{6,2},{7,3},{8,12},{9,13},{10,... | collective-permute-start | bytes 786440 | tf_op jit(solution)/shard_map/ppermute | solution.py:555
  87.0 16.9 %collective-permute-start.22 = (bf16[256,512]{1,0:T(8,128)(2,1)S(1)}, bf16[256,512]{1,0:T(8,128)(2,1)S(1)}, u32[]{:S(2)}, u32[]{:S(2)}) collective-permute-start(bf16[256,512]{1,0:T(8,128)(2,1)S(1)} %shard_map.95), channel_id=1, source_target_pairs={{0,4},{1,5},{2,6},{3,7},{4,0},{5,1},{6,2},{7,3},{8,12},{9,13},{10,... | collective-permute-start | bytes 786440 | tf_op jit(solution)/shard_map/ppermute | solution.py:555
  88.0 18.5 %collective-permute-start.24 = (bf16[128,512]{1,0:T(8,128)(2,1)S(1)}, bf16[128,512]{1,0:T(8,128)(2,1)S(1)}, u32[]{:S(2)}, u32[]{:S(2)}) collective-permute-start(bf16[128,512]{1,0:T(8,128)(2,1)S(1)} %get-tuple-element.73), channel_id=1, source_target_pairs={{0,8},{1,9},{2,10},{3,11},{4,12},{5,13},{6,14},{7,15},{8,16},{9,17... | collective-permute-start | bytes 393224 | tf_op jit(solution)/shard_map/ppermute | solution.py:676
  90.4 16.6 %collective-permute-start.29 = (bf16[128,512]{1,0:T(8,128)(2,1)S(1)}, bf16[128,512]{1,0:T(8,128)(2,1)S(1)}, u32[]{:S(2)}, u32[]{:S(2)}) collective-permute-start(bf16[128,512]{1,0:T(8,128)(2,1)S(1)} %get-tuple-element.79), channel_id=1, source_target_pairs={{0,9},{1,8},{2,11},{3,10},{4,13},{5,12},{6,15},{7,14},{8,17},{9,16... | collective-permute-start | bytes 393224 | tf_op jit(solution)/shard_map/ppermute | solution.py:677
  94.2 14.4 %collective-permute-start.18 = (bf16[128,512]{1,0:T(8,128)(2,1)S(1)}, bf16[128,512]{1,0:T(8,128)(2,1)S(1)}, u32[]{:S(2)}, u32[]{:S(2)}) collective-permute-start(bf16[128,512]{1,0:T(8,128)(2,1)S(1)} %get-tuple-element.71), channel_id=1, source_target_pairs={{0,8},{1,9},{2,10},{3,11},{4,12},{5,13},{6,14},{7,15},{8,16},{9,17... | collective-permute-start | bytes 393224 | tf_op jit(solution)/shard_map/ppermute | solution.py:676
  98.8 10.7 %collective-permute-start.27 = (bf16[128,512]{1,0:T(8,128)(2,1)S(1)}, bf16[128,512]{1,0:T(8,128)(2,1)S(1)}, u32[]{:S(2)}, u32[]{:S(2)}) collective-permute-start(bf16[128,512]{1,0:T(8,128)(2,1)S(1)} %get-tuple-element.77), channel_id=1, source_target_pairs={{0,9},{1,8},{2,11},{3,10},{4,13},{5,12},{6,15},{7,14},{8,17},{9,16... | collective-permute-start | bytes 393224 | tf_op jit(solution)/shard_map/ppermute | solution.py:677
  103.8 6.8 %collective-permute-start.26 = (bf16[128,512]{1,0:T(8,128)(2,1)S(1)}, bf16[128,512]{1,0:T(8,128)(2,1)S(1)}, u32[]{:S(2)}, u32[]{:S(2)}) collective-permute-start(bf16[128,512]{1,0:T(8,128)(2,1)S(1)} %get-tuple-element.76), channel_id=1, source_target_pairs={{0,8},{1,9},{2,10},{3,11},{4,12},{5,13},{6,14},{7,15},{8,16},{9,17... | collective-permute-start | bytes 393224 | tf_op jit(solution)/shard_map/ppermute | solution.py:676
  106.4 7.6 %collective-permute-start.30 = (bf16[128,512]{1,0:T(8,128)(2,1)S(1)}, bf16[128,512]{1,0:T(8,128)(2,1)S(1)}, u32[]{:S(2)}, u32[]{:S(2)}) collective-permute-start(bf16[128,512]{1,0:T(8,128)(2,1)S(1)} %get-tuple-element.80), channel_id=1, source_target_pairs={{0,9},{1,8},{2,11},{3,10},{4,13},{5,12},{6,15},{7,14},{8,17},{9,16... | collective-permute-start | bytes 393224 | tf_op jit(solution)/shard_map/ppermute | solution.py:677
  107.0 8.9 %collective-permute-start.23 = (bf16[128,512]{1,0:T(8,128)(2,1)S(1)}, bf16[128,512]{1,0:T(8,128)(2,1)S(1)}, u32[]{:S(2)}, u32[]{:S(2)}) collective-permute-start(bf16[128,512]{1,0:T(8,128)(2,1)S(1)} %get-tuple-element.75), channel_id=1, source_target_pairs={{0,8},{1,9},{2,10},{3,11},{4,12},{5,13},{6,14},{7,15},{8,16},{9,17... | collective-permute-start | bytes 393224 | tf_op jit(solution)/shard_map/ppermute | solution.py:676
  108.6 10.6 %collective-permute-start.28 = (bf16[128,512]{1,0:T(8,128)(2,1)S(1)}, bf16[128,512]{1,0:T(8,128)(2,1)S(1)}, u32[]{:S(2)}, u32[]{:S(2)}) collective-permute-start(bf16[128,512]{1,0:T(8,128)(2,1)S(1)} %get-tuple-element.78), channel_id=1, source_target_pairs={{0,9},{1,8},{2,11},{3,10},{4,13},{5,12},{6,15},{7,14},{8,17},{9,16... | collective-permute-start | bytes 393224 | tf_op jit(solution)/shard_map/ppermute | solution.py:677
  (8 other events, 16.3 us)

commit v2 on v1

--- a/solution.py
+++ b/solution.py
@@ -620,15 +620,13 @@
     far0_a = swap(swap_a, 2, range(4))
     far0_b = swap(swap_b, 2, range(4))
     o_x = swap(after(o_here, w_across), 2)
-    o_x_c = swap(after(o_x, swap_a), 1)
-    o_xy = swap(after(o_y, far0_b, far1_b), 2)
     o_y_c = swap(after(o_y, kv_a), 1)
 
-    def attend_near(part):
+    def attend_near(part, gate):
         return local_kernel(
             functools.partial(attend_near_kernel, part),
             [shape((chip_rows, 2 * half), f32), shape((chip_rows, half), f32)],
-            [place, full, swap_a, swap_b, kv_a, kv_b, bias],
+            [place, full, swap_a, swap_b, kv_a, kv_b, after(bias, gate)],
             [pltpu.VMEM((own_rows, pair), bf16)],
             flops=2 * own_rows * own_rows * half,
         )
@@ -641,9 +639,10 @@
             flops=own_rows * own_rows * half,
         )[0]
 
-    sums_there = attend_near(1)
-    sums_here = attend_near(0)
+    sums_there = attend_near(1, bias)
+    o_xy = swap(after(o_y, far0_a, far1_a), 2)
     attended_there = attend_far(1, sums_there, far0_a, far1_a)
+    o_x_c = swap(after(o_x, attended_there), 1)
 
     chunk = 2 * w_o.shape[1]
     came = {}
@@ -679,12 +678,13 @@
 
     last = share(0, attended_there, o_here, o_here_c)
     last = share(2, after(attended_there, last), o_y, o_y_c)
-    last = share(1, after(attended_there, last), o_x, o_x_c)
+    sums_here = attend_near(0, last)
+    last = share(1, after(attended_there, sums_here[1]), o_x, o_x_c)
     attended_here = attend_far(0, sums_here, far0_b, far1_b, last)
     last = finish(2, o_y, o_y_c)
     o_xy_c = swap(after(o_xy, last), 1)
-    share(3, attended_there, o_xy, o_xy_c)
-    finish(0, o_here, o_here_c)
+    last = finish(0, o_here, o_here_c)
+    share(3, after(attended_there, last), o_xy, o_xy_c)
     finish(3, o_xy, o_xy_c)
     finish(1, o_x, o_x_c)
     (result,) = local_kernel(

time: 121 us -> 119 us (0.983)
    ppermute x4, waiting for transfers between devices: 3 us -> 7.23 us  [finish(): arrived[0, relative] = lax.ppermute(own, ('section', 'dp'), ring)]
    ppermute x23, waiting for transfers between devices: 48 us -> 44.8 us  [swap(): return lax.ppermute(value, 'dp', [(i, i ^ bits) for i in among])]
    ppermute x4, waiting for transfers between devices: 6.75 us -> 4.66 us  [finish(): arrived[1, relative] = lax.ppermute(other, ('section', 'dp'), cross)]
where the time goes in v2:
time: 119 us
  waiting for transfers between devices  56.7 us (48%)
  starting transfers between devices  29.3 us (25%)
  Pallas kernels  26.4 us (22%)
  local copies, waits for them, and re-layouts  5.88 us (5%)
    ppermute x23, waiting for transfers between devices, swap(): return lax.ppermute(value, 'dp', [(i, i ^ bits) for i in among])  44.8 us
    pallas_call x16, Pallas kernels, local_kernel(): pl.pallas_call(body, out_shape=tuple(outs), in_specs=[SMEM] * scalars + [...  23.6 us
    ppermute x23, starting transfers between devices, swap(): return lax.ppermute(value, 'dp', [(i, i ^ bits) for i in among])  20.4 us
    ppermute x4, waiting for transfers between devices, finish(): arrived[0, relative] = lax.ppermute(own, ('section', 'dp'), ring)  7.23 us
    ppermute x4, starting transfers between devices, finish(): arrived[0, relative] = lax.ppermute(own, ('section', 'dp'), ring)  6.36 us
    unnamed x18, local copies, waits for them, and re-layouts  5.88 us
    ppermute x4, waiting for transfers between devices, finish(): arrived[1, relative] = lax.ppermute(other, ('section', 'dp'), cross)  4.66 us
    pallas_call x1, Pallas kernels, on_chip_grid(): pl.pallas_call(prepare_kernel, out_shape=(shape((11,), jnp.int32), shape(...  2.78 us
  transfers between devices with their start and end apart: 31, of which 14 were waited for; matrix products, arithmetic and copies ran while one was open for 0% of the time, Pallas kernels for 21%

profile of v2, /device:TPU:0, one launch (start us, length us, event | category | flops | bytes accessed | tf_op | source)
XLA Modules:
  0.0 118.6 jit_solution(11789863456077333251)
XLA Ops:
  0.6 2.9 %collective-permute-start.2 = (bf16[2,128,2048]{2,1,0:T(8,128)(2,1)}, bf16[2,128,2048]{2,1,0:T(8,128)(2,1)}, u32[]{:S(2)}, u32[]{:S(2)}) collective-permute-start(bf16[2,128,2048]{2,1,0:T(8,128)(2,1)} %bitcast.9), channel_id=1, source_target_pairs={{0,4},{1,5},{2,6},{3,7},{4,0},{5,1},{6,2},{7,3},{8,12},{9,13},{10,... | collective-permute-start | bytes 3145736 | tf_op jit(solution)/shard_map/ppermute | solution.py:555
  3.5 1.5 %collective-permute-start.4 = (bf16[320,2048]{1,0:T(8,128)(2,1)}, bf16[320,2048]{1,0:T(8,128)(2,1)}, u32[]{:S(2)}, u32[]{:S(2)}) collective-permute-start(bf16[320,2048]{1,0:T(8,128)(2,1)} %bitcast.16), channel_id=1, source_target_pairs={{0,2},{1,3},{2,0},{3,1},{4,6},{5,7},{6,4},{7,5},{8,10},{9,11},{10,... | collective-permute-start | bytes 3932168 | tf_op jit(solution)/shard_map/ppermute | solution.py:555
  7.6 2.8 %shard_map.82 = (s32[11]{0:T(128)S(1)}, f32[512,1024]{1,0:T(8,128)S(1)}, f32[512,128]{1,0:T(8,128)S(1)}, f32[512,128]{1,0:T(8,128)S(1)}, bf16[1024,256]{1,0:T(8,128)(2,1)S(1)}, /*index=5*/bf16[1024,256]{1,0:T(8,128)(2,1)S(1)}) custom-call(s32[1]{0:T(128)} %bitcast.here_ref, s32[2,8]{1,0:T(2,128)S(1)} %bitcast.20, f32[1,128]{1,0:T(1,128)S(1)} %copy-done.8, ...), custom_call_target="tpu_custom_call" | custom-call | tf_op jit(solution)/shard_map/pallas_call | solution.py:574
  13.7 2.1 %shard_map.83 = (bf16[256,640]{1,0:T(8,128)(2,1)S(1)}, bf16[256,2048]{1,0:T(8,128)(2,1)S(1)}) custom-call(s32[11]{0:T(128)S(1)} %get-tuple-element.46.place_ref, bf16[2,128,2048]{2,1,0:T(8,128)(2,1)S(1)} %bitcast.10, bf16[2,128,2048]{2,1,0:T(8,128)(2,1)S(1)} %collective-permute-done.x1_ref, f32[1,2048]{1,0:T(1,128)S(1)} %copy-done.4, ...), custom_call_target="tpu_custom_call" | custom-call | flops 671088640 | bytes 6628396 | tf_op jit(solution)/shard_map/pallas_call | solution.py:150
  15.8 11.4 %collective-permute-done.2.x0_ref = bf16[2,128,2048]{2,1,0:T(8,128)(2,1)} collective-permute-done((bf16[2,128,2048]{2,1,0:T(8,128)(2,1)}, bf16[2,128,2048]{2,1,0:T(8,128)(2,1)}, u32[]{:S(2)}, u32[]{:S(2)}) %collective-permute-start.2) | collective-permute-done | bytes 1048608 | tf_op jit(solution)/shard_map/ppermute | solution.py:555
  27.2 7.1 %collective-permute-done.4.w_own = bf16[320,2048]{1,0:T(8,128)(2,1)} collective-permute-done((bf16[320,2048]{1,0:T(8,128)(2,1)}, bf16[320,2048]{1,0:T(8,128)(2,1)}, u32[]{:S(2)}, u32[]{:S(2)}) %collective-permute-start.4) | collective-permute-done | bytes 1310752 | tf_op jit(solution)/shard_map/ppermute | solution.py:555
  34.6 1.7 %collective-permute-start.15 = (bf16[1024,256]{1,0:T(8,128)(2,1)S(1)}, bf16[1024,256]{1,0:T(8,128)(2,1)S(1)}, u32[]{:S(2)}, u32[]{:S(2)}) collective-permute-start(bf16[1024,256]{1,0:T(8,128)(2,1)S(1)} %get-tuple-element.72.w0_ref), channel_id=1, source_target_pairs={{0,2},{1,3},{2,0},{3,1},{4,6},{5,7},{6,4},{7,5},{8,10},{9,11},{10,... | collective-permute-start | bytes 1572872 | tf_op jit(solution)/shard_map/ppermute | solution.py:555
  36.3 2.8 %shard_map.84 = (bf16[256,640]{1,0:T(8,128)(2,1)S(1)}, bf16[256,2048]{1,0:T(8,128)(2,1)S(1)}) custom-call(s32[11]{0:T(128)S(1)} %get-tuple-element.46.place_ref, bf16[2,128,2048]{2,1,0:T(8,128)(2,1)} %collective-permute-done.2.x0_ref, bf16[2,128,2048]{2,1,0:T(8,128)(2,1)S(1)} %collective-permute-done.3.x1_ref, f32[1,2048]{1,0:T(1,128)S(1)} %copy-done.4, ...), custom_call_target="tpu_custom_call" | custom-call | flops 671088640 | bytes 6628396 | tf_op jit(solution)/shard_map/pallas_call | solution.py:150
  39.1 3.7 %shard_map.85 = (bf16[512,1280]{1,0:T(8,128)(2,1)S(1)}, bf16[256,256]{1,0:T(8,128)(2,1)S(1)}, bf16[256,256]{1,0:T(8,128)(2,1)S(1)}, bf16[256,256]{1,0:T(8,128)(2,1)S(1)}, bf16[256,256]{1,0:T(8,128)(2,1)S(1)}) custom-call(s32[11]{0:T(128)S(1)} %get-tuple-element.46.place_ref, bf16[256,2048]{1,0:T(8,128)(2,1)S(1)} %get-tuple-element.49.normed0_ref, ...), custom_call_target="tpu_custom_call" | custom-call | flops 1342177280 | bytes 7734316 | tf_op jit(solution)/shard_map/pallas_call | solution.py:150
  42.8 1.6 %collective-permute-start.6 = (bf16[256,256]{1,0:T(8,128)(2,1)S(1)}, bf16[256,256]{1,0:T(8,128)(2,1)S(1)}, u32[]{:S(2)}, u32[]{:S(2)}) collective-permute-start(bf16[256,256]{1,0:T(8,128)(2,1)S(1)} %get-tuple-element.57), channel_id=1, source_target_pairs={{0,4},{1,5},{2,6},{3,7},{4,0},{5,1},{6,2},{7,3},{8,12},{9,13},{10,... | collective-permute-start | bytes 393224 | tf_op jit(solution)/shard_map/ppermute | solution.py:555
  44.9 4.2 %collective-permute-done.13.w0_ref = bf16[1024,256]{1,0:T(8,128)(2,1)S(1)} collective-permute-done((bf16[1024,256]{1,0:T(8,128)(2,1)S(1)}, bf16[1024,256]{1,0:T(8,128)(2,1)S(1)}, u32[]{:S(2)}, u32[]{:S(2)}) %collective-permute-start.13) | collective-permute-done | bytes 524320 | tf_op jit(solution)/shard_map/ppermute | solution.py:555
  49.8 2.1 %collective-permute-done.6.swap_a_ref = bf16[256,256]{1,0:T(8,128)(2,1)S(1)} collective-permute-done((bf16[256,256]{1,0:T(8,128)(2,1)S(1)}, bf16[256,256]{1,0:T(8,128)(2,1)S(1)}, u32[]{:S(2)}, u32[]{:S(2)}) %collective-permute-start.6) | collective-permute-done | bytes 131104 | tf_op jit(solution)/shard_map/ppermute | solution.py:555
  51.9 3.4 %collective-permute-start.10 = (bf16[256,256]{1,0:T(8,128)(2,1)S(1)}, bf16[256,256]{1,0:T(8,128)(2,1)S(1)}, u32[]{:S(2)}, u32[]{:S(2)}) collective-permute-start(bf16[256,256]{1,0:T(8,128)(2,1)S(1)} %collective-permute-done.6.swap_a_ref), channel_id=1, source_target_pairs={{0,2},{1,3},{2,0},{3,1},{8,10},{9,11},{10,8},{11,9},{16,18},{17,19... | collective-permute-start | bytes 393224 | tf_op jit(solution)/shard_map/ppermute | solution.py:555
  55.4 1.5 %shard_map.86 = (f32[256,2048]{1,0:T(8,128)S(1)}, f32[256,1024]{1,0:T(8,128)S(1)}) custom-call(s32[11]{0:T(128)S(1)} %get-tuple-element.46.place_ref, bf16[512,1280]{1,0:T(8,128)(2,1)S(1)} %get-tuple-element.56.full_ref, bf16[256,256]{1,0:T(8,128)(2,1)S(1)} %collective-permute-done.6.swap_a_ref, bf16[256,256]{1,0:T(8,128)(2,1)S(1)} %collective-permute-done.7.swap_b_ref, ...), custom_call_target="tpu_custom_call" | custom-call | flops 536870912 | bytes 7077932 | tf_op jit(solution)/shard_map/pallas_call | solution.py:150
  56.9 1.8 %collective-permute-done.10.far0_ref = bf16[256,256]{1,0:T(8,128)(2,1)S(1)} collective-permute-done((bf16[256,256]{1,0:T(8,128)(2,1)S(1)}, bf16[256,256]{1,0:T(8,128)(2,1)S(1)}, u32[]{:S(2)}, u32[]{:S(2)}) %collective-permute-start.10) | collective-permute-done | bytes 131104 | tf_op jit(solution)/shard_map/ppermute | solution.py:555
  58.8 1.7 %shard_map.87.a_ref = bf16[256,1024]{1,0:T(8,128)(2,1)S(1)} custom-call(s32[11]{0:T(128)S(1)} %get-tuple-element.46.place_ref, bf16[512,1280]{1,0:T(8,128)(2,1)S(1)} %get-tuple-element.56.full_ref, bf16[256,256]{1,0:T(8,128)(2,1)S(1)} %collective-permute-done.6.swap_a_ref, bf16[256,256]{1,0:T(8,128)(2,1)S(1)} %collective-permute-done.7.swap_b_ref, ...), custom_call_target="tpu_custom_call" | custom-call | flops 268435456 | bytes 7602220 | tf_op jit(solution)/shard_map/pallas_call | solution.py:150
  60.6 1.5 %collective-permute-start.19 = (bf16[1024,256]{1,0:T(8,128)(2,1)S(1)}, bf16[1024,256]{1,0:T(8,128)(2,1)S(1)}, u32[]{:S(2)}, u32[]{:S(2)}) collective-permute-start(bf16[1024,256]{1,0:T(8,128)(2,1)S(1)} %collective-permute-done.13.w0_ref), channel_id=1, source_target_pairs={{0,2},{1,3},{2,0},{3,1},{4,6},{5,7},{6,4},{7,5},{8,10},{9,11},{10,... | collective-permute-start | bytes 1572872 | tf_op jit(solution)/shard_map/ppermute | solution.py:555
  63.9 2.6 %collective-permute-start.8 = (bf16[256,256]{1,0:T(8,128)(2,1)S(1)}, bf16[256,256]{1,0:T(8,128)(2,1)S(1)}, u32[]{:S(2)}, u32[]{:S(2)}) collective-permute-start(bf16[256,256]{1,0:T(8,128)(2,1)S(1)} %collective-permute-done.7.swap_b_ref), channel_id=1, source_target_pairs={{0,2},{1,3},{2,0},{3,1},{8,10},{9,11},{10,8},{11,9},{16,18},{17,19... | collective-permute-start | bytes 393224 | tf_op jit(solution)/shard_map/ppermute | solution.py:555
  67.5 1.5 %shard_map.90 = (f32[256,2048]{1,0:T(8,128)S(1)}, f32[256,1024]{1,0:T(8,128)S(1)}) custom-call(s32[11]{0:T(128)S(1)} %get-tuple-element.46.place_ref, bf16[512,1280]{1,0:T(8,128)(2,1)S(1)} %get-tuple-element.56.full_ref, bf16[256,256]{1,0:T(8,128)(2,1)S(1)} %collective-permute-done.6.swap_a_ref, bf16[256,256]{1,0:T(8,128)(2,1)S(1)} %collective-permute-done.7.swap_b_ref, ...), custom_call_target="tpu_custom_call" | custom-call | flops 536870912 | bytes 7077932 | tf_op jit(solution)/shard_map/pallas_call | solution.py:150
  70.1 7.7 %collective-permute-done.8.far0_ref = bf16[256,256]{1,0:T(8,128)(2,1)S(1)} collective-permute-done((bf16[256,256]{1,0:T(8,128)(2,1)S(1)}, bf16[256,256]{1,0:T(8,128)(2,1)S(1)}, u32[]{:S(2)}, u32[]{:S(2)}) %collective-permute-start.8) | collective-permute-done | bytes 131104 | tf_op jit(solution)/shard_map/ppermute | solution.py:555
  79.6 2.0 %collective-permute-start.25 = (bf16[256,512]{1,0:T(8,128)(2,1)S(1)}, bf16[256,512]{1,0:T(8,128)(2,1)S(1)}, u32[]{:S(2)}, u32[]{:S(2)}) collective-permute-start(bf16[256,512]{1,0:T(8,128)(2,1)S(1)} %shard_map.91), channel_id=1, source_target_pairs={{0,4},{1,5},{2,6},{3,7},{4,0},{5,1},{6,2},{7,3},{8,12},{9,13},{10,... | collective-permute-start | bytes 786440 | tf_op jit(solution)/shard_map/ppermute | solution.py:555
  81.7 7.2 %collective-permute-done.17.came_ref = bf16[256,512]{1,0:T(8,128)(2,1)S(1)} collective-permute-done((bf16[256,512]{1,0:T(8,128)(2,1)S(1)}, bf16[256,512]{1,0:T(8,128)(2,1)S(1)}, u32[]{:S(2)}, u32[]{:S(2)}) %collective-permute-start.17) | collective-permute-done | bytes 262176 | tf_op jit(solution)/shard_map/ppermute | solution.py:555
  90.9 1.6 %collective-permute-start.24 = (bf16[128,512]{1,0:T(8,128)(2,1)S(1)}, bf16[128,512]{1,0:T(8,128)(2,1)S(1)}, u32[]{:S(2)}, u32[]{:S(2)}) collective-permute-start(bf16[128,512]{1,0:T(8,128)(2,1)S(1)} %get-tuple-element.79), channel_id=1, source_target_pairs={{0,8},{1,9},{2,10},{3,11},{4,12},{5,13},{6,14},{7,15},{8,16},{9,17... | collective-permute-start | bytes 393224 | tf_op jit(solution)/shard_map/ppermute | solution.py:675
  92.7 1.6 %collective-permute-start.18 = (bf16[128,512]{1,0:T(8,128)(2,1)S(1)}, bf16[128,512]{1,0:T(8,128)(2,1)S(1)}, u32[]{:S(2)}, u32[]{:S(2)}) collective-permute-start(bf16[128,512]{1,0:T(8,128)(2,1)S(1)} %get-tuple-element.76), channel_id=1, source_target_pairs={{0,8},{1,9},{2,10},{3,11},{4,12},{5,13},{6,14},{7,15},{8,16},{9,17... | collective-permute-start | bytes 393224 | tf_op jit(solution)/shard_map/ppermute | solution.py:675
  96.4 3.1 %collective-permute-done.22.came_ref = bf16[256,512]{1,0:T(8,128)(2,1)S(1)} collective-permute-done((bf16[256,512]{1,0:T(8,128)(2,1)S(1)}, bf16[256,512]{1,0:T(8,128)(2,1)S(1)}, u32[]{:S(2)}, u32[]{:S(2)}) %collective-permute-start.22) | collective-permute-done | bytes 262176 | tf_op jit(solution)/shard_map/ppermute | solution.py:555
  99.5 1.6 %collective-permute-start.26 = (bf16[128,512]{1,0:T(8,128)(2,1)S(1)}, bf16[128,512]{1,0:T(8,128)(2,1)S(1)}, u32[]{:S(2)}, u32[]{:S(2)}) collective-permute-start(bf16[128,512]{1,0:T(8,128)(2,1)S(1)} %get-tuple-element.82), channel_id=1, source_target_pairs={{0,8},{1,9},{2,10},{3,11},{4,12},{5,13},{6,14},{7,15},{8,16},{9,17... | collective-permute-start | bytes 393224 | tf_op jit(solution)/shard_map/ppermute | solution.py:675
  102.6 1.6 %collective-permute-start.23 = (bf16[128,512]{1,0:T(8,128)(2,1)S(1)}, bf16[128,512]{1,0:T(8,128)(2,1)S(1)}, u32[]{:S(2)}, u32[]{:S(2)}) collective-permute-start(bf16[128,512]{1,0:T(8,128)(2,1)S(1)} %get-tuple-element.81), channel_id=1, source_target_pairs={{0,8},{1,9},{2,10},{3,11},{4,12},{5,13},{6,14},{7,15},{8,16},{9,17... | collective-permute-start | bytes 393224 | tf_op jit(solution)/shard_map/ppermute | solution.py:675
  105.7 3.6 %collective-permute-done.26.refs_3_ = bf16[128,512]{1,0:T(8,128)(2,1)S(1)} collective-permute-done((bf16[128,512]{1,0:T(8,128)(2,1)S(1)}, bf16[128,512]{1,0:T(8,128)(2,1)S(1)}, u32[]{:S(2)}, u32[]{:S(2)}) %collective-permute-start.26) | collective-permute-done | bytes 131104 | tf_op jit(solution)/shard_map/ppermute | solution.py:675
  109.4 2.0 %collective-permute-done.30.refs_7_ = bf16[128,512]{1,0:T(8,128)(2,1)S(1)} collective-permute-done((bf16[128,512]{1,0:T(8,128)(2,1)S(1)}, bf16[128,512]{1,0:T(8,128)(2,1)S(1)}, u32[]{:S(2)}, u32[]{:S(2)}) %collective-permute-start.30) | collective-permute-done | bytes 131104 | tf_op jit(solution)/shard_map/ppermute | solution.py:676
  111.4 3.6 %collective-permute-done.23.refs_1_ = bf16[128,512]{1,0:T(8,128)(2,1)S(1)} collective-permute-done((bf16[128,512]{1,0:T(8,128)(2,1)S(1)}, bf16[128,512]{1,0:T(8,128)(2,1)S(1)}, u32[]{:S(2)}, u32[]{:S(2)}) %collective-permute-start.23) | collective-permute-done | bytes 131104 | tf_op jit(solution)/shard_map/ppermute | solution.py:675
  115.0 2.0 %collective-permute-done.28.refs_5_ = bf16[128,512]{1,0:T(8,128)(2,1)S(1)} collective-permute-done((bf16[128,512]{1,0:T(8,128)(2,1)S(1)}, bf16[128,512]{1,0:T(8,128)(2,1)S(1)}, u32[]{:S(2)}, u32[]{:S(2)}) %collective-permute-start.28) | collective-permute-done | bytes 131104 | tf_op jit(solution)/shard_map/ppermute | solution.py:676
  117.0 1.6 %shard_map.98 = bf16[2,128,2048]{2,1,0:T(8,128)(2,1)} custom-call(s32[11]{0:T(128)S(1)} %get-tuple-element.46.place_ref, bf16[128,512]{1,0:T(8,128)(2,1)S(1)} %collective-permute-done.18.refs_0_, bf16[128,512]{1,0:T(8,128)(2,1)S(1)} %collective-permute-done.23.refs_1_, bf16[128,512]{1,0:T(8,128)(2,1)S(1)} %collective-permute-done.24.refs_2_, ...), custom_call_target="tpu_custom_call" | custom-call | bytes 2097196 | tf_op jit(solution)/shard_map/pallas_call | solution.py:150
  (65 shorter events, 21.0 us)
Async XLA Ops:
  0.0 10.4 %collective-permute-start.1 = (bf16[320,2048]{1,0:T(8,128)(2,1)}, bf16[320,2048]{1,0:T(8,128)(2,1)S(1)}, u32[]{:S(2)}, u32[]{:S(2)}) collective-permute-start(bf16[320,2048]{1,0:T(8,128)(2,1)} %bitcast.15), channel_id=1, source_target_pairs={{0,1},{1,0},{2,3},{3,2},{4,5},{5,4},{6,7},{7,6},{8,9},{9,8},{10,11... | collective-permute-start | bytes 3932168 | tf_op jit(solution)/shard_map/ppermute | solution.py:555
  0.5 9.9 %collective-permute-start = (bf16[2,128,2048]{2,1,0:T(8,128)(2,1)}, bf16[2,128,2048]{2,1,0:T(8,128)(2,1)S(1)}, u32[]{:S(2)}, u32[]{:S(2)}) collective-permute-start(bf16[2,128,2048]{2,1,0:T(8,128)(2,1)} %bitcast.8), channel_id=1, source_target_pairs={{0,1},{1,0},{2,3},{3,2},{4,5},{5,4},{6,7},{7,6},{8,9},{9,8},{10,11... | collective-permute-start | bytes 3145736 | tf_op jit(solution)/shard_map/ppermute | solution.py:555
  0.6 26.6 %collective-permute-start.2 = (bf16[2,128,2048]{2,1,0:T(8,128)(2,1)}, bf16[2,128,2048]{2,1,0:T(8,128)(2,1)}, u32[]{:S(2)}, u32[]{:S(2)}) collective-permute-start(bf16[2,128,2048]{2,1,0:T(8,128)(2,1)} %bitcast.9), channel_id=1, source_target_pairs={{0,4},{1,5},{2,6},{3,7},{4,0},{5,1},{6,2},{7,3},{8,12},{9,13},{10,... | collective-permute-start | bytes 3145736 | tf_op jit(solution)/shard_map/ppermute | solution.py:555
  3.5 30.8 %collective-permute-start.4 = (bf16[320,2048]{1,0:T(8,128)(2,1)}, bf16[320,2048]{1,0:T(8,128)(2,1)}, u32[]{:S(2)}, u32[]{:S(2)}) collective-permute-start(bf16[320,2048]{1,0:T(8,128)(2,1)} %bitcast.16), channel_id=1, source_target_pairs={{0,2},{1,3},{2,0},{3,1},{4,6},{5,7},{6,4},{7,5},{8,10},{9,11},{10,... | collective-permute-start | bytes 3932168 | tf_op jit(solution)/shard_map/ppermute | solution.py:555
  13.7 22.6 %copy-start.2 = (bf16[1,2048,320]{1,2,0:T(8,128)(2,1)S(1)}, bf16[1,2048,320]{1,2,0:T(8,128)(2,1)}, u32[]{:S(2)}) copy-start(bf16[1,2048,320]{1,2,0:T(8,128)(2,1)} %param.10) | copy-start | bytes 3932164
  27.2 7.1 %collective-permute-start.3 = (bf16[2,128,2048]{2,1,0:T(8,128)(2,1)}, bf16[2,128,2048]{2,1,0:T(8,128)(2,1)S(1)}, u32[]{:S(2)}, u32[]{:S(2)}) collective-permute-start(bf16[2,128,2048]{2,1,0:T(8,128)(2,1)} %collective-permute-done.2.x0_ref), channel_id=1, source_target_pairs={{0,1},{1,0},{2,3},{3,2},{4,5},{5,4},{6,7},{7,6},{8,9},{9,8},{10,11... | collective-permute-start | bytes 3145736 | tf_op jit(solution)/shard_map/ppermute | solution.py:555
  34.3 4.8 %collective-permute-start.5 = (bf16[320,2048]{1,0:T(8,128)(2,1)}, bf16[320,2048]{1,0:T(8,128)(2,1)S(1)}, u32[]{:S(2)}, u32[]{:S(2)}) collective-permute-start(bf16[320,2048]{1,0:T(8,128)(2,1)} %collective-permute-done.4.w_own), channel_id=1, source_target_pairs={{0,1},{1,0},{2,3},{3,2},{4,5},{5,4},{6,7},{7,6},{8,9},{9,8},{10,11... | collective-permute-start | bytes 3932168 | tf_op jit(solution)/shard_map/ppermute | solution.py:555
  34.3 14.8 %collective-permute-start.13 = (bf16[1024,256]{1,0:T(8,128)(2,1)S(1)}, bf16[1024,256]{1,0:T(8,128)(2,1)S(1)}, u32[]{:S(2)}, u32[]{:S(2)}) collective-permute-start(bf16[1024,256]{1,0:T(8,128)(2,1)S(1)} %get-tuple-element.67), channel_id=1, source_target_pairs={{0,4},{1,5},{2,6},{3,7},{4,0},{5,1},{6,2},{7,3},{8,12},{9,13},{10,... | collective-permute-start | bytes 1572872 | tf_op jit(solution)/shard_map/ppermute | solution.py:555
  34.6 25.9 %collective-permute-start.15 = (bf16[1024,256]{1,0:T(8,128)(2,1)S(1)}, bf16[1024,256]{1,0:T(8,128)(2,1)S(1)}, u32[]{:S(2)}, u32[]{:S(2)}) collective-permute-start(bf16[1024,256]{1,0:T(8,128)(2,1)S(1)} %get-tuple-element.72.w0_ref), channel_id=1, source_target_pairs={{0,2},{1,3},{2,0},{3,1},{4,6},{5,7},{6,4},{7,5},{8,10},{9,11},{10,... | collective-permute-start | bytes 1572872 | tf_op jit(solution)/shard_map/ppermute | solution.py:555
  42.8 9.1 %collective-permute-start.6 = (bf16[256,256]{1,0:T(8,128)(2,1)S(1)}, bf16[256,256]{1,0:T(8,128)(2,1)S(1)}, u32[]{:S(2)}, u32[]{:S(2)}) collective-permute-start(bf16[256,256]{1,0:T(8,128)(2,1)S(1)} %get-tuple-element.57), channel_id=1, source_target_pairs={{0,4},{1,5},{2,6},{3,7},{4,0},{5,1},{6,2},{7,3},{8,12},{9,13},{10,... | collective-permute-start | bytes 393224 | tf_op jit(solution)/shard_map/ppermute | solution.py:555
  44.4 10.9 %collective-permute-start.7 = (bf16[256,256]{1,0:T(8,128)(2,1)S(1)}, bf16[256,256]{1,0:T(8,128)(2,1)S(1)}, u32[]{:S(2)}, u32[]{:S(2)}) collective-permute-start(bf16[256,256]{1,0:T(8,128)(2,1)S(1)} %get-tuple-element.58), channel_id=1, source_target_pairs={{0,4},{1,5},{2,6},{3,7},{4,0},{5,1},{6,2},{7,3},{8,12},{9,13},{10,... | collective-permute-start | bytes 393224 | tf_op jit(solution)/shard_map/ppermute | solution.py:555
  44.9 17.2 %collective-permute-start.12 = (bf16[1024,256]{1,0:T(8,128)(2,1)S(1)}, bf16[1024,256]{1,0:T(8,128)(2,1)S(1)}, u32[]{:S(2)}, u32[]{:S(2)}) collective-permute-start(bf16[1024,256]{1,0:T(8,128)(2,1)S(1)} %get-tuple-element.72.w0_ref), channel_id=1, source_target_pairs={{0,1},{1,0},{2,3},{3,2},{4,5},{5,4},{6,7},{7,6},{8,9},{9,8},{10,11... | collective-permute-start | bytes 1572872 | tf_op jit(solution)/shard_map/ppermute | solution.py:555
  49.1 7.8 %collective-permute-start.11 = (bf16[256,256]{1,0:T(8,128)(2,1)S(1)}, bf16[256,256]{1,0:T(8,128)(2,1)S(1)}, u32[]{:S(2)}, u32[]{:S(2)}) collective-permute-start(bf16[256,256]{1,0:T(8,128)(2,1)S(1)} %get-tuple-element.61.kv_a_ref), channel_id=1, source_target_pairs={{4,6},{5,7},{6,4},{7,5},{12,14},{13,15},{14,12},{15,13},{20,22},{2... | collective-permute-start | bytes 393224 | tf_op jit(solution)/shard_map/ppermute | solution.py:555
  51.9 6.8 %collective-permute-start.10 = (bf16[256,256]{1,0:T(8,128)(2,1)S(1)}, bf16[256,256]{1,0:T(8,128)(2,1)S(1)}, u32[]{:S(2)}, u32[]{:S(2)}) collective-permute-start(bf16[256,256]{1,0:T(8,128)(2,1)S(1)} %collective-permute-done.6.swap_a_ref), channel_id=1, source_target_pairs={{0,2},{1,3},{2,0},{3,1},{8,10},{9,11},{10,8},{11,9},{16,18},{17,19... | collective-permute-start | bytes 393224 | tf_op jit(solution)/shard_map/ppermute | solution.py:555
  55.3 8.6 %collective-permute-start.14 = (bf16[1024,256]{1,0:T(8,128)(2,1)S(1)}, bf16[1024,256]{1,0:T(8,128)(2,1)S(1)}, u32[]{:S(2)}, u32[]{:S(2)}) collective-permute-start(bf16[1024,256]{1,0:T(8,128)(2,1)S(1)} %collective-permute-done.13.w0_ref), channel_id=1, source_target_pairs={{0,1},{1,0},{2,3},{3,2},{4,5},{5,4},{6,7},{7,6},{8,9},{9,8},{10,11... | collective-permute-start | bytes 1572872 | tf_op jit(solution)/shard_map/ppermute | solution.py:555
  60.5 8.5 %collective-permute-start.16 = (bf16[1024,256]{1,0:T(8,128)(2,1)S(1)}, bf16[1024,256]{1,0:T(8,128)(2,1)S(1)}, u32[]{:S(2)}, u32[]{:S(2)}) collective-permute-start(bf16[1024,256]{1,0:T(8,128)(2,1)S(1)} %collective-permute-done.15.w0_ref), channel_id=1, source_target_pairs={{0,1},{1,0},{2,3},{3,2},{4,5},{5,4},{6,7},{7,6},{8,9},{9,8},{10,11... | collective-permute-start | bytes 1572872 | tf_op jit(solution)/shard_map/ppermute | solution.py:555
  60.6 18.9 %collective-permute-start.19 = (bf16[1024,256]{1,0:T(8,128)(2,1)S(1)}, bf16[1024,256]{1,0:T(8,128)(2,1)S(1)}, u32[]{:S(2)}, u32[]{:S(2)}) collective-permute-start(bf16[1024,256]{1,0:T(8,128)(2,1)S(1)} %collective-permute-done.13.w0_ref), channel_id=1, source_target_pairs={{0,2},{1,3},{2,0},{3,1},{4,6},{5,7},{6,4},{7,5},{8,10},{9,11},{10,... | collective-permute-start | bytes 1572872 | tf_op jit(solution)/shard_map/ppermute | solution.py:555
  63.1 15.3 %collective-permute-start.20 = (bf16[256,512]{1,0:T(8,128)(2,1)S(1)}, bf16[256,512]{1,0:T(8,128)(2,1)S(1)}, u32[]{:S(2)}, u32[]{:S(2)}) collective-permute-start(bf16[256,512]{1,0:T(8,128)(2,1)S(1)} %shard_map.88), channel_id=1, source_target_pairs={{0,4},{1,5},{2,6},{3,7},{4,0},{5,1},{6,2},{7,3},{8,12},{9,13},{10,... | collective-permute-start | bytes 786440 | tf_op jit(solution)/shard_map/ppermute | solution.py:555
  63.2 6.9 %collective-permute-start.9 = (bf16[256,256]{1,0:T(8,128)(2,1)S(1)}, bf16[256,256]{1,0:T(8,128)(2,1)S(1)}, u32[]{:S(2)}, u32[]{:S(2)}) collective-permute-start(bf16[256,256]{1,0:T(8,128)(2,1)S(1)} %get-tuple-element.59.kv_b_ref), channel_id=1, source_target_pairs={{4,6},{5,7},{6,4},{7,5},{12,14},{13,15},{14,12},{15,13},{20,22},{2... | collective-permute-start | bytes 393224 | tf_op jit(solution)/shard_map/ppermute | solution.py:555
  63.9 13.8 %collective-permute-start.8 = (bf16[256,256]{1,0:T(8,128)(2,1)S(1)}, bf16[256,256]{1,0:T(8,128)(2,1)S(1)}, u32[]{:S(2)}, u32[]{:S(2)}) collective-permute-start(bf16[256,256]{1,0:T(8,128)(2,1)S(1)} %collective-permute-done.7.swap_b_ref), channel_id=1, source_target_pairs={{0,2},{1,3},{2,0},{3,1},{8,10},{9,11},{10,8},{11,9},{16,18},{17,19... | collective-permute-start | bytes 393224 | tf_op jit(solution)/shard_map/ppermute | solution.py:555
  79.5 10.3 %collective-permute-start.21 = (bf16[1024,256]{1,0:T(8,128)(2,1)S(1)}, bf16[1024,256]{1,0:T(8,128)(2,1)S(1)}, u32[]{:S(2)}, u32[]{:S(2)}) collective-permute-start(bf16[1024,256]{1,0:T(8,128)(2,1)S(1)} %collective-permute-done.19.w0_ref), channel_id=1, source_target_pairs={{0,1},{1,0},{2,3},{3,2},{4,5},{5,4},{6,7},{7,6},{8,9},{9,8},{10,11... | collective-permute-start | bytes 1572872 | tf_op jit(solution)/shard_map/ppermute | solution.py:555
  79.6 9.2 %collective-permute-start.17 = (bf16[256,512]{1,0:T(8,128)(2,1)S(1)}, bf16[256,512]{1,0:T(8,128)(2,1)S(1)}, u32[]{:S(2)}, u32[]{:S(2)}) collective-permute-start(bf16[256,512]{1,0:T(8,128)(2,1)S(1)} %shard_map.89), channel_id=1, source_target_pairs={{0,4},{1,5},{2,6},{3,7},{4,0},{5,1},{6,2},{7,3},{8,12},{9,13},{10,... | collective-permute-start | bytes 786440 | tf_op jit(solution)/shard_map/ppermute | solution.py:555
  79.6 14.8 %collective-permute-start.25 = (bf16[256,512]{1,0:T(8,128)(2,1)S(1)}, bf16[256,512]{1,0:T(8,128)(2,1)S(1)}, u32[]{:S(2)}, u32[]{:S(2)}) collective-permute-start(bf16[256,512]{1,0:T(8,128)(2,1)S(1)} %shard_map.91), channel_id=1, source_target_pairs={{0,4},{1,5},{2,6},{3,7},{4,0},{5,1},{6,2},{7,3},{8,12},{9,13},{10,... | collective-permute-start | bytes 786440 | tf_op jit(solution)/shard_map/ppermute | solution.py:555
  90.8 8.7 %collective-permute-start.22 = (bf16[256,512]{1,0:T(8,128)(2,1)S(1)}, bf16[256,512]{1,0:T(8,128)(2,1)S(1)}, u32[]{:S(2)}, u32[]{:S(2)}) collective-permute-start(bf16[256,512]{1,0:T(8,128)(2,1)S(1)} %shard_map.95), channel_id=1, source_target_pairs={{0,4},{1,5},{2,6},{3,7},{4,0},{5,1},{6,2},{7,3},{8,12},{9,13},{10,... | collective-permute-start | bytes 786440 | tf_op jit(solution)/shard_map/ppermute | solution.py:555
  90.9 11.2 %collective-permute-start.24 = (bf16[128,512]{1,0:T(8,128)(2,1)S(1)}, bf16[128,512]{1,0:T(8,128)(2,1)S(1)}, u32[]{:S(2)}, u32[]{:S(2)}) collective-permute-start(bf16[128,512]{1,0:T(8,128)(2,1)S(1)} %get-tuple-element.79), channel_id=1, source_target_pairs={{0,8},{1,9},{2,10},{3,11},{4,12},{5,13},{6,14},{7,15},{8,16},{9,17... | collective-permute-start | bytes 393224 | tf_op jit(solution)/shard_map/ppermute | solution.py:675
  92.5 10.1 %collective-permute-start.29 = (bf16[128,512]{1,0:T(8,128)(2,1)S(1)}, bf16[128,512]{1,0:T(8,128)(2,1)S(1)}, u32[]{:S(2)}, u32[]{:S(2)}) collective-permute-start(bf16[128,512]{1,0:T(8,128)(2,1)S(1)} %get-tuple-element.85), channel_id=1, source_target_pairs={{0,9},{1,8},{2,11},{3,10},{4,13},{5,12},{6,15},{7,14},{8,17},{9,16... | collective-permute-start | bytes 393224 | tf_op jit(solution)/shard_map/ppermute | solution.py:676
  92.7 11.5 %collective-permute-start.18 = (bf16[128,512]{1,0:T(8,128)(2,1)S(1)}, bf16[128,512]{1,0:T(8,128)(2,1)S(1)}, u32[]{:S(2)}, u32[]{:S(2)}) collective-permute-start(bf16[128,512]{1,0:T(8,128)(2,1)S(1)} %get-tuple-element.76), channel_id=1, source_target_pairs={{0,8},{1,9},{2,10},{3,11},{4,12},{5,13},{6,14},{7,15},{8,16},{9,17... | collective-permute-start | bytes 393224 | tf_op jit(solution)/shard_map/ppermute | solution.py:675
  94.4 11.3 %collective-permute-start.27 = (bf16[128,512]{1,0:T(8,128)(2,1)S(1)}, bf16[128,512]{1,0:T(8,128)(2,1)S(1)}, u32[]{:S(2)}, u32[]{:S(2)}) collective-permute-start(bf16[128,512]{1,0:T(8,128)(2,1)S(1)} %get-tuple-element.83), channel_id=1, source_target_pairs={{0,9},{1,8},{2,11},{3,10},{4,13},{5,12},{6,15},{7,14},{8,17},{9,16... | collective-permute-start | bytes 393224 | tf_op jit(solution)/shard_map/ppermute | solution.py:676
  99.5 9.9 %collective-permute-start.26 = (bf16[128,512]{1,0:T(8,128)(2,1)S(1)}, bf16[128,512]{1,0:T(8,128)(2,1)S(1)}, u32[]{:S(2)}, u32[]{:S(2)}) collective-permute-start(bf16[128,512]{1,0:T(8,128)(2,1)S(1)} %get-tuple-element.82), channel_id=1, source_target_pairs={{0,8},{1,9},{2,10},{3,11},{4,12},{5,13},{6,14},{7,15},{8,16},{9,17... | collective-permute-start | bytes 393224 | tf_op jit(solution)/shard_map/ppermute | solution.py:675
  102.1 9.3 %collective-permute-start.30 = (bf16[128,512]{1,0:T(8,128)(2,1)S(1)}, bf16[128,512]{1,0:T(8,128)(2,1)S(1)}, u32[]{:S(2)}, u32[]{:S(2)}) collective-permute-start(bf16[128,512]{1,0:T(8,128)(2,1)S(1)} %get-tuple-element.86), channel_id=1, source_target_pairs={{0,9},{1,8},{2,11},{3,10},{4,13},{5,12},{6,15},{7,14},{8,17},{9,16... | collective-permute-start | bytes 393224 | tf_op jit(solution)/shard_map/ppermute | solution.py:676
  102.6 12.4 %collective-permute-start.23 = (bf16[128,512]{1,0:T(8,128)(2,1)S(1)}, bf16[128,512]{1,0:T(8,128)(2,1)S(1)}, u32[]{:S(2)}, u32[]{:S(2)}) collective-permute-start(bf16[128,512]{1,0:T(8,128)(2,1)S(1)} %get-tuple-element.81), channel_id=1, source_target_pairs={{0,8},{1,9},{2,10},{3,11},{4,12},{5,13},{6,14},{7,15},{8,16},{9,17... | collective-permute-start | bytes 393224 | tf_op jit(solution)/shard_map/ppermute | solution.py:675
  104.2 12.8 %collective-permute-start.28 = (bf16[128,512]{1,0:T(8,128)(2,1)S(1)}, bf16[128,512]{1,0:T(8,128)(2,1)S(1)}, u32[]{:S(2)}, u32[]{:S(2)}) collective-permute-start(bf16[128,512]{1,0:T(8,128)(2,1)S(1)} %get-tuple-element.84), channel_id=1, source_target_pairs={{0,9},{1,8},{2,11},{3,10},{4,13},{5,12},{6,15},{7,14},{8,17},{9,16... | collective-permute-start | bytes 393224 | tf_op jit(solution)/shard_map/ppermute | solution.py:676
  (8 other events, 16.3 us)

commit v3 on v2

--- a/solution.py
+++ b/solution.py
@@ -145,7 +145,7 @@
 SMEM = pl.BlockSpec(memory_space=pltpu.SMEM)
 
 
-def local_kernel(body, outs, inputs, scratch=(), flops=0, grant=24, scalars=1):
+def local_kernel(body, outs, inputs, scratch=(), flops=0, grant=12, scalars=1):
     moved = sum(math.prod(s.shape) * s.dtype.itemsize for s in (*outs, *inputs))
     return pl.pallas_call(
         body,
@@ -272,11 +272,22 @@
             middle[pl.ds(there, rest), :] = piece[pl.ds(here, rest), :]
 
 
+def norm_rows(core, x_ref, gain_ref):
+    x = x_ref[core].astype(jnp.float32)
+    scale = lax.rsqrt(jnp.mean(x * x, axis=-1, keepdims=True) + EPSILON)
+    return (x * scale * gain_ref[...]).astype(jnp.bfloat16)
+
+
+def norm_kernel(place_ref, x_ref, gain_ref, normed_ref):
+    normed_ref[...] = norm_rows(place_ref[2], x_ref, gain_ref)
+
+
 def project_own_kernel(
     offset,
+    keep,
     place_ref,
-    x0_ref,
-    x1_ref,
+    ready_ref,
+    x_ref,
     gain_ref,
     w_own,
     w_partner,
@@ -286,17 +297,16 @@
     k_gain_ref,
     out_ref,
     normed_ref,
-    middle,
+    *rest_refs,
 ):
     line, column, core = place_ref[0], place_ref[1], place_ref[2]
-    rows = x0_ref.shape[1]
+    *kept, middle = rest_refs
     join_middle(core, middle, w_own, w_partner)
-    for number, x_ref in enumerate((x0_ref, x1_ref)):
-        x = x_ref[core].astype(jnp.float32)
-        scale = lax.rsqrt(jnp.mean(x * x, axis=-1, keepdims=True) + EPSILON)
-        normed_ref[number * rows : (number + 1) * rows, :] = (x * scale * gain_ref[...]).astype(
-            jnp.bfloat16
-        )
+    if keep:
+        kept[0][...] = w_partner[...]
+    rows = ready_ref.shape[0]
+    normed_ref[:rows, :] = ready_ref[...]
+    normed_ref[rows:, :] = norm_rows(core, x_ref, gain_ref)
     blocks = out_ref.shape[1] // HEAD
     span = slice(offset, offset + 2 * rows)
 
@@ -310,6 +320,7 @@
 
 
 def project_far_kernel(
+    order,
     place_ref,
     normed0_ref,
     normed1_ref,
@@ -322,10 +333,8 @@
     near0_ref,
     near1_ref,
     full,
-    swap_a_ref,
-    swap_b_ref,
-    kv_a_ref,
-    kv_b_ref,
+    swap_ref,
+    kv_ref,
     middle,
 ):
     line, column, core = place_ref[0], place_ref[1], place_ref[2]
@@ -334,45 +343,37 @@
     blocks = chip_width // HEAD
     which = 1 - column
     step = normed0_ref.shape[0]
-    own = pl.multiple_of(column * chip_width, HEAD)
-    for number, (normed_ref, near_ref) in enumerate(
-        ((normed0_ref, near0_ref), (normed1_ref, near1_ref))
-    ):
-        span = slice(number * step, (number + 1) * step)
-        full[span, pl.ds(own, chip_width)] = near_ref[...]
-
-        def write(block, projected, span=span):
-            head = (line * 2 + which) * blocks + block
-            start = pl.multiple_of((which * blocks + block) * HEAD, HEAD)
-            full[span, pl.ds(start, HEAD)] = project_block(
-                projected, head, cos_ref[span, :], sin_ref[span, :], (q_gain_ref, k_gain_ref)
-            )
-
-        project_with(normed_ref[...], w_own, w_partner, middle, core, write)
+    part = column if order == 0 else 1 - column
+    normed = jnp.where(part == 0, normed0_ref[...], normed1_ref[...])
+    span = pl.ds(pl.multiple_of(part * step, step), step)
+    cosine, sine = cos_ref[span, :], sin_ref[span, :]
+    full[:, pl.ds(pl.multiple_of(column * chip_width, HEAD), chip_width)] = jnp.where(
+        part == 0, near0_ref[...], near1_ref[...]
+    )
+
+    def write(block, projected):
+        head = (line * 2 + which) * blocks + block
+        start = pl.multiple_of((which * blocks + block) * HEAD, HEAD)
+        full[:, pl.ds(start, HEAD)] = project_block(
+            projected, head, cosine, sine, (q_gain_ref, k_gain_ref)
+        )
+
+    project_with(normed, w_own, w_partner, middle, core, write)
     inner = HEADS // 2 * HEAD
-    pair = swap_a_ref.shape[1]
+    pair = swap_ref.shape[1]
     half = pair // 2
     left = inner - pair
-    first = pl.ds(pl.multiple_of(column * step, step), step)
-    second = pl.ds(pl.multiple_of((1 - column) * step, step), step)
 
     @pl.when(line == 0)
     def _():
-        swap_a_ref[...] = full[first, inner : inner + pair]
-        swap_b_ref[...] = full[second, inner : inner + pair]
-        kv_a_ref[...] = jnp.zeros_like(kv_a_ref)
-        kv_b_ref[...] = jnp.zeros_like(kv_b_ref)
+        swap_ref[...] = full[:, inner : inner + pair]
+        kv_ref[...] = jnp.zeros_like(kv_ref)
 
     @pl.when(line == 1)
     def _():
-        for out, rows, skip in (
-            (swap_a_ref, first, 0),
-            (swap_b_ref, second, 0),
-            (kv_a_ref, second, half),
-            (kv_b_ref, first, half),
-        ):
-            out[:, :half] = full[rows, left + skip : left + skip + half]
-            out[:, half:] = full[rows, left + skip + pair : left + skip + pair + half]
+        for out, skip in ((swap_ref, 0), (kv_ref, half)):
+            out[:, :half] = full[:, left + skip : left + skip + half]
+            out[:, half:] = full[:, left + skip + pair : left + skip + pair + half]
 
 
 SHRINK = math.log2(math.e) / math.sqrt(HEAD)
@@ -382,17 +383,17 @@
     return jnp.concatenate([values, jnp.ones_like(values)], axis=1)
 
 
-def query_of(head, part, place_ref, full_ref, swap_a_ref, swap_b_ref):
+def query_of(head, part, place_ref, full_refs, swap_refs):
     line, column = place_ref[0], place_ref[1]
-    rows = swap_a_ref.shape[0]
-    span = slice(part * rows, (part + 1) * rows)
-    moved = swap_a_ref.shape[1] // HEAD
-    lanes = slice(head * HEAD, (head + 1) * HEAD)
+    moved = swap_refs[0].shape[1] // HEAD
+    start = pl.multiple_of(jnp.maximum(head - moved * line, 0) * HEAD, HEAD)
+    lanes = pl.ds(start, HEAD)
+    q = jnp.where(column == part, full_refs[0][:, lanes], full_refs[1][:, lanes])
     if head < moved:
-        came = jnp.where(column == 1 - part, swap_a_ref[:, lanes], swap_b_ref[:, lanes])
-        return jnp.where(line == 1, came, full_ref[span, lanes])
-    start = pl.multiple_of((head - moved * line) * HEAD, HEAD)
-    return full_ref[span, pl.ds(start, HEAD)]
+        there = slice(head * HEAD, (head + 1) * HEAD)
+        came = jnp.where(column == 1 - part, swap_refs[0][:, there], swap_refs[1][:, there])
+        q = jnp.where(line == 1, came, q)
+    return q
 
 
 def scores_of(q, keys, bias):
@@ -405,7 +406,8 @@
 def attend_near_kernel(
     part,
     place_ref,
-    full_ref,
+    full0_ref,
+    full1_ref,
     swap_a_ref,
     swap_b_ref,
     kv_a_ref,
@@ -429,7 +431,7 @@
         values = with_ones(near[block, half:])
         bias = bias_ref[span, block]
         for head in range(heads):
-            q = query_of(head, part, place_ref, full_ref, swap_a_ref, swap_b_ref)
+            q = query_of(head, part, place_ref, (full0_ref, full1_ref), (swap_a_ref, swap_b_ref))
             s = scores_of(q, keys, bias)
             top = jnp.max(s, axis=-1, keepdims=True)
             weight = jnp.exp2((s - top) * SHRINK).astype(jnp.bfloat16)
@@ -452,7 +454,8 @@
 def attend_far_kernel(
     part,
     place_ref,
-    full_ref,
+    full0_ref,
+    full1_ref,
     swap_a_ref,
     swap_b_ref,
     far0_ref,
@@ -487,7 +490,7 @@
         values = with_ones(far[:, half:])
         bias = bias_ref[span, pl.ds(pl.multiple_of(block * rows, rows), rows)]
         for head in range(heads):
-            q = query_of(head, part, place_ref, full_ref, swap_a_ref, swap_b_ref)
+            q = query_of(head, part, place_ref, (full0_ref, full1_ref), (swap_a_ref, swap_b_ref))
             s = scores_of(q, keys, bias)
             before = top_ref[:, head * HEAD : (head + 1) * HEAD]
             top = jnp.maximum(before, jnp.max(s, axis=-1, keepdims=True))
@@ -501,6 +504,25 @@
             finish(head, summed)
 
 
+def attend_kernel(part, place_ref, *refs):
+    fulls, swaps, kvs, fars, bias, (out_ref, near, sums, tops) = (
+        refs[0:2], refs[2:4], refs[4:6], refs[6:8], refs[8], refs[9:13]
+    )
+    attend_near_kernel(part, place_ref, *fulls, *swaps, *kvs, bias, sums, tops, near)
+    attend_far_kernel(part, place_ref, *fulls, *swaps, *fars, bias, sums, tops, out_ref)
+
+
+def attend_share_kernel(part, place_ref, *refs):
+    *before, w0_ref, w1_ref, out_ref, share_ref = refs
+    attend_far_kernel(part, place_ref, *before, out_ref)
+    share_kernel(place_ref, out_ref, w0_ref, w1_ref, share_ref)
+
+
+def share_two_kernel(place_ref, a_ref, w0_ref, w1_ref, w2_ref, w3_ref, out0_ref, out1_ref):
+    share_kernel(place_ref, a_ref, w0_ref, w1_ref, out0_ref)
+    share_kernel(place_ref, a_ref, w2_ref, w3_ref, out1_ref)
+
+
 def share_kernel(place_ref, a_ref, w0_ref, w1_ref, out_ref):
     core = place_ref[2]
     width = w0_ref.shape[1]
@@ -512,35 +534,63 @@
 
 
 def finish_kernel(
-    relative, place_ref, a_ref, w0_ref, w1_ref, came_ref, x0_ref, x1_ref, own_ref, pair_ref
+    relative, place_ref, a_ref, w0_ref, w1_ref, came_ref, x0_ref, x1_ref, *out_refs
 ):
     chip = place_ref[0] * 2 + place_ref[1]
     core = place_ref[2]
     width = w0_ref.shape[1]
-    rows = own_ref.shape[0]
+    rows = x0_ref.shape[1]
     for turn, w_ref in enumerate((w0_ref, w1_ref)):
         start = pl.multiple_of((core ^ turn) * width, HEAD)
         mixed = jnp.dot(
             a_ref[...], w_ref[...], preferred_element_type=jnp.float32
         ) + came_ref[:, pl.ds(start, width)].astype(jnp.float32)
         where = pl.multiple_of((chip ^ relative) * 2 * width + start, HEAD)
-        for number, (x_ref, out_ref) in enumerate(((x0_ref, own_ref), (x1_ref, pair_ref))):
-            out_ref[:, pl.ds(start, width)] = (
-                x_ref[core, :, pl.ds(where, width)].astype(jnp.float32)
-                + mixed[number * rows : (number + 1) * rows, :]
+        for number, x_ref in enumerate((x0_ref, x1_ref)):
+            span = slice(number * rows, (number + 1) * rows)
+            value = (
+                x_ref[core, :, pl.ds(where, width)].astype(jnp.float32) + mixed[span, :]
             ).astype(jnp.bfloat16)
+            if len(out_refs) == 1:
+                out_refs[0][span, pl.ds(start, width)] = value
+            else:
+                out_refs[number][:, pl.ds(start, width)] = value
 
 
 def gather_kernel(place_ref, *refs):
     out_ref = refs[-1]
     chip = place_ref[0] * 2 + place_ref[1]
     core = place_ref[2]
+    rows = out_ref.shape[1]
     for turn in range(2):
-        for relative in range(4):
-            piece = refs[turn * 4 + relative]
+        for number, relative in enumerate(EARLY):
+            piece = refs[turn * len(EARLY) + number]
             width = piece.shape[1]
             start = pl.multiple_of((chip ^ relative) * width, HEAD)
-            out_ref[core ^ turn, :, pl.ds(start, width)] = piece[...]
+            out_ref[core ^ turn, :, pl.ds(start, width)] = piece[
+                turn * rows : (turn + 1) * rows, :
+            ]
+
+
+def gather_last_kernel(place_ref, own_ref, other_ref, before_ref, out_ref, semaphores):
+    width = own_ref.shape[1]
+    start = pl.multiple_of(((place_ref[0] * 2 + place_ref[1]) ^ LATE) * width, HEAD)
+    copies = [
+        pltpu.make_async_copy(
+            piece,
+            out_ref.at[place_ref[2] ^ turn, :, pl.ds(start, width)],
+            semaphores.at[turn],
+        )
+        for turn, piece in enumerate((own_ref, other_ref))
+    ]
+    for copy in copies:
+        copy.start()
+    for copy in copies:
+        copy.wait()
+
+
+EARLY = (2, 0, 3)
+LATE = 1
 
 
 def on_chip_grid(held, norm_gain, w_qkv, q_gain, k_gain, w_out, lengths):
@@ -591,71 +641,83 @@
     flops = 2 * own_rows * width * 2 * part
     chip_rows = own_rows // 2
 
-    def project_own(offset, gain, first, second):
+    def normalise(value):
         return local_kernel(
-            functools.partial(project_own_kernel, offset),
-            [shape((chip_rows, 2 * part), bf16), shape((chip_rows, width), bf16)],
-            [place, first, second, gain, w_in, w_c, cosine, sine, q_gain, k_gain],
+            norm_kernel, [shape((rows, width), bf16)], [place, value, norm_gain]
+        )[0]
+
+    def project_own(offset, ready, second, w_other, keep):
+        return local_kernel(
+            functools.partial(project_own_kernel, offset, keep),
+            [shape((chip_rows, 2 * part), bf16), shape((chip_rows, width), bf16)]
+            + [shape(w_c.shape, bf16)] * keep,
+            [place, ready, second, norm_gain, w_in, w_other, cosine, sine, q_gain, k_gain],
             [pltpu.VMEM((HEAD, width), bf16)],
             flops // 2,
         )
 
-    near0, normed0 = project_own(0, norm_gain, kept, x_c)
+    near0, normed0, w_c = project_own(0, normalise(kept), x_c, w_c, True)
     x_y, near0 = lax.optimization_barrier((x_y, near0))
     x_yc = swap(x_y, 1)
-    near1, normed1 = project_own(chip_rows, norm_gain, x_y, x_yc)
+    ready = normalise(x_y)
+    near1, normed1 = project_own(chip_rows, ready, x_yc, w_c, False)
     o_y = swap(o_there, 4)
-    w_across_c = swap(after(w_across, x_yc), 1)
-    full, swapping_a, swapping_b, kv_a, kv_b = local_kernel(
-        project_far_kernel,
-        [shape((own_rows, 4 * part), bf16)] + [shape((chip_rows, pair), bf16)] * 4,
-        [place, normed0, normed1, w_across, w_across_c, cosine, sine, q_gain, k_gain, near0, near1],
-        [pltpu.VMEM((HEAD, width), bf16)],
-        flops,
-    )
+    o_x = swap(o_here, 2)
+    w_across_c = swap(after(w_across, ready), 1)
+
+    def project_far(order, gate):
+        return local_kernel(
+            functools.partial(project_far_kernel, order),
+            [shape((chip_rows, 4 * part), bf16)] + [shape((chip_rows, pair), bf16)] * 2,
+            [
+                place,
+                normed0,
+                normed1,
+                w_across,
+                w_across_c,
+                cosine,
+                sine,
+                after(q_gain, gate),
+                k_gain,
+                near0,
+                near1,
+            ],
+            [pltpu.VMEM((HEAD, width), bf16)],
+            flops // 2,
+        )
+
+    full0, swapping_a, kv_b = project_far(0, near1)
+    full1, swapping_b, kv_a = project_far(1, swapping_a)
     swap_a = swap(swapping_a, 4)
     swap_b = swap(swapping_b, 4)
     far1_a = swap(kv_a, 2, range(4, 8))
     far1_b = swap(kv_b, 2, range(4, 8))
     far0_a = swap(swap_a, 2, range(4))
     far0_b = swap(swap_b, 2, range(4))
-    o_x = swap(after(o_here, w_across), 2)
     o_y_c = swap(after(o_y, kv_a), 1)
 
-    def attend_near(part, gate):
-        return local_kernel(
-            functools.partial(attend_near_kernel, part),
-            [shape((chip_rows, 2 * half), f32), shape((chip_rows, half), f32)],
-            [place, full, swap_a, swap_b, kv_a, kv_b, after(bias, gate)],
-            [pltpu.VMEM((own_rows, pair), bf16)],
-            flops=2 * own_rows * own_rows * half,
-        )
-
-    def attend_far(part, before, far0, far1, *others):
-        return local_kernel(
-            functools.partial(attend_far_kernel, part),
-            [shape((chip_rows, half), bf16)],
-            [place, full, swap_a, swap_b, far0, far1, after(bias, *others), *before],
-            flops=own_rows * own_rows * half,
-        )[0]
-
-    sums_there = attend_near(1, bias)
+    queries = (full0, full1, swap_a, swap_b)
+    partial_shapes = [shape((chip_rows, 2 * half), f32), shape((chip_rows, half), f32)]
+    attend_flops = 2 * own_rows * own_rows * half
+    chunk = 2 * w_o.shape[1]
+    chunk_flops = own_rows * half * chunk
+    chunk_shape = shape((chip_rows, chunk), bf16)
+    rows_shape = shape((chip_rows, half), bf16)
+    sums_there = local_kernel(
+        functools.partial(attend_near_kernel, 1),
+        partial_shapes,
+        [place, *queries, kv_a, kv_b, bias],
+        [pltpu.VMEM((own_rows, pair), bf16)],
+        attend_flops,
+    )
     o_xy = swap(after(o_y, far0_a, far1_a), 2)
-    attended_there = attend_far(1, sums_there, far0_a, far1_a)
-    o_x_c = swap(after(o_x, attended_there), 1)
-
-    chunk = 2 * w_o.shape[1]
-    came = {}
-
-    def share(relative, rows_there, *pieces):
-        (value,) = local_kernel(
-            share_kernel,
-            [shape((own_rows // 2, chunk), bf16)],
-            [place, rows_there, *pieces],
-            flops=own_rows * half * chunk,
-        )
-        came[relative ^ 2] = swap(value, 4)
-        return value
+    attended_there, share0 = local_kernel(
+        functools.partial(attend_share_kernel, 1),
+        [rows_shape, chunk_shape],
+        [place, *queries, far0_a, far1_a, bias, *sums_there, o_here, o_here_c],
+        flops=attend_flops // 2 + chunk_flops,
+    )
+    o_x_c = swap(after(o_x, kv_a), 1)
 
     ring = [
         (s * devices + i, (s + 1) % sections * devices + i)
@@ -666,32 +728,64 @@
     arrived = {}
 
     def finish(relative, *pieces):
-        own, other = local_kernel(
+        late = relative == LATE
+        values = local_kernel(
             functools.partial(finish_kernel, relative),
-            [shape((rows, chunk), bf16)] * 2,
+            [shape((rows, chunk), bf16)] * 2 if late else [chunk_shape],
             [place, attended_here, *pieces, came[relative], kept, x_c],
-            flops=own_rows * half * chunk,
+            flops=chunk_flops,
         )
-        arrived[0, relative] = lax.ppermute(own, ("section", "dp"), ring)
-        arrived[1, relative] = lax.ppermute(other, ("section", "dp"), cross)
-        return own
-
-    last = share(0, attended_there, o_here, o_here_c)
-    last = share(2, after(attended_there, last), o_y, o_y_c)
-    sums_here = attend_near(0, last)
-    last = share(1, after(attended_there, sums_here[1]), o_x, o_x_c)
-    attended_here = attend_far(0, sums_here, far0_b, far1_b, last)
+        arrived[0, relative] = lax.ppermute(values[0], ("section", "dp"), ring)
+        if late:
+            arrived[1, relative] = lax.ppermute(values[1], ("section", "dp"), cross)
+        return values[0]
+
+    came = {2: swap(share0, 4)}
+    (attended_here,) = local_kernel(
+        functools.partial(attend_kernel, 0),
+        [rows_shape],
+        [place, *queries, kv_a, kv_b, far0_b, far1_b, after(bias, share0)],
+        [pltpu.VMEM((own_rows, pair), bf16)]
+        + [pltpu.VMEM(each.shape, each.dtype) for each in partial_shapes],
+        2 * attend_flops,
+    )
+    share2, share1 = local_kernel(
+        share_two_kernel,
+        [chunk_shape, chunk_shape],
+        [place, after(attended_there, share0), o_y, o_y_c, o_x, o_x_c],
+        flops=2 * chunk_flops,
+    )
+    came[0] = swap(share2, 4)
+    came[3] = swap(share1, 4)
+    attended_here = after(attended_here, share1)
     last = finish(2, o_y, o_y_c)
     o_xy_c = swap(after(o_xy, last), 1)
     last = finish(0, o_here, o_here_c)
-    share(3, after(attended_there, last), o_xy, o_xy_c)
+    (share3,) = local_kernel(
+        share_kernel,
+        [chunk_shape],
+        [place, after(attended_there, last), o_xy, o_xy_c],
+        flops=chunk_flops,
+    )
+    came[1] = swap(share3, 4)
     finish(3, o_xy, o_xy_c)
-    finish(1, o_x, o_x_c)
+    last = finish(1, o_x, o_x_c)
+    for relative in EARLY:
+        arrived[1, relative] = swap(after(arrived[0, relative], last), 1)
     (result,) = local_kernel(
         gather_kernel,
         [shape((micro, rows, width), bf16)],
-        [place, *[arrived[turn, relative] for turn in range(2) for relative in range(4)]],
-    )
+        [place, *[arrived[turn, relative] for turn in range(2) for relative in EARLY]],
+    )
+    result = pl.pallas_call(
+        gather_last_kernel,
+        out_shape=shape((micro, rows, width), bf16),
+        in_specs=[SMEM, VMEM, VMEM, pl.BlockSpec(memory_space=pl.ANY)],
+        out_specs=pl.BlockSpec(memory_space=pl.ANY),
+        scratch_shapes=[pltpu.SemaphoreType.DMA((2,))],
+        input_output_aliases={3: 0},
+        compiler_params=pltpu.CompilerParams(vmem_limit_bytes=4 * MIB),
+    )(place, arrived[0, LATE], arrived[1, LATE], result)
     return result[None]
 
 

time: 119 us -> 127 us (1.067)
  starting transfers between devices: 29.3 us -> 35.8 us
  local copies, waits for them, and re-layouts: 5.88 us -> 3.27 us
  Pallas kernels: 26.4 us -> 28.6 us
  waiting for transfers between devices: 56.7 us -> 58.6 us
    ppermute x8 -> x5, waiting for transfers between devices: 11.9 us -> 21.5 us  [the longest x4 19.7 us: finish(): arrived[0, relative] = lax.ppermute(values[0], ('section', 'dp'), ring)]
    ppermute x23 -> x26, starting transfers between devices: 20.4 us -> 29.9 us  [swap(): return lax.ppermute(value, 'dp', [(i, i ^ bits) for i in among])]
    ppermute x23 -> x26, waiting for transfers between devices: 44.8 us -> 37.1 us  [swap(): return lax.ppermute(value, 'dp', [(i, i ^ bits) for i in among])]
    ppermute x8 -> x5, starting transfers between devices: 8.9 us -> 5.9 us  [the longest x4 4.78 us: finish(): arrived[0, relative] = lax.ppermute(values[0], ('section', 'dp'), ring)]
    unnamed x18, local copies, waits for them, and re-layouts: 5.88 us -> 3.27 us
  transfers between devices with their start and end apart: 31 -> 31, of which waited for: 14 -> 15; matrix products, arithmetic and copies ran while one was open for 0% -> 0% of each run, Pallas kernels for 21% -> 22%
where the time goes in v3:
time: 127 us
  waiting for transfers between devices  58.6 us (46%)
  starting transfers between devices  35.8 us (28%)
  Pallas kernels  28.6 us (23%)
  local copies, waits for them, and re-layouts  3.27 us (3%)
    ppermute x26, waiting for transfers between devices, swap(): return lax.ppermute(value, 'dp', [(i, i ^ bits) for i in among])  37.1 us
    ppermute x26, starting transfers between devices, swap(): return lax.ppermute(value, 'dp', [(i, i ^ bits) for i in among])  29.9 us
    pallas_call x16, Pallas kernels, local_kernel(): pl.pallas_call(body, out_shape=tuple(outs), in_specs=[SMEM] * scalars + [...  24.5 us
    ppermute x4, waiting for transfers between devices, finish(): arrived[0, relative] = lax.ppermute(values[0], ('section', 'dp'), ring)  19.7 us
    ppermute x4, starting transfers between devices, finish(): arrived[0, relative] = lax.ppermute(values[0], ('section', 'dp'), ring)  4.78 us
    unnamed x18, local copies, waits for them, and re-layouts  3.27 us
    pallas_call x1, Pallas kernels, on_chip_grid(): pl.pallas_call(prepare_kernel, out_shape=(shape((11,), jnp.int32), shape(...  2.78 us
  transfers between devices with their start and end apart: 31, of which 15 were waited for; matrix products, arithmetic and copies ran while one was open for 0% of the time, Pallas kernels for 22%

profile of v3, /device:TPU:0, one launch (start us, length us, event | category | flops | bytes accessed | tf_op | source)
XLA Modules:
  0.0 126.8 jit_solution(1934078291360930834)
XLA Ops:
  0.5 2.5 %collective-permute-start.4 = (bf16[320,2048]{1,0:T(8,128)(2,1)}, bf16[320,2048]{1,0:T(8,128)(2,1)S(1)}, u32[]{:S(2)}, u32[]{:S(2)}) collective-permute-start(bf16[320,2048]{1,0:T(8,128)(2,1)} %bitcast.16), channel_id=1, source_target_pairs={{0,2},{1,3},{2,0},{3,1},{4,6},{5,7},{6,4},{7,5},{8,10},{9,11},{10,... | collective-permute-start | bytes 3932168 | tf_op jit(solution)/shard_map/ppermute | solution.py:605
  7.3 2.8 %shard_map.82 = (s32[11]{0:T(128)S(1)}, f32[512,1024]{1,0:T(8,128)S(1)}, f32[512,128]{1,0:T(8,128)S(1)}, f32[512,128]{1,0:T(8,128)S(1)}, bf16[1024,256]{1,0:T(8,128)(2,1)S(1)}, /*index=5*/bf16[1024,256]{1,0:T(8,128)(2,1)S(1)}) custom-call(s32[1]{0:T(128)} %bitcast.here_ref, s32[2,8]{1,0:T(2,128)S(1)} %bitcast.20, f32[1,128]{1,0:T(1,128)S(1)} %copy-done.8, ...), custom_call_target="tpu_custom_call" | custom-call | tf_op jit(solution)/shard_map/pallas_call | solution.py:624
  11.6 2.9 %shard_map.84 = (bf16[256,640]{1,0:T(8,128)(2,1)S(1)}, bf16[256,2048]{1,0:T(8,128)(2,1)S(1)}, bf16[320,2048]{1,0:T(8,128)(2,1)S(1)}) custom-call(s32[11]{0:T(128)S(1)} %get-tuple-element.46.place_ref, bf16[128,2048]{1,0:T(8,128)(2,1)S(1)} %shard_map.83.ready_ref, bf16[2,128,2048]{2,1,0:T(8,128)(2,1)S(1)} %collective-permute-done.x_ref.x1_ref, ...), custom_call_target="tpu_custom_call" | custom-call | flops 671088640 | bytes 7414828 | tf_op jit(solution)/shard_map/pallas_call | solution.py:150
  14.5 14.4 %collective-permute-done.2.x_ref = bf16[2,128,2048]{2,1,0:T(8,128)(2,1)} collective-permute-done((bf16[2,128,2048]{2,1,0:T(8,128)(2,1)}, bf16[2,128,2048]{2,1,0:T(8,128)(2,1)}, u32[]{:S(2)}, u32[]{:S(2)}) %collective-permute-start.2) | collective-permute-done | bytes 1048608 | tf_op jit(solution)/shard_map/ppermute | solution.py:605
  30.4 2.2 %collective-permute-done.4.w_own = bf16[320,2048]{1,0:T(8,128)(2,1)S(1)} collective-permute-done((bf16[320,2048]{1,0:T(8,128)(2,1)}, bf16[320,2048]{1,0:T(8,128)(2,1)S(1)}, u32[]{:S(2)}, u32[]{:S(2)}) %collective-permute-start.4) | collective-permute-done | bytes 1310752 | tf_op jit(solution)/shard_map/ppermute | solution.py:605
  33.1 1.8 %collective-permute-start.13 = (bf16[1024,256]{1,0:T(8,128)(2,1)S(1)}, bf16[1024,256]{1,0:T(8,128)(2,1)S(1)}, u32[]{:S(2)}, u32[]{:S(2)}) collective-permute-start(bf16[1024,256]{1,0:T(8,128)(2,1)S(1)} %get-tuple-element.72), channel_id=1, source_target_pairs={{0,4},{1,5},{2,6},{3,7},{4,0},{5,1},{6,2},{7,3},{8,12},{9,13},{10,... | collective-permute-start | bytes 1572872 | tf_op jit(solution)/shard_map/ppermute | solution.py:605
  37.2 2.0 %shard_map.86 = (bf16[256,640]{1,0:T(8,128)(2,1)S(1)}, bf16[256,2048]{1,0:T(8,128)(2,1)S(1)}) custom-call(s32[11]{0:T(128)S(1)} %get-tuple-element.46.place_ref, bf16[128,2048]{1,0:T(8,128)(2,1)S(1)} %shard_map.85.ready_ref, bf16[2,128,2048]{2,1,0:T(8,128)(2,1)S(1)} %collective-permute-done.3.x_ref, f32[1,2048]{1,0:T(1,128)S(1)} %copy-done.4, ...), custom_call_target="tpu_custom_call" | custom-call | flops 671088640 | bytes 6104108 | tf_op jit(solution)/shard_map/pallas_call | solution.py:150
  39.2 2.0 %shard_map.87 = (bf16[256,1280]{1,0:T(8,128)(2,1)S(1)}, bf16[256,256]{1,0:T(8,128)(2,1)S(1)}, bf16[256,256]{1,0:T(8,128)(2,1)S(1)}) custom-call(s32[11]{0:T(128)S(1)} %get-tuple-element.46.place_ref, bf16[256,2048]{1,0:T(8,128)(2,1)S(1)} %get-tuple-element.49.normed0_ref, bf16[256,2048]{1,0:T(8,128)(2,1)S(1)} %get-tuple-element.53.normed1_ref, ...), custom_call_target="tpu_custom_call" | custom-call | flops 671088640 | bytes 6816812 | tf_op jit(solution)/shard_map/pallas_call | solution.py:150
  41.2 1.9 %collective-permute-start.6 = (bf16[256,256]{1,0:T(8,128)(2,1)S(1)}, bf16[256,256]{1,0:T(8,128)(2,1)S(1)}, u32[]{:S(2)}, u32[]{:S(2)}) collective-permute-start(bf16[256,256]{1,0:T(8,128)(2,1)S(1)} %get-tuple-element.59), channel_id=1, source_target_pairs={{0,4},{1,5},{2,6},{3,7},{4,0},{5,1},{6,2},{7,3},{8,12},{9,13},{10,... | collective-permute-start | bytes 393224 | tf_op jit(solution)/shard_map/ppermute | solution.py:605
  43.1 2.0 %shard_map.88 = (bf16[256,1280]{1,0:T(8,128)(2,1)S(1)}, bf16[256,256]{1,0:T(8,128)(2,1)S(1)}, bf16[256,256]{1,0:T(8,128)(2,1)S(1)}) custom-call(s32[11]{0:T(128)S(1)} %get-tuple-element.46.place_ref, bf16[256,2048]{1,0:T(8,128)(2,1)S(1)} %get-tuple-element.49.normed0_ref, bf16[256,2048]{1,0:T(8,128)(2,1)S(1)} %get-tuple-element.53.normed1_ref, ...), custom_call_target="tpu_custom_call" | custom-call | flops 671088640 | bytes 6816812 | tf_op jit(solution)/shard_map/pallas_call | solution.py:150
  45.8 4.1 %collective-permute-done.6.swap_a_ref.refs_2_ = bf16[256,256]{1,0:T(8,128)(2,1)S(1)} collective-permute-done((bf16[256,256]{1,0:T(8,128)(2,1)S(1)}, bf16[256,256]{1,0:T(8,128)(2,1)S(1)}, u32[]{:S(2)}, u32[]{:S(2)}) %collective-permute-start.6) | collective-permute-done | bytes 131104 | tf_op jit(solution)/shard_map/ppermute | solution.py:605
  49.8 3.6 %collective-permute-start.10 = (bf16[256,256]{1,0:T(8,128)(2,1)S(1)}, bf16[256,256]{1,0:T(8,128)(2,1)S(1)}, u32[]{:S(2)}, u32[]{:S(2)}) collective-permute-start(bf16[256,256]{1,0:T(8,128)(2,1)S(1)} %collective-permute-done.6.swap_a_ref.refs_2_), channel_id=1, source_target_pairs={{0,2},{1,3},{2,0},{3,1},{8,10},{9,11},{10,8},{11,9},{16,18},{17,19... | collective-permute-start | bytes 393224 | tf_op jit(solution)/shard_map/ppermute | solution.py:605
  54.0 2.6 %collective-permute-done.10.refs_4_ = bf16[256,256]{1,0:T(8,128)(2,1)S(1)} collective-permute-done((bf16[256,256]{1,0:T(8,128)(2,1)S(1)}, bf16[256,256]{1,0:T(8,128)(2,1)S(1)}, u32[]{:S(2)}, u32[]{:S(2)}) %collective-permute-start.10) | collective-permute-done | bytes 131104 | tf_op jit(solution)/shard_map/ppermute | solution.py:605
  56.7 1.7 %collective-permute-start.18 = (bf16[1024,256]{1,0:T(8,128)(2,1)S(1)}, bf16[1024,256]{1,0:T(8,128)(2,1)S(1)}, u32[]{:S(2)}, u32[]{:S(2)}) collective-permute-start(bf16[1024,256]{1,0:T(8,128)(2,1)S(1)} %collective-permute-done.13.w0_ref), channel_id=1, source_target_pairs={{0,2},{1,3},{2,0},{3,1},{4,6},{5,7},{6,4},{7,5},{8,10},{9,11},{10,... | collective-permute-start | bytes 1572872 | tf_op jit(solution)/shard_map/ppermute | solution.py:605
  61.7 3.0 %collective-permute-start.8 = (bf16[256,256]{1,0:T(8,128)(2,1)S(1)}, bf16[256,256]{1,0:T(8,128)(2,1)S(1)}, u32[]{:S(2)}, u32[]{:S(2)}) collective-permute-start(bf16[256,256]{1,0:T(8,128)(2,1)S(1)} %collective-permute-done.7.swap_b_ref.refs_3_), channel_id=1, source_target_pairs={{0,2},{1,3},{2,0},{3,1},{8,10},{9,11},{10,8},{11,9},{16,18},{17,19... | collective-permute-start | bytes 393224 | tf_op jit(solution)/shard_map/ppermute | solution.py:605
  64.7 2.4 %shard_map.90 = (bf16[256,1024]{1,0:T(8,128)(2,1)S(1)}, bf16[256,512]{1,0:T(8,128)(2,1)S(1)}) custom-call(s32[11]{0:T(128)S(1)} %get-tuple-element.46.place_ref, bf16[256,1280]{1,0:T(8,128)(2,1)S(1)} %get-tuple-element.58.full0_ref.refs_0_, bf16[256,1280]{1,0:T(8,128)(2,1)S(1)} %get-tuple-element.61.full1_ref.refs_1_, ...), custom_call_target="tpu_custom_call" | custom-call | flops 536870912 | bytes 8912940 | tf_op jit(solution)/shard_map/pallas_call | solution.py:150
  67.2 5.3 %collective-permute-start.19 = (bf16[256,512]{1,0:T(8,128)(2,1)S(1)}, bf16[256,512]{1,0:T(8,128)(2,1)S(1)}, u32[]{:S(2)}, u32[]{:S(2)}) collective-permute-start(bf16[256,512]{1,0:T(8,128)(2,1)S(1)} %get-tuple-element.69), channel_id=1, source_target_pairs={{0,4},{1,5},{2,6},{3,7},{4,0},{5,1},{6,2},{7,3},{8,12},{9,13},{10,... | collective-permute-start | bytes 786440 | tf_op jit(solution)/shard_map/ppermute | solution.py:605
  72.5 1.7 %shard_map.91.a_ref = bf16[256,1024]{1,0:T(8,128)(2,1)S(1)} custom-call(s32[11]{0:T(128)S(1)} %get-tuple-element.46.place_ref, bf16[256,1280]{1,0:T(8,128)(2,1)S(1)} %get-tuple-element.58.full0_ref.refs_0_, bf16[256,1280]{1,0:T(8,128)(2,1)S(1)} %get-tuple-element.61.full1_ref.refs_1_, bf16[256,256]{1,0:T(8,128)(2,1)S(1)} %collective-permute-done.6.swap_a_ref.refs_2_, ...), custom_call_target="tpu_custom_call" | custom-call | flops 1073741824 | bytes 4718636 | tf_op jit(solution)/shard_map/pallas_call | solution.py:150
  75.5 2.4 %collective-permute-done.19.came_ref = bf16[256,512]{1,0:T(8,128)(2,1)S(1)} collective-permute-done((bf16[256,512]{1,0:T(8,128)(2,1)S(1)}, bf16[256,512]{1,0:T(8,128)(2,1)S(1)}, u32[]{:S(2)}, u32[]{:S(2)}) %collective-permute-start.19) | collective-permute-done | bytes 262176 | tf_op jit(solution)/shard_map/ppermute | solution.py:605
  79.0 1.8 %collective-permute-start.17 = (bf16[256,512]{1,0:T(8,128)(2,1)S(1)}, bf16[256,512]{1,0:T(8,128)(2,1)S(1)}, u32[]{:S(2)}, u32[]{:S(2)}) collective-permute-start(bf16[256,512]{1,0:T(8,128)(2,1)S(1)} %get-tuple-element.77), channel_id=1, source_target_pairs={{0,4},{1,5},{2,6},{3,7},{4,0},{5,1},{6,2},{7,3},{8,12},{9,13},{10,... | collective-permute-start | bytes 786440 | tf_op jit(solution)/shard_map/ppermute | solution.py:605
  81.1 7.2 %collective-permute-done.17.came_ref = bf16[256,512]{1,0:T(8,128)(2,1)S(1)} collective-permute-done((bf16[256,512]{1,0:T(8,128)(2,1)S(1)}, bf16[256,512]{1,0:T(8,128)(2,1)S(1)}, u32[]{:S(2)}, u32[]{:S(2)}) %collective-permute-start.17) | collective-permute-done | bytes 262176 | tf_op jit(solution)/shard_map/ppermute | solution.py:605
  90.3 1.8 %collective-permute-start.21 = (bf16[256,512]{1,0:T(8,128)(2,1)S(1)}, bf16[256,512]{1,0:T(8,128)(2,1)S(1)}, u32[]{:S(2)}, u32[]{:S(2)}) collective-permute-start(bf16[256,512]{1,0:T(8,128)(2,1)S(1)} %shard_map.95), channel_id=1, source_target_pairs={{0,4},{1,5},{2,6},{3,7},{4,0},{5,1},{6,2},{7,3},{8,12},{9,13},{10,... | collective-permute-start | bytes 786440 | tf_op jit(solution)/shard_map/ppermute | solution.py:605
  92.1 1.8 %collective-permute-done.26.came_ref = bf16[256,512]{1,0:T(8,128)(2,1)S(1)} collective-permute-done((bf16[256,512]{1,0:T(8,128)(2,1)S(1)}, bf16[256,512]{1,0:T(8,128)(2,1)S(1)}, u32[]{:S(2)}, u32[]{:S(2)}) %collective-permute-start.26) | collective-permute-done | bytes 262176 | tf_op jit(solution)/shard_map/ppermute | solution.py:605
  94.9 1.6 %collective-permute-start.27 = (bf16[256,512]{1,0:T(8,128)(2,1)S(1)}, bf16[256,512]{1,0:T(8,128)(2,1)S(1)}, u32[]{:S(2)}, u32[]{:S(2)}) collective-permute-start(bf16[256,512]{1,0:T(8,128)(2,1)S(1)} %shard_map.97), channel_id=1, source_target_pairs={{0,8},{1,9},{2,10},{3,11},{4,12},{5,13},{6,14},{7,15},{8,16},{9,17... | collective-permute-start | bytes 786440 | tf_op jit(solution)/shard_map/ppermute | solution.py:738
  96.5 1.6 %collective-permute-start.25 = (bf16[256,512]{1,0:T(8,128)(2,1)S(1)}, bf16[256,512]{1,0:T(8,128)(2,1)S(1)}, u32[]{:S(2)}, u32[]{:S(2)}) collective-permute-start(bf16[256,512]{1,0:T(8,128)(2,1)S(1)} %shard_map.93), channel_id=1, source_target_pairs={{0,8},{1,9},{2,10},{3,11},{4,12},{5,13},{6,14},{7,15},{8,16},{9,17... | collective-permute-start | bytes 786440 | tf_op jit(solution)/shard_map/ppermute | solution.py:738
  98.1 1.6 %collective-permute-start.24 = (bf16[256,512]{1,0:T(8,128)(2,1)S(1)}, bf16[256,512]{1,0:T(8,128)(2,1)S(1)}, u32[]{:S(2)}, u32[]{:S(2)}) collective-permute-start(bf16[256,512]{1,0:T(8,128)(2,1)S(1)} %shard_map.94), channel_id=1, source_target_pairs={{0,8},{1,9},{2,10},{3,11},{4,12},{5,13},{6,14},{7,15},{8,16},{9,17... | collective-permute-start | bytes 786440 | tf_op jit(solution)/shard_map/ppermute | solution.py:738
  100.7 5.2 %collective-permute-done.27.refs_2_ = bf16[256,512]{1,0:T(8,128)(2,1)S(1)} collective-permute-done((bf16[256,512]{1,0:T(8,128)(2,1)S(1)}, bf16[256,512]{1,0:T(8,128)(2,1)S(1)}, u32[]{:S(2)}, u32[]{:S(2)}) %collective-permute-start.27) | collective-permute-done | bytes 262176 | tf_op jit(solution)/shard_map/ppermute | solution.py:738
  105.9 5.6 %collective-permute-done.25.refs_1_ = bf16[256,512]{1,0:T(8,128)(2,1)S(1)} collective-permute-done((bf16[256,512]{1,0:T(8,128)(2,1)S(1)}, bf16[256,512]{1,0:T(8,128)(2,1)S(1)}, u32[]{:S(2)}, u32[]{:S(2)}) %collective-permute-start.25) | collective-permute-done | bytes 262176 | tf_op jit(solution)/shard_map/ppermute | solution.py:738
  111.5 3.7 %collective-permute-done.24.refs_0_ = bf16[256,512]{1,0:T(8,128)(2,1)S(1)} collective-permute-done((bf16[256,512]{1,0:T(8,128)(2,1)S(1)}, bf16[256,512]{1,0:T(8,128)(2,1)S(1)}, u32[]{:S(2)}, u32[]{:S(2)}) %collective-permute-start.24) | collective-permute-done | bytes 262176 | tf_op jit(solution)/shard_map/ppermute | solution.py:738
  116.8 1.6 %shard_map.98.before_ref = bf16[2,128,2048]{2,1,0:T(8,128)(2,1)} custom-call(s32[11]{0:T(128)S(1)} %get-tuple-element.46.place_ref, bf16[256,512]{1,0:T(8,128)(2,1)S(1)} %collective-permute-done.24.refs_0_, bf16[256,512]{1,0:T(8,128)(2,1)S(1)} %collective-permute-done.25.refs_1_, bf16[256,512]{1,0:T(8,128)(2,1)S(1)} %collective-permute-done.27.refs_2_, ...), custom_call_target="tpu_custom_call" | custom-call | bytes 2621484 | tf_op jit(solution)/shard_map/pallas_call | solution.py:150
  118.4 5.1 %collective-permute-done.22.own_ref = bf16[128,512]{1,0:T(8,128)(2,1)S(1)} collective-permute-done((bf16[128,512]{1,0:T(8,128)(2,1)S(1)}, bf16[128,512]{1,0:T(8,128)(2,1)S(1)}, u32[]{:S(2)}, u32[]{:S(2)}) %collective-permute-start.22) | collective-permute-done | bytes 131104 | tf_op jit(solution)/shard_map/ppermute | solution.py:738
  123.5 1.9 %collective-permute-done.23.other_ref = bf16[128,512]{1,0:T(8,128)(2,1)S(1)} collective-permute-done((bf16[128,512]{1,0:T(8,128)(2,1)S(1)}, bf16[128,512]{1,0:T(8,128)(2,1)S(1)}, u32[]{:S(2)}, u32[]{:S(2)}) %collective-permute-start.23) | collective-permute-done | bytes 131104 | tf_op jit(solution)/shard_map/ppermute | solution.py:740
  (66 shorter events, 24.4 us)
Async XLA Ops:
  0.0 10.1 %copy-start = (bf16[1,2,128,2048]{3,2,1,0:T(8,128)(2,1)S(1)}, bf16[1,2,128,2048]{3,2,1,0:T(8,128)(2,1)}, u32[]{:S(2)}) copy-start(bf16[1,2,128,2048]{3,2,1,0:T(8,128)(2,1)} %param.8) | copy-start | bytes 3145732
  0.0 11.6 %collective-permute-start.1 = (bf16[320,2048]{1,0:T(8,128)(2,1)}, bf16[320,2048]{1,0:T(8,128)(2,1)}, u32[]{:S(2)}, u32[]{:S(2)}) collective-permute-start(bf16[320,2048]{1,0:T(8,128)(2,1)} %bitcast.15), channel_id=1, source_target_pairs={{0,1},{1,0},{2,3},{3,2},{4,5},{5,4},{6,7},{7,6},{8,9},{9,8},{10,11... | collective-permute-start | bytes 3932168 | tf_op jit(solution)/shard_map/ppermute | solution.py:605
  0.5 32.1 %collective-permute-start.4 = (bf16[320,2048]{1,0:T(8,128)(2,1)}, bf16[320,2048]{1,0:T(8,128)(2,1)S(1)}, u32[]{:S(2)}, u32[]{:S(2)}) collective-permute-start(bf16[320,2048]{1,0:T(8,128)(2,1)} %bitcast.16), channel_id=1, source_target_pairs={{0,2},{1,3},{2,0},{3,1},{4,6},{5,7},{6,4},{7,5},{8,10},{9,11},{10,... | collective-permute-start | bytes 3932168 | tf_op jit(solution)/shard_map/ppermute | solution.py:605
  3.0 8.5 %collective-permute-start = (bf16[2,128,2048]{2,1,0:T(8,128)(2,1)}, bf16[2,128,2048]{2,1,0:T(8,128)(2,1)S(1)}, u32[]{:S(2)}, u32[]{:S(2)}) collective-permute-start(bf16[2,128,2048]{2,1,0:T(8,128)(2,1)} %bitcast.8), channel_id=1, source_target_pairs={{0,1},{1,0},{2,3},{3,2},{4,5},{5,4},{6,7},{7,6},{8,9},{9,8},{10,11... | collective-permute-start | bytes 3145736 | tf_op jit(solution)/shard_map/ppermute | solution.py:605
  3.2 25.7 %collective-permute-start.2 = (bf16[2,128,2048]{2,1,0:T(8,128)(2,1)}, bf16[2,128,2048]{2,1,0:T(8,128)(2,1)}, u32[]{:S(2)}, u32[]{:S(2)}) collective-permute-start(bf16[2,128,2048]{2,1,0:T(8,128)(2,1)} %bitcast.9), channel_id=1, source_target_pairs={{0,4},{1,5},{2,6},{3,7},{4,0},{5,1},{6,2},{7,3},{8,12},{9,13},{10,... | collective-permute-start | bytes 3145736 | tf_op jit(solution)/shard_map/ppermute | solution.py:605
  32.6 6.5 %collective-permute-start.5 = (bf16[320,2048]{1,0:T(8,128)(2,1)S(1)}, bf16[320,2048]{1,0:T(8,128)(2,1)S(1)}, u32[]{:S(2)}, u32[]{:S(2)}) collective-permute-start(bf16[320,2048]{1,0:T(8,128)(2,1)S(1)} %collective-permute-done.4.w_own), channel_id=1, source_target_pairs={{0,1},{1,0},{2,3},{3,2},{4,5},{5,4},{6,7},{7,6},{8,9},{9,8},{10,11... | collective-permute-start | bytes 3932168 | tf_op jit(solution)/shard_map/ppermute | solution.py:605
  32.6 4.5 %collective-permute-start.3 = (bf16[2,128,2048]{2,1,0:T(8,128)(2,1)}, bf16[2,128,2048]{2,1,0:T(8,128)(2,1)S(1)}, u32[]{:S(2)}, u32[]{:S(2)}) collective-permute-start(bf16[2,128,2048]{2,1,0:T(8,128)(2,1)} %collective-permute-done.2.x_ref), channel_id=1, source_target_pairs={{0,1},{1,0},{2,3},{3,2},{4,5},{5,4},{6,7},{7,6},{8,9},{9,8},{10,11... | collective-permute-start | bytes 3145736 | tf_op jit(solution)/shard_map/ppermute | solution.py:605
  33.1 20.3 %collective-permute-start.13 = (bf16[1024,256]{1,0:T(8,128)(2,1)S(1)}, bf16[1024,256]{1,0:T(8,128)(2,1)S(1)}, u32[]{:S(2)}, u32[]{:S(2)}) collective-permute-start(bf16[1024,256]{1,0:T(8,128)(2,1)S(1)} %get-tuple-element.72), channel_id=1, source_target_pairs={{0,4},{1,5},{2,6},{3,7},{4,0},{5,1},{6,2},{7,3},{8,12},{9,13},{10,... | collective-permute-start | bytes 1572872 | tf_op jit(solution)/shard_map/ppermute | solution.py:605
  34.9 18.6 %collective-permute-start.15 = (bf16[1024,256]{1,0:T(8,128)(2,1)S(1)}, bf16[1024,256]{1,0:T(8,128)(2,1)S(1)}, u32[]{:S(2)}, u32[]{:S(2)}) collective-permute-start(bf16[1024,256]{1,0:T(8,128)(2,1)S(1)} %get-tuple-element.68.refs_9_.w0_ref), channel_id=1, source_target_pairs={{0,2},{1,3},{2,0},{3,1},{4,6},{5,7},{6,4},{7,5},{8,10},{9,11},{10,... | collective-permute-start | bytes 1572872 | tf_op jit(solution)/shard_map/ppermute | solution.py:605
  36.4 25.3 %collective-permute-start.12 = (bf16[1024,256]{1,0:T(8,128)(2,1)S(1)}, bf16[1024,256]{1,0:T(8,128)(2,1)S(1)}, u32[]{:S(2)}, u32[]{:S(2)}) collective-permute-start(bf16[1024,256]{1,0:T(8,128)(2,1)S(1)} %get-tuple-element.68.refs_9_.w0_ref), channel_id=1, source_target_pairs={{0,1},{1,0},{2,3},{3,2},{4,5},{5,4},{6,7},{7,6},{8,9},{9,8},{10,11... | collective-permute-start | bytes 1572872 | tf_op jit(solution)/shard_map/ppermute | solution.py:605
  41.2 8.6 %collective-permute-start.6 = (bf16[256,256]{1,0:T(8,128)(2,1)S(1)}, bf16[256,256]{1,0:T(8,128)(2,1)S(1)}, u32[]{:S(2)}, u32[]{:S(2)}) collective-permute-start(bf16[256,256]{1,0:T(8,128)(2,1)S(1)} %get-tuple-element.59), channel_id=1, source_target_pairs={{0,4},{1,5},{2,6},{3,7},{4,0},{5,1},{6,2},{7,3},{8,12},{9,13},{10,... | collective-permute-start | bytes 393224 | tf_op jit(solution)/shard_map/ppermute | solution.py:605
  45.1 8.9 %collective-permute-start.11 = (bf16[256,256]{1,0:T(8,128)(2,1)S(1)}, bf16[256,256]{1,0:T(8,128)(2,1)S(1)}, u32[]{:S(2)}, u32[]{:S(2)}) collective-permute-start(bf16[256,256]{1,0:T(8,128)(2,1)S(1)} %get-tuple-element.63.kv_a_ref.refs_4_), channel_id=1, source_target_pairs={{4,6},{5,7},{6,4},{7,5},{12,14},{13,15},{14,12},{15,13},{20,22},{2... | collective-permute-start | bytes 393224 | tf_op jit(solution)/shard_map/ppermute | solution.py:605
  49.8 6.8 %collective-permute-start.10 = (bf16[256,256]{1,0:T(8,128)(2,1)S(1)}, bf16[256,256]{1,0:T(8,128)(2,1)S(1)}, u32[]{:S(2)}, u32[]{:S(2)}) collective-permute-start(bf16[256,256]{1,0:T(8,128)(2,1)S(1)} %collective-permute-done.6.swap_a_ref.refs_2_), channel_id=1, source_target_pairs={{0,2},{1,3},{2,0},{3,1},{8,10},{9,11},{10,8},{11,9},{16,18},{17,19... | collective-permute-start | bytes 393224 | tf_op jit(solution)/shard_map/ppermute | solution.py:605
  53.4 20.8 %collective-permute-start.14 = (bf16[1024,256]{1,0:T(8,128)(2,1)S(1)}, bf16[1024,256]{1,0:T(8,128)(2,1)S(1)}, u32[]{:S(2)}, u32[]{:S(2)}) collective-permute-start(bf16[1024,256]{1,0:T(8,128)(2,1)S(1)} %collective-permute-done.13.w0_ref), channel_id=1, source_target_pairs={{0,1},{1,0},{2,3},{3,2},{4,5},{5,4},{6,7},{7,6},{8,9},{9,8},{10,11... | collective-permute-start | bytes 1572872 | tf_op jit(solution)/shard_map/ppermute | solution.py:605
  53.5 20.7 %collective-permute-start.16 = (bf16[1024,256]{1,0:T(8,128)(2,1)S(1)}, bf16[1024,256]{1,0:T(8,128)(2,1)S(1)}, u32[]{:S(2)}, u32[]{:S(2)}) collective-permute-start(bf16[1024,256]{1,0:T(8,128)(2,1)S(1)} %collective-permute-done.15.w2_ref.w0_ref), channel_id=1, source_target_pairs={{0,1},{1,0},{2,3},{3,2},{4,5},{5,4},{6,7},{7,6},{8,9},{9,8},{10,11... | collective-permute-start | bytes 1572872 | tf_op jit(solution)/shard_map/ppermute | solution.py:605
  54.0 5.5 %collective-permute-start.7 = (bf16[256,256]{1,0:T(8,128)(2,1)S(1)}, bf16[256,256]{1,0:T(8,128)(2,1)S(1)}, u32[]{:S(2)}, u32[]{:S(2)}) collective-permute-start(bf16[256,256]{1,0:T(8,128)(2,1)S(1)} %get-tuple-element.62), channel_id=1, source_target_pairs={{0,4},{1,5},{2,6},{3,7},{4,0},{5,1},{6,2},{7,3},{8,12},{9,13},{10,... | collective-permute-start | bytes 393224 | tf_op jit(solution)/shard_map/ppermute | solution.py:605
  56.7 22.3 %collective-permute-start.18 = (bf16[1024,256]{1,0:T(8,128)(2,1)S(1)}, bf16[1024,256]{1,0:T(8,128)(2,1)S(1)}, u32[]{:S(2)}, u32[]{:S(2)}) collective-permute-start(bf16[1024,256]{1,0:T(8,128)(2,1)S(1)} %collective-permute-done.13.w0_ref), channel_id=1, source_target_pairs={{0,2},{1,3},{2,0},{3,1},{4,6},{5,7},{6,4},{7,5},{8,10},{9,11},{10,... | collective-permute-start | bytes 1572872 | tf_op jit(solution)/shard_map/ppermute | solution.py:605
  59.5 7.6 %collective-permute-start.9 = (bf16[256,256]{1,0:T(8,128)(2,1)S(1)}, bf16[256,256]{1,0:T(8,128)(2,1)S(1)}, u32[]{:S(2)}, u32[]{:S(2)}) collective-permute-start(bf16[256,256]{1,0:T(8,128)(2,1)S(1)} %get-tuple-element.64.kv_b_ref.refs_5_), channel_id=1, source_target_pairs={{4,6},{5,7},{6,4},{7,5},{12,14},{13,15},{14,12},{15,13},{20,22},{2... | collective-permute-start | bytes 393224 | tf_op jit(solution)/shard_map/ppermute | solution.py:605
  61.7 10.8 %collective-permute-start.8 = (bf16[256,256]{1,0:T(8,128)(2,1)S(1)}, bf16[256,256]{1,0:T(8,128)(2,1)S(1)}, u32[]{:S(2)}, u32[]{:S(2)}) collective-permute-start(bf16[256,256]{1,0:T(8,128)(2,1)S(1)} %collective-permute-done.7.swap_b_ref.refs_3_), channel_id=1, source_target_pairs={{0,2},{1,3},{2,0},{3,1},{8,10},{9,11},{10,8},{11,9},{16,18},{17,19... | collective-permute-start | bytes 393224 | tf_op jit(solution)/shard_map/ppermute | solution.py:605
  67.2 10.8 %collective-permute-start.19 = (bf16[256,512]{1,0:T(8,128)(2,1)S(1)}, bf16[256,512]{1,0:T(8,128)(2,1)S(1)}, u32[]{:S(2)}, u32[]{:S(2)}) collective-permute-start(bf16[256,512]{1,0:T(8,128)(2,1)S(1)} %get-tuple-element.69), channel_id=1, source_target_pairs={{0,4},{1,5},{2,6},{3,7},{4,0},{5,1},{6,2},{7,3},{8,12},{9,13},{10,... | collective-permute-start | bytes 786440 | tf_op jit(solution)/shard_map/ppermute | solution.py:605
  78.9 10.3 %collective-permute-start.20 = (bf16[1024,256]{1,0:T(8,128)(2,1)S(1)}, bf16[1024,256]{1,0:T(8,128)(2,1)S(1)}, u32[]{:S(2)}, u32[]{:S(2)}) collective-permute-start(bf16[1024,256]{1,0:T(8,128)(2,1)S(1)} %collective-permute-done.18.w0_ref), channel_id=1, source_target_pairs={{0,1},{1,0},{2,3},{3,2},{4,5},{5,4},{6,7},{7,6},{8,9},{9,8},{10,11... | collective-permute-start | bytes 1572872 | tf_op jit(solution)/shard_map/ppermute | solution.py:605
  79.0 9.2 %collective-permute-start.17 = (bf16[256,512]{1,0:T(8,128)(2,1)S(1)}, bf16[256,512]{1,0:T(8,128)(2,1)S(1)}, u32[]{:S(2)}, u32[]{:S(2)}) collective-permute-start(bf16[256,512]{1,0:T(8,128)(2,1)S(1)} %get-tuple-element.77), channel_id=1, source_target_pairs={{0,4},{1,5},{2,6},{3,7},{4,0},{5,1},{6,2},{7,3},{8,12},{9,13},{10,... | collective-permute-start | bytes 786440 | tf_op jit(solution)/shard_map/ppermute | solution.py:605
  80.8 13.1 %collective-permute-start.26 = (bf16[256,512]{1,0:T(8,128)(2,1)S(1)}, bf16[256,512]{1,0:T(8,128)(2,1)S(1)}, u32[]{:S(2)}, u32[]{:S(2)}) collective-permute-start(bf16[256,512]{1,0:T(8,128)(2,1)S(1)} %get-tuple-element.75), channel_id=1, source_target_pairs={{0,4},{1,5},{2,6},{3,7},{4,0},{5,1},{6,2},{7,3},{8,12},{9,13},{10,... | collective-permute-start | bytes 786440 | tf_op jit(solution)/shard_map/ppermute | solution.py:605
  90.3 9.4 %collective-permute-start.21 = (bf16[256,512]{1,0:T(8,128)(2,1)S(1)}, bf16[256,512]{1,0:T(8,128)(2,1)S(1)}, u32[]{:S(2)}, u32[]{:S(2)}) collective-permute-start(bf16[256,512]{1,0:T(8,128)(2,1)S(1)} %shard_map.95), channel_id=1, source_target_pairs={{0,4},{1,5},{2,6},{3,7},{4,0},{5,1},{6,2},{7,3},{8,12},{9,13},{10,... | collective-permute-start | bytes 786440 | tf_op jit(solution)/shard_map/ppermute | solution.py:605
  94.9 11.0 %collective-permute-start.27 = (bf16[256,512]{1,0:T(8,128)(2,1)S(1)}, bf16[256,512]{1,0:T(8,128)(2,1)S(1)}, u32[]{:S(2)}, u32[]{:S(2)}) collective-permute-start(bf16[256,512]{1,0:T(8,128)(2,1)S(1)} %shard_map.97), channel_id=1, source_target_pairs={{0,8},{1,9},{2,10},{3,11},{4,12},{5,13},{6,14},{7,15},{8,16},{9,17... | collective-permute-start | bytes 786440 | tf_op jit(solution)/shard_map/ppermute | solution.py:738
  96.5 15.0 %collective-permute-start.25 = (bf16[256,512]{1,0:T(8,128)(2,1)S(1)}, bf16[256,512]{1,0:T(8,128)(2,1)S(1)}, u32[]{:S(2)}, u32[]{:S(2)}) collective-permute-start(bf16[256,512]{1,0:T(8,128)(2,1)S(1)} %shard_map.93), channel_id=1, source_target_pairs={{0,8},{1,9},{2,10},{3,11},{4,12},{5,13},{6,14},{7,15},{8,16},{9,17... | collective-permute-start | bytes 786440 | tf_op jit(solution)/shard_map/ppermute | solution.py:738
  98.1 17.2 %collective-permute-start.24 = (bf16[256,512]{1,0:T(8,128)(2,1)S(1)}, bf16[256,512]{1,0:T(8,128)(2,1)S(1)}, u32[]{:S(2)}, u32[]{:S(2)}) collective-permute-start(bf16[256,512]{1,0:T(8,128)(2,1)S(1)} %shard_map.94), channel_id=1, source_target_pairs={{0,8},{1,9},{2,10},{3,11},{4,12},{5,13},{6,14},{7,15},{8,16},{9,17... | collective-permute-start | bytes 786440 | tf_op jit(solution)/shard_map/ppermute | solution.py:738
  105.9 10.5 %collective-permute-start.30 = (bf16[256,512]{1,0:T(8,128)(2,1)S(1)}, bf16[256,512]{1,0:T(8,128)(2,1)S(1)}, u32[]{:S(2)}, u32[]{:S(2)}) collective-permute-start(bf16[256,512]{1,0:T(8,128)(2,1)S(1)} %collective-permute-done.27.refs_2_), channel_id=1, source_target_pairs={{0,1},{1,0},{2,3},{3,2},{4,5},{5,4},{6,7},{7,6},{8,9},{9,8},{10,11... | collective-permute-start | bytes 786440 | tf_op jit(solution)/shard_map/ppermute | solution.py:605
  111.5 4.9 %collective-permute-start.29 = (bf16[256,512]{1,0:T(8,128)(2,1)S(1)}, bf16[256,512]{1,0:T(8,128)(2,1)S(1)}, u32[]{:S(2)}, u32[]{:S(2)}) collective-permute-start(bf16[256,512]{1,0:T(8,128)(2,1)S(1)} %collective-permute-done.25.refs_1_), channel_id=1, source_target_pairs={{0,1},{1,0},{2,3},{3,2},{4,5},{5,4},{6,7},{7,6},{8,9},{9,8},{10,11... | collective-permute-start | bytes 786440 | tf_op jit(solution)/shard_map/ppermute | solution.py:605
  115.3 1.5 %collective-permute-start.28 = (bf16[256,512]{1,0:T(8,128)(2,1)S(1)}, bf16[256,512]{1,0:T(8,128)(2,1)S(1)}, u32[]{:S(2)}, u32[]{:S(2)}) collective-permute-start(bf16[256,512]{1,0:T(8,128)(2,1)S(1)} %collective-permute-done.24.refs_0_), channel_id=1, source_target_pairs={{0,1},{1,0},{2,3},{3,2},{4,5},{5,4},{6,7},{7,6},{8,9},{9,8},{10,11... | collective-permute-start | bytes 786440 | tf_op jit(solution)/shard_map/ppermute | solution.py:605
  115.3 8.2 %collective-permute-start.22 = (bf16[128,512]{1,0:T(8,128)(2,1)S(1)}, bf16[128,512]{1,0:T(8,128)(2,1)S(1)}, u32[]{:S(2)}, u32[]{:S(2)}) collective-permute-start(bf16[128,512]{1,0:T(8,128)(2,1)S(1)} %get-tuple-element.81), channel_id=1, source_target_pairs={{0,8},{1,9},{2,10},{3,11},{4,12},{5,13},{6,14},{7,15},{8,16},{9,17... | collective-permute-start | bytes 393224 | tf_op jit(solution)/shard_map/ppermute | solution.py:738
  115.3 10.0 %collective-permute-start.23 = (bf16[128,512]{1,0:T(8,128)(2,1)S(1)}, bf16[128,512]{1,0:T(8,128)(2,1)S(1)}, u32[]{:S(2)}, u32[]{:S(2)}) collective-permute-start(bf16[128,512]{1,0:T(8,128)(2,1)S(1)} %get-tuple-element.82), channel_id=1, source_target_pairs={{0,9},{1,8},{2,11},{3,10},{4,13},{5,12},{6,15},{7,14},{8,17},{9,16... | collective-permute-start | bytes 393224 | tf_op jit(solution)/shard_map/ppermute | solution.py:740
  (8 other events, 10.0 us)

commit v4 on v3

--- a/solution.py
+++ b/solution.py
@@ -332,33 +332,52 @@
     k_gain_ref,
     near0_ref,
     near1_ref,
-    full,
-    swap_ref,
-    kv_ref,
-    middle,
+    *refs,
 ):
+    *outs, middle = refs
+    full, swap_ref, kv_ref = outs[:3]
     line, column, core = place_ref[0], place_ref[1], place_ref[2]
-    join_middle(core, middle, w_own, w_partner)
     chip_width = near0_ref.shape[1]
     blocks = chip_width // HEAD
     which = 1 - column
     step = normed0_ref.shape[0]
-    part = column if order == 0 else 1 - column
-    normed = jnp.where(part == 0, normed0_ref[...], normed1_ref[...])
-    span = pl.ds(pl.multiple_of(part * step, step), step)
-    cosine, sine = cos_ref[span, :], sin_ref[span, :]
-    full[:, pl.ds(pl.multiple_of(column * chip_width, HEAD), chip_width)] = jnp.where(
-        part == 0, near0_ref[...], near1_ref[...]
-    )
-
-    def write(block, projected):
-        head = (line * 2 + which) * blocks + block
-        start = pl.multiple_of((which * blocks + block) * HEAD, HEAD)
-        full[:, pl.ds(start, HEAD)] = project_block(
-            projected, head, cosine, sine, (q_gain_ref, k_gain_ref)
+
+    def copy_near(part, out):
+        out[:, pl.ds(pl.multiple_of(column * chip_width, HEAD), chip_width)] = jnp.where(
+            part == 0, near0_ref[...], near1_ref[...]
         )
 
-    project_with(normed, w_own, w_partner, middle, core, write)
+    def project(part, out):
+        normed = jnp.where(part == 0, normed0_ref[...], normed1_ref[...])
+        span = pl.ds(pl.multiple_of(part * step, step), step)
+        cosine, sine = cos_ref[span, :], sin_ref[span, :]
+
+        def write(block, projected):
+            head = (line * 2 + which) * blocks + block
+            start = pl.multiple_of((which * blocks + block) * HEAD, HEAD)
+            out[:, pl.ds(start, HEAD)] = project_block(
+                projected, head, cosine, sine, (q_gain_ref, k_gain_ref)
+            )
+
+        project_with(normed, w_own, w_partner, middle, core, write)
+
+    if order == 0:
+        copy_near(column, full)
+
+        @pl.when(column == 0)
+        def _():
+            join_middle(core, middle, w_own, w_partner)
+            project(0, full)
+    else:
+        join_middle(core, middle, w_own, w_partner)
+        copy_near(1 - column, full)
+        project(1 - column, full)
+
+        @pl.when(column == 1)
+        def _():
+            copy_near(1, outs[3])
+            project(1, outs[3])
+
     inner = HEADS // 2 * HEAD
     pair = swap_ref.shape[1]
     half = pair // 2
@@ -388,7 +407,8 @@
     moved = swap_refs[0].shape[1] // HEAD
     start = pl.multiple_of(jnp.maximum(head - moved * line, 0) * HEAD, HEAD)
     lanes = pl.ds(start, HEAD)
-    q = jnp.where(column == part, full_refs[0][:, lanes], full_refs[1][:, lanes])
+    first = jnp.where(column == 0, full_refs[0][:, lanes], full_refs[2][:, lanes])
+    q = jnp.where(column == part, first, full_refs[1][:, lanes])
     if head < moved:
         there = slice(head * HEAD, (head + 1) * HEAD)
         came = jnp.where(column == 1 - part, swap_refs[0][:, there], swap_refs[1][:, there])
@@ -408,6 +428,7 @@
     place_ref,
     full0_ref,
     full1_ref,
+    full2_ref,
     swap_a_ref,
     swap_b_ref,
     kv_a_ref,
@@ -431,7 +452,7 @@
         values = with_ones(near[block, half:])
         bias = bias_ref[span, block]
         for head in range(heads):
-            q = query_of(head, part, place_ref, (full0_ref, full1_ref), (swap_a_ref, swap_b_ref))
+            q = query_of(head, part, place_ref, (full0_ref, full1_ref, full2_ref), (swap_a_ref, swap_b_ref))
             s = scores_of(q, keys, bias)
             top = jnp.max(s, axis=-1, keepdims=True)
             weight = jnp.exp2((s - top) * SHRINK).astype(jnp.bfloat16)
@@ -456,6 +477,7 @@
     place_ref,
     full0_ref,
     full1_ref,
+    full2_ref,
     swap_a_ref,
     swap_b_ref,
     far0_ref,
@@ -490,7 +512,7 @@
         values = with_ones(far[:, half:])
         bias = bias_ref[span, pl.ds(pl.multiple_of(block * rows, rows), rows)]
         for head in range(heads):
-            q = query_of(head, part, place_ref, (full0_ref, full1_ref), (swap_a_ref, swap_b_ref))
+            q = query_of(head, part, place_ref, (full0_ref, full1_ref, full2_ref), (swap_a_ref, swap_b_ref))
             s = scores_of(q, keys, bias)
             before = top_ref[:, head * HEAD : (head + 1) * HEAD]
             top = jnp.maximum(before, jnp.max(s, axis=-1, keepdims=True))
@@ -506,16 +528,23 @@
 
 def attend_kernel(part, place_ref, *refs):
     fulls, swaps, kvs, fars, bias, (out_ref, near, sums, tops) = (
-        refs[0:2], refs[2:4], refs[4:6], refs[6:8], refs[8], refs[9:13]
+        refs[0:3], refs[3:5], refs[5:7], refs[7:9], refs[9], refs[10:14]
     )
     attend_near_kernel(part, place_ref, *fulls, *swaps, *kvs, bias, sums, tops, near)
     attend_far_kernel(part, place_ref, *fulls, *swaps, *fars, bias, sums, tops, out_ref)
 
 
 def attend_share_kernel(part, place_ref, *refs):
-    *before, w0_ref, w1_ref, out_ref, share_ref = refs
+    *before, w0_ref, w1_ref, out_ref, share0_ref, share1_ref = refs
     attend_far_kernel(part, place_ref, *before, out_ref)
-    share_kernel(place_ref, out_ref, w0_ref, w1_ref, share_ref)
+    share_apart_kernel(place_ref, out_ref, w0_ref, w1_ref, share0_ref, share1_ref)
+
+
+def share_apart_kernel(place_ref, a_ref, w0_ref, w1_ref, share0_ref, share1_ref):
+    for w_ref, share_ref in ((w0_ref, share0_ref), (w1_ref, share1_ref)):
+        share_ref[...] = jnp.dot(
+            a_ref[...], w_ref[...], preferred_element_type=jnp.float32
+        ).astype(jnp.bfloat16)
 
 
 def share_two_kernel(place_ref, a_ref, w0_ref, w1_ref, w2_ref, w3_ref, out0_ref, out1_ref):
@@ -533,19 +562,22 @@
         ).astype(jnp.bfloat16)
 
 
-def finish_kernel(
-    relative, place_ref, a_ref, w0_ref, w1_ref, came_ref, x0_ref, x1_ref, *out_refs
-):
+def column_of(turn, turns, core, width):
+    return 0 if len(turns) == 1 else pl.multiple_of((core ^ turn) * width, HEAD)
+
+
+def finish_kernel(relative, turns, place_ref, a_ref, came_ref, x0_ref, x1_ref, *refs):
+    w_refs, out_refs = refs[: len(turns)], refs[len(turns) :]
     chip = place_ref[0] * 2 + place_ref[1]
     core = place_ref[2]
-    width = w0_ref.shape[1]
+    width = w_refs[0].shape[1]
     rows = x0_ref.shape[1]
-    for turn, w_ref in enumerate((w0_ref, w1_ref)):
-        start = pl.multiple_of((core ^ turn) * width, HEAD)
+    for turn, w_ref in zip(turns, w_refs):
+        start = column_of(turn, turns, core, width)
         mixed = jnp.dot(
             a_ref[...], w_ref[...], preferred_element_type=jnp.float32
         ) + came_ref[:, pl.ds(start, width)].astype(jnp.float32)
-        where = pl.multiple_of((chip ^ relative) * 2 * width + start, HEAD)
+        where = pl.multiple_of(((chip ^ relative) * 2 + (core ^ turn)) * width, HEAD)
         for number, x_ref in enumerate((x0_ref, x1_ref)):
             span = slice(number * rows, (number + 1) * rows)
             value = (
@@ -557,40 +589,45 @@
                 out_refs[number][:, pl.ds(start, width)] = value
 
 
+def place_of(cross, chunk, place_ref, wide):
+    relative, turns = chunk
+    core = place_ref[2] ^ cross
+    chip = (place_ref[0] * 2 + place_ref[1]) ^ relative
+    if len(turns) == 2:
+        return core, pl.multiple_of(chip * wide, HEAD)
+    return core, pl.multiple_of((chip * 2 + (core ^ turns[0])) * wide, HEAD)
+
+
 def gather_kernel(place_ref, *refs):
     out_ref = refs[-1]
-    chip = place_ref[0] * 2 + place_ref[1]
-    core = place_ref[2]
     rows = out_ref.shape[1]
-    for turn in range(2):
-        for number, relative in enumerate(EARLY):
-            piece = refs[turn * len(EARLY) + number]
-            width = piece.shape[1]
-            start = pl.multiple_of((chip ^ relative) * width, HEAD)
-            out_ref[core ^ turn, :, pl.ds(start, width)] = piece[
-                turn * rows : (turn + 1) * rows, :
-            ]
-
-
-def gather_last_kernel(place_ref, own_ref, other_ref, before_ref, out_ref, semaphores):
-    width = own_ref.shape[1]
-    start = pl.multiple_of(((place_ref[0] * 2 + place_ref[1]) ^ LATE) * width, HEAD)
-    copies = [
-        pltpu.make_async_copy(
-            piece,
-            out_ref.at[place_ref[2] ^ turn, :, pl.ds(start, width)],
-            semaphores.at[turn],
-        )
-        for turn, piece in enumerate((own_ref, other_ref))
-    ]
+    for cross in range(2):
+        for number, chunk in enumerate(EARLY):
+            piece = refs[cross * len(EARLY) + number]
+            wide = piece.shape[1]
+            core, start = place_of(cross, chunk, place_ref, wide)
+            out_ref[core, :, pl.ds(start, wide)] = piece[cross * rows : (cross + 1) * rows, :]
+
+
+def gather_last_kernel(place_ref, *refs):
+    *pieces, before_ref, out_ref, semaphores = refs
+    copies = []
+    for cross in range(2):
+        for number, chunk in enumerate(LATE):
+            index = cross * len(LATE) + number
+            wide = pieces[index].shape[1]
+            core, start = place_of(cross, chunk, place_ref, wide)
+            there = out_ref.at[core, :, pl.ds(start, wide)]
+            copies.append(pltpu.make_async_copy(pieces[index], there, semaphores.at[index]))
     for copy in copies:
         copy.start()
     for copy in copies:
         copy.wait()
 
 
-EARLY = (2, 0, 3)
-LATE = 1
+BOTH = (0, 1)
+EARLY = ((2, (0,)), (2, (1,)), (0, BOTH))
+LATE = ((3, BOTH), (1, (0,)), (1, (1,)))
 
 
 def on_chip_grid(held, norm_gain, w_qkv, q_gain, k_gain, w_out, lengths):
@@ -662,13 +699,15 @@
     ready = normalise(x_y)
     near1, normed1 = project_own(chip_rows, ready, x_yc, w_c, False)
     o_y = swap(o_there, 4)
-    o_x = swap(o_here, 2)
+    o_x = swap(after(o_here, x_y), 2)
     w_across_c = swap(after(w_across, ready), 1)
 
     def project_far(order, gate):
         return local_kernel(
             functools.partial(project_far_kernel, order),
-            [shape((chip_rows, 4 * part), bf16)] + [shape((chip_rows, pair), bf16)] * 2,
+            [shape((chip_rows, 4 * part), bf16)]
+            + [shape((chip_rows, pair), bf16)] * 2
+            + [shape((chip_rows, 4 * part), bf16)] * order,
             [
                 place,
                 normed0,
@@ -687,21 +726,20 @@
         )
 
     full0, swapping_a, kv_b = project_far(0, near1)
-    full1, swapping_b, kv_a = project_far(1, swapping_a)
+    full1, swapping_b, kv_a, full2 = project_far(1, swapping_a)
     swap_a = swap(swapping_a, 4)
     swap_b = swap(swapping_b, 4)
     far1_a = swap(kv_a, 2, range(4, 8))
-    far1_b = swap(kv_b, 2, range(4, 8))
     far0_a = swap(swap_a, 2, range(4))
-    far0_b = swap(swap_b, 2, range(4))
     o_y_c = swap(after(o_y, kv_a), 1)
 
-    queries = (full0, full1, swap_a, swap_b)
+    queries = (full0, full1, full2, swap_a, swap_b)
     partial_shapes = [shape((chip_rows, 2 * half), f32), shape((chip_rows, half), f32)]
     attend_flops = 2 * own_rows * own_rows * half
     chunk = 2 * w_o.shape[1]
     chunk_flops = own_rows * half * chunk
     chunk_shape = shape((chip_rows, chunk), bf16)
+    half_shape = shape((chip_rows, chunk // 2), bf16)
     rows_shape = shape((chip_rows, half), bf16)
     sums_there = local_kernel(
         functools.partial(attend_near_kernel, 1),
@@ -710,14 +748,16 @@
         [pltpu.VMEM((own_rows, pair), bf16)],
         attend_flops,
     )
-    o_xy = swap(after(o_y, far0_a, far1_a), 2)
-    attended_there, share0 = local_kernel(
+    far1_b = swap(after(kv_b, sums_there[1]), 2, range(4, 8))
+    far0_b = swap(after(swap_b, sums_there[1]), 2, range(4))
+    o_xy = swap(after(o_y, sums_there[1]), 2)
+    o_x_c = swap(after(o_x, sums_there[1]), 1)
+    attended_there, share0, share0_c = local_kernel(
         functools.partial(attend_share_kernel, 1),
-        [rows_shape, chunk_shape],
+        [rows_shape, half_shape, half_shape],
         [place, *queries, far0_a, far1_a, bias, *sums_there, o_here, o_here_c],
         flops=attend_flops // 2 + chunk_flops,
     )
-    o_x_c = swap(after(o_x, kv_a), 1)
 
     ring = [
         (s * devices + i, (s + 1) % sections * devices + i)
@@ -727,20 +767,23 @@
     cross = [(source, target ^ 1) for source, target in ring]
     arrived = {}
 
-    def finish(relative, *pieces):
-        late = relative == LATE
+    def finish(relative, turns, pieces):
+        key = (relative, turns)
+        late = key in LATE
+        taken = [pieces[turn] for turn in turns]
+        wide = sum(piece.shape[1] for piece in taken)
         values = local_kernel(
-            functools.partial(finish_kernel, relative),
-            [shape((rows, chunk), bf16)] * 2 if late else [chunk_shape],
-            [place, attended_here, *pieces, came[relative], kept, x_c],
-            flops=chunk_flops,
+            functools.partial(finish_kernel, relative, turns),
+            [shape((rows, wide), bf16)] * 2 if late else [shape((2 * rows, wide), bf16)],
+            [place, attended_here, came[key], kept, x_c, *taken],
+            flops=own_rows * half * wide,
         )
-        arrived[0, relative] = lax.ppermute(values[0], ("section", "dp"), ring)
+        arrived[0, key] = lax.ppermute(values[0], ("section", "dp"), ring)
         if late:
-            arrived[1, relative] = lax.ppermute(values[1], ("section", "dp"), cross)
+            arrived[1, key] = lax.ppermute(values[1], ("section", "dp"), cross)
         return values[0]
 
-    came = {2: swap(share0, 4)}
+    came = {(2, (0,)): swap(share0, 4), (2, (1,)): swap(share0_c, 4)}
     (attended_here,) = local_kernel(
         functools.partial(attend_kernel, 0),
         [rows_shape],
@@ -755,37 +798,45 @@
         [place, after(attended_there, share0), o_y, o_y_c, o_x, o_x_c],
         flops=2 * chunk_flops,
     )
-    came[0] = swap(share2, 4)
-    came[3] = swap(share1, 4)
+    came[0, BOTH] = swap(share2, 4)
+    came[3, BOTH] = swap(share1, 4)
     attended_here = after(attended_here, share1)
-    last = finish(2, o_y, o_y_c)
+    last = finish(2, (0,), (o_y, o_y_c))
+    attended_here = after(attended_here, last)
+    last = finish(2, (1,), (o_y, o_y_c))
+    attended_here = after(attended_here, last)
     o_xy_c = swap(after(o_xy, last), 1)
-    last = finish(0, o_here, o_here_c)
-    (share3,) = local_kernel(
-        share_kernel,
-        [chunk_shape],
+    last = finish(0, BOTH, (o_here, o_here_c))
+    share3, share3_c = local_kernel(
+        share_apart_kernel,
+        [half_shape, half_shape],
         [place, after(attended_there, last), o_xy, o_xy_c],
         flops=chunk_flops,
     )
-    came[1] = swap(share3, 4)
-    finish(3, o_xy, o_xy_c)
-    last = finish(1, o_x, o_x_c)
-    for relative in EARLY:
-        arrived[1, relative] = swap(after(arrived[0, relative], last), 1)
+    came[1, (0,)] = swap(share3, 4)
+    came[1, (1,)] = swap(share3_c, 4)
+    last = finish(3, BOTH, (o_xy, o_xy_c))
+    attended_here = after(attended_here, last)
+    last = finish(1, (0,), (o_x, o_x_c))
+    attended_here = after(attended_here, last)
+    last = finish(1, (1,), (o_x, o_x_c))
+    for key in EARLY:
+        arrived[1, key] = swap(after(arrived[0, key], last), 1)
     (result,) = local_kernel(
         gather_kernel,
         [shape((micro, rows, width), bf16)],
-        [place, *[arrived[turn, relative] for turn in range(2) for relative in EARLY]],
-    )
+        [place, *[arrived[turn, key] for turn in range(2) for key in EARLY]],
+    )
+    late = [arrived[turn, key] for turn in range(2) for key in LATE]
     result = pl.pallas_call(
         gather_last_kernel,
         out_shape=shape((micro, rows, width), bf16),
-        in_specs=[SMEM, VMEM, VMEM, pl.BlockSpec(memory_space=pl.ANY)],
+        in_specs=[SMEM] + [VMEM] * len(late) + [pl.BlockSpec(memory_space=pl.ANY)],
         out_specs=pl.BlockSpec(memory_space=pl.ANY),
-        scratch_shapes=[pltpu.SemaphoreType.DMA((2,))],
-        input_output_aliases={3: 0},
+        scratch_shapes=[pltpu.SemaphoreType.DMA((len(late),))],
+        input_output_aliases={1 + len(late): 0},
         compiler_params=pltpu.CompilerParams(vmem_limit_bytes=4 * MIB),
-    )(place, arrived[0, LATE], arrived[1, LATE], result)
+    )(place, *late, result)
     return result[None]
 
 

time: 127 us -> 126 us (level)
  waiting for transfers between devices: 58.6 us -> 50.2 us
  starting transfers between devices: 35.8 us -> 41.8 us
  Pallas kernels: 28.6 us -> 29.9 us
    ppermute x5 -> x9, waiting for transfers between devices: 21.5 us -> 9.13 us  [the longest x3 4.84 us: finish(): arrived[1, key] = lax.ppermute(values[1], ('section', 'dp'), cross)]
    ppermute x5 -> x9, starting transfers between devices: 5.9 us -> 11.1 us  [the longest x6 7.02 us: finish(): arrived[0, key] = lax.ppermute(values[0], ('section', 'dp'), ring)]
    ppermute x26 -> x28, waiting for transfers between devices: 37.1 us -> 41 us  [swap(): return lax.ppermute(value, 'dp', [(i, i ^ bits) for i in among])]
    pallas_call x16 -> x18, Pallas kernels: 24.5 us -> 25.7 us  [local_kernel(): pl.pallas_call(body, out_shape=tuple(outs), in_specs=[SMEM] * scalars + [...]
    ppermute x26 -> x28, starting transfers between devices: 29.9 us -> 30.7 us  [swap(): return lax.ppermute(value, 'dp', [(i, i ^ bits) for i in among])]
    unnamed x18 -> x16, local copies, waits for them, and re-layouts: 3.27 us -> 3.26 us
  transfers between devices with their start and end apart: 31 -> 37, of which waited for: 15 -> 14; matrix products, arithmetic and copies ran while one was open for 0% -> 0% of each run, Pallas kernels for 22% -> 23%
where the time goes in v4:
time: 126 us
  waiting for transfers between devices  50.2 us (40%)
  starting transfers between devices  41.8 us (33%)
  Pallas kernels  29.9 us (24%)
  local copies, waits for them, and re-layouts  3.26 us (3%)
    ppermute x28, waiting for transfers between devices, swap(): return lax.ppermute(value, 'dp', [(i, i ^ bits) for i in among])  41 us
    ppermute x28, starting transfers between devices, swap(): return lax.ppermute(value, 'dp', [(i, i ^ bits) for i in among])  30.7 us
    pallas_call x18, Pallas kernels, local_kernel(): pl.pallas_call(body, out_shape=tuple(outs), in_specs=[SMEM] * scalars + [...  25.7 us
    ppermute x6, starting transfers between devices, finish(): arrived[0, key] = lax.ppermute(values[0], ('section', 'dp'), ring)  7.02 us
    ppermute x3, waiting for transfers between devices, finish(): arrived[1, key] = lax.ppermute(values[1], ('section', 'dp'), cross)  4.84 us
    ppermute x6, waiting for transfers between devices, finish(): arrived[0, key] = lax.ppermute(values[0], ('section', 'dp'), ring)  4.29 us
    ppermute x3, starting transfers between devices, finish(): arrived[1, key] = lax.ppermute(values[1], ('section', 'dp'), cross)  4.03 us
    unnamed x16, local copies, waits for them, and re-layouts  3.26 us
  transfers between devices with their start and end apart: 37, of which 14 were waited for; matrix products, arithmetic and copies ran while one was open for 0% of the time, Pallas kernels for 23%

profile of v4, /device:TPU:0, one launch (start us, length us, event | category | flops | bytes accessed | tf_op | source)
XLA Modules:
  0.0 125.6 jit_solution(16673908690949133868)
XLA Ops:
  0.5 2.5 %collective-permute-start.4 = (bf16[320,2048]{1,0:T(8,128)(2,1)}, bf16[320,2048]{1,0:T(8,128)(2,1)S(1)}, u32[]{:S(2)}, u32[]{:S(2)}) collective-permute-start(bf16[320,2048]{1,0:T(8,128)(2,1)} %bitcast.18), channel_id=1, source_target_pairs={{0,2},{1,3},{2,0},{3,1},{4,6},{5,7},{6,4},{7,5},{8,10},{9,11},{10,... | collective-permute-start | bytes 3932168 | tf_op jit(solution)/shard_map/ppermute | solution.py:642
  7.3 2.8 %shard_map.82 = (s32[11]{0:T(128)S(1)}, f32[512,1024]{1,0:T(8,128)S(1)}, f32[512,128]{1,0:T(8,128)S(1)}, f32[512,128]{1,0:T(8,128)S(1)}, bf16[1024,256]{1,0:T(8,128)(2,1)S(1)}, /*index=5*/bf16[1024,256]{1,0:T(8,128)(2,1)S(1)}) custom-call(s32[1]{0:T(128)} %bitcast.here_ref, s32[2,8]{1,0:T(2,128)S(1)} %bitcast.22, f32[1,128]{1,0:T(1,128)S(1)} %copy-done.7, ...), custom_call_target="tpu_custom_call" | custom-call | tf_op jit(solution)/shard_map/pallas_call | solution.py:661
  11.6 2.9 %shard_map.84 = (bf16[256,640]{1,0:T(8,128)(2,1)S(1)}, bf16[256,2048]{1,0:T(8,128)(2,1)S(1)}, bf16[320,2048]{1,0:T(8,128)(2,1)S(1)}) custom-call(s32[11]{0:T(128)S(1)} %get-tuple-element.61.place_ref, bf16[128,2048]{1,0:T(8,128)(2,1)S(1)} %shard_map.83.ready_ref, bf16[2,128,2048]{2,1,0:T(8,128)(2,1)S(1)} %collective-permute-done.x_ref.x1_ref, ...), custom_call_target="tpu_custom_call" | custom-call | flops 671088640 | bytes 7414828 | tf_op jit(solution)/shard_map/pallas_call | solution.py:150
  14.5 14.4 %collective-permute-done.2.x_ref = bf16[2,128,2048]{2,1,0:T(8,128)(2,1)} collective-permute-done((bf16[2,128,2048]{2,1,0:T(8,128)(2,1)}, bf16[2,128,2048]{2,1,0:T(8,128)(2,1)}, u32[]{:S(2)}, u32[]{:S(2)}) %collective-permute-start.2) | collective-permute-done | bytes 1048608 | tf_op jit(solution)/shard_map/ppermute | solution.py:642
  30.4 2.2 %collective-permute-done.4.w_own = bf16[320,2048]{1,0:T(8,128)(2,1)S(1)} collective-permute-done((bf16[320,2048]{1,0:T(8,128)(2,1)}, bf16[320,2048]{1,0:T(8,128)(2,1)S(1)}, u32[]{:S(2)}, u32[]{:S(2)}) %collective-permute-start.4) | collective-permute-done | bytes 1310752 | tf_op jit(solution)/shard_map/ppermute | solution.py:642
  33.1 1.8 %collective-permute-start.13 = (bf16[1024,256]{1,0:T(8,128)(2,1)S(1)}, bf16[1024,256]{1,0:T(8,128)(2,1)S(1)}, u32[]{:S(2)}, u32[]{:S(2)}) collective-permute-start(bf16[1024,256]{1,0:T(8,128)(2,1)S(1)} %get-tuple-element.91), channel_id=1, source_target_pairs={{0,4},{1,5},{2,6},{3,7},{4,0},{5,1},{6,2},{7,3},{8,12},{9,13},{10,... | collective-permute-start | bytes 1572872 | tf_op jit(solution)/shard_map/ppermute | solution.py:642
  37.2 2.0 %shard_map.86 = (bf16[256,640]{1,0:T(8,128)(2,1)S(1)}, bf16[256,2048]{1,0:T(8,128)(2,1)S(1)}) custom-call(s32[11]{0:T(128)S(1)} %get-tuple-element.61.place_ref, bf16[128,2048]{1,0:T(8,128)(2,1)S(1)} %shard_map.85.ready_ref, bf16[2,128,2048]{2,1,0:T(8,128)(2,1)S(1)} %collective-permute-done.3.x_ref, f32[1,2048]{1,0:T(1,128)S(1)} %copy-done.3, ...), custom_call_target="tpu_custom_call" | custom-call | flops 671088640 | bytes 6104108 | tf_op jit(solution)/shard_map/pallas_call | solution.py:150
  39.2 1.9 %shard_map.87 = (bf16[256,1280]{1,0:T(8,128)(2,1)S(1)}, bf16[256,256]{1,0:T(8,128)(2,1)S(1)}, bf16[256,256]{1,0:T(8,128)(2,1)S(1)}) custom-call(s32[11]{0:T(128)S(1)} %get-tuple-element.61.place_ref, bf16[256,2048]{1,0:T(8,128)(2,1)S(1)} %get-tuple-element.64.normed0_ref, bf16[256,2048]{1,0:T(8,128)(2,1)S(1)} %get-tuple-element.68.normed1_ref, ...), custom_call_target="tpu_custom_call" | custom-call | flops 671088640 | bytes 6816812 | tf_op jit(solution)/shard_map/pallas_call | solution.py:150
  41.1 2.0 %shard_map.88 = (bf16[256,1280]{1,0:T(8,128)(2,1)S(1)}, bf16[256,256]{1,0:T(8,128)(2,1)S(1)}, bf16[256,256]{1,0:T(8,128)(2,1)S(1)}, bf16[256,1280]{1,0:T(8,128)(2,1)S(1)}) custom-call(s32[11]{0:T(128)S(1)} %get-tuple-element.61.place_ref, bf16[256,2048]{1,0:T(8,128)(2,1)S(1)} %get-tuple-element.64.normed0_ref, ...), custom_call_target="tpu_custom_call" | custom-call | flops 671088640 | bytes 7472172 | tf_op jit(solution)/shard_map/pallas_call | solution.py:150
  43.2 1.9 %collective-permute-start.7 = (bf16[256,256]{1,0:T(8,128)(2,1)S(1)}, bf16[256,256]{1,0:T(8,128)(2,1)S(1)}, u32[]{:S(2)}, u32[]{:S(2)}) collective-permute-start(bf16[256,256]{1,0:T(8,128)(2,1)S(1)} %get-tuple-element.78), channel_id=1, source_target_pairs={{0,4},{1,5},{2,6},{3,7},{4,0},{5,1},{6,2},{7,3},{8,12},{9,13},{10,... | collective-permute-start | bytes 393224 | tf_op jit(solution)/shard_map/ppermute | solution.py:642
  45.2 2.7 %collective-permute-done.13.w0_ref.refs_0_ = bf16[1024,256]{1,0:T(8,128)(2,1)S(1)} collective-permute-done((bf16[1024,256]{1,0:T(8,128)(2,1)S(1)}, bf16[1024,256]{1,0:T(8,128)(2,1)S(1)}, u32[]{:S(2)}, u32[]{:S(2)}) %collective-permute-start.13) | collective-permute-done | bytes 524320 | tf_op jit(solution)/shard_map/ppermute | solution.py:642
  47.9 2.8 %collective-permute-done.7.swap_b_ref.refs_4_ = bf16[256,256]{1,0:T(8,128)(2,1)S(1)} collective-permute-done((bf16[256,256]{1,0:T(8,128)(2,1)S(1)}, bf16[256,256]{1,0:T(8,128)(2,1)S(1)}, u32[]{:S(2)}, u32[]{:S(2)}) %collective-permute-start.7) | collective-permute-done | bytes 131104 | tf_op jit(solution)/shard_map/ppermute | solution.py:642
  50.7 1.9 %collective-permute-done.6.swap_a_ref.refs_3_ = bf16[256,256]{1,0:T(8,128)(2,1)S(1)} collective-permute-done((bf16[256,256]{1,0:T(8,128)(2,1)S(1)}, bf16[256,256]{1,0:T(8,128)(2,1)S(1)}, u32[]{:S(2)}, u32[]{:S(2)}) %collective-permute-start.6) | collective-permute-done | bytes 131104 | tf_op jit(solution)/shard_map/ppermute | solution.py:642
  54.2 2.6 %collective-permute-start.20 = (bf16[1024,256]{1,0:T(8,128)(2,1)S(1)}, bf16[1024,256]{1,0:T(8,128)(2,1)S(1)}, u32[]{:S(2)}, u32[]{:S(2)}) collective-permute-start(bf16[1024,256]{1,0:T(8,128)(2,1)S(1)} %collective-permute-done.13.w0_ref.refs_0_), channel_id=1, source_target_pairs={{0,2},{1,3},{2,0},{3,1},{4,6},{5,7},{6,4},{7,5},{8,10},{9,11},{10,... | collective-permute-start | bytes 1572872 | tf_op jit(solution)/shard_map/ppermute | solution.py:642
  57.5 2.1 %collective-permute-start.10 = (bf16[256,256]{1,0:T(8,128)(2,1)S(1)}, bf16[256,256]{1,0:T(8,128)(2,1)S(1)}, u32[]{:S(2)}, u32[]{:S(2)}) collective-permute-start(bf16[256,256]{1,0:T(8,128)(2,1)S(1)} %collective-permute-done.6.swap_a_ref.refs_3_), channel_id=1, source_target_pairs={{0,2},{1,3},{2,0},{3,1},{8,10},{9,11},{10,8},{11,9},{16,18},{17,19... | collective-permute-start | bytes 393224 | tf_op jit(solution)/shard_map/ppermute | solution.py:642
  59.6 3.9 %collective-permute-start.8 = (bf16[256,256]{1,0:T(8,128)(2,1)S(1)}, bf16[256,256]{1,0:T(8,128)(2,1)S(1)}, u32[]{:S(2)}, u32[]{:S(2)}) collective-permute-start(bf16[256,256]{1,0:T(8,128)(2,1)S(1)} %collective-permute-done.7.swap_b_ref.refs_4_), channel_id=1, source_target_pairs={{0,2},{1,3},{2,0},{3,1},{8,10},{9,11},{10,8},{11,9},{16,18},{17,19... | collective-permute-start | bytes 393224 | tf_op jit(solution)/shard_map/ppermute | solution.py:642
  63.5 8.9 %collective-permute-done.10.refs_5_ = bf16[256,256]{1,0:T(8,128)(2,1)S(1)} collective-permute-done((bf16[256,256]{1,0:T(8,128)(2,1)S(1)}, bf16[256,256]{1,0:T(8,128)(2,1)S(1)}, u32[]{:S(2)}, u32[]{:S(2)}) %collective-permute-start.10) | collective-permute-done | bytes 131104 | tf_op jit(solution)/shard_map/ppermute | solution.py:642
  73.1 2.3 %shard_map.90 = (bf16[256,1024]{1,0:T(8,128)(2,1)S(1)}, bf16[256,256]{1,0:T(8,128)(2,1)S(1)}, bf16[256,256]{1,0:T(8,128)(2,1)S(1)}) custom-call(s32[11]{0:T(128)S(1)} %get-tuple-element.61.place_ref, bf16[256,1280]{1,0:T(8,128)(2,1)S(1)} %get-tuple-element.73.full0_ref.refs_0_, bf16[256,1280]{1,0:T(8,128)(2,1)S(1)} %get-tuple-element.76.full1_ref.refs_1_, ...), custom_call_target="tpu_custom_call" | custom-call | flops 536870912 | bytes 9568300 | tf_op jit(solution)/shard_map/pallas_call | solution.py:150
  75.3 3.1 %collective-permute-start.17 = (bf16[256,256]{1,0:T(8,128)(2,1)S(1)}, bf16[256,256]{1,0:T(8,128)(2,1)S(1)}, u32[]{:S(2)}, u32[]{:S(2)}) collective-permute-start(bf16[256,256]{1,0:T(8,128)(2,1)S(1)} %get-tuple-element.87), channel_id=1, source_target_pairs={{0,4},{1,5},{2,6},{3,7},{4,0},{5,1},{6,2},{7,3},{8,12},{9,13},{10,... | collective-permute-start | bytes 393224 | tf_op jit(solution)/shard_map/ppermute | solution.py:642
  78.5 2.2 %collective-permute-start.18 = (bf16[256,256]{1,0:T(8,128)(2,1)S(1)}, bf16[256,256]{1,0:T(8,128)(2,1)S(1)}, u32[]{:S(2)}, u32[]{:S(2)}) collective-permute-start(bf16[256,256]{1,0:T(8,128)(2,1)S(1)} %get-tuple-element.98), channel_id=1, source_target_pairs={{0,4},{1,5},{2,6},{3,7},{4,0},{5,1},{6,2},{7,3},{8,12},{9,13},{10,... | collective-permute-start | bytes 393224 | tf_op jit(solution)/shard_map/ppermute | solution.py:642
  80.7 1.7 %shard_map.91.a_ref = bf16[256,1024]{1,0:T(8,128)(2,1)S(1)} custom-call(s32[11]{0:T(128)S(1)} %get-tuple-element.61.place_ref, bf16[256,1280]{1,0:T(8,128)(2,1)S(1)} %get-tuple-element.73.full0_ref.refs_0_, bf16[256,1280]{1,0:T(8,128)(2,1)S(1)} %get-tuple-element.76.full1_ref.refs_1_, bf16[256,1280]{1,0:T(8,128)(2,1)S(1)} %get-tuple-element.77.full2_ref.refs_2_, ...), custom_call_target="tpu_custom_call" | custom-call | flops 1073741824 | bytes 5373996 | tf_op jit(solution)/shard_map/pallas_call | solution.py:150
  85.5 1.7 %collective-permute-start.23 = (bf16[256,512]{1,0:T(8,128)(2,1)S(1)}, bf16[256,512]{1,0:T(8,128)(2,1)S(1)}, u32[]{:S(2)}, u32[]{:S(2)}) collective-permute-start(bf16[256,512]{1,0:T(8,128)(2,1)S(1)} %get-tuple-element.104), channel_id=1, source_target_pairs={{0,4},{1,5},{2,6},{3,7},{4,0},{5,1},{6,2},{7,3},{8,12},{9,13},{10,... | collective-permute-start | bytes 786440 | tf_op jit(solution)/shard_map/ppermute | solution.py:642
  87.6 7.2 %collective-permute-done.23.came_ref = bf16[256,512]{1,0:T(8,128)(2,1)S(1)} collective-permute-done((bf16[256,512]{1,0:T(8,128)(2,1)S(1)}, bf16[256,512]{1,0:T(8,128)(2,1)S(1)}, u32[]{:S(2)}, u32[]{:S(2)}) %collective-permute-start.23) | collective-permute-done | bytes 262176 | tf_op jit(solution)/shard_map/ppermute | solution.py:642
  95.7 1.6 %collective-permute-start.33 = (bf16[256,512]{1,0:T(8,128)(2,1)S(1)}, bf16[256,512]{1,0:T(8,128)(2,1)S(1)}, u32[]{:S(2)}, u32[]{:S(2)}) collective-permute-start(bf16[256,512]{1,0:T(8,128)(2,1)S(1)} %shard_map.96), channel_id=1, source_target_pairs={{0,8},{1,9},{2,10},{3,11},{4,12},{5,13},{6,14},{7,15},{8,16},{9,17... | collective-permute-start | bytes 786440 | tf_op jit(solution)/shard_map/ppermute | solution.py:781
  98.3 1.9 %collective-permute-start.24 = (bf16[256,256]{1,0:T(8,128)(2,1)S(1)}, bf16[256,256]{1,0:T(8,128)(2,1)S(1)}, u32[]{:S(2)}, u32[]{:S(2)}) collective-permute-start(bf16[256,256]{1,0:T(8,128)(2,1)S(1)} %get-tuple-element.106), channel_id=1, source_target_pairs={{0,4},{1,5},{2,6},{3,7},{4,0},{5,1},{6,2},{7,3},{8,12},{9,13},{10,... | collective-permute-start | bytes 393224 | tf_op jit(solution)/shard_map/ppermute | solution.py:642
  100.4 1.6 %collective-permute-start.32 = (bf16[256,256]{1,0:T(8,128)(2,1)S(1)}, bf16[256,256]{1,0:T(8,128)(2,1)S(1)}, u32[]{:S(2)}, u32[]{:S(2)}) collective-permute-start(bf16[256,256]{1,0:T(8,128)(2,1)S(1)} %shard_map.94), channel_id=1, source_target_pairs={{0,8},{1,9},{2,10},{3,11},{4,12},{5,13},{6,14},{7,15},{8,16},{9,17... | collective-permute-start | bytes 393224 | tf_op jit(solution)/shard_map/ppermute | solution.py:781
  102.0 1.6 %collective-permute-start.31 = (bf16[256,256]{1,0:T(8,128)(2,1)S(1)}, bf16[256,256]{1,0:T(8,128)(2,1)S(1)}, u32[]{:S(2)}, u32[]{:S(2)}) collective-permute-start(bf16[256,256]{1,0:T(8,128)(2,1)S(1)} %shard_map.93), channel_id=1, source_target_pairs={{0,8},{1,9},{2,10},{3,11},{4,12},{5,13},{6,14},{7,15},{8,16},{9,17... | collective-permute-start | bytes 393224 | tf_op jit(solution)/shard_map/ppermute | solution.py:781
  106.6 1.6 %collective-permute-start.28 = (bf16[128,512]{1,0:T(8,128)(2,1)S(1)}, bf16[128,512]{1,0:T(8,128)(2,1)S(1)}, u32[]{:S(2)}, u32[]{:S(2)}) collective-permute-start(bf16[128,512]{1,0:T(8,128)(2,1)S(1)} %get-tuple-element.111), channel_id=1, source_target_pairs={{0,9},{1,8},{2,11},{3,10},{4,13},{5,12},{6,15},{7,14},{8,17},{9,16... | collective-permute-start | bytes 393224 | tf_op jit(solution)/shard_map/ppermute | solution.py:783
  108.2 2.3 %collective-permute-done.31.refs_0_ = bf16[256,256]{1,0:T(8,128)(2,1)S(1)} collective-permute-done((bf16[256,256]{1,0:T(8,128)(2,1)S(1)}, bf16[256,256]{1,0:T(8,128)(2,1)S(1)}, u32[]{:S(2)}, u32[]{:S(2)}) %collective-permute-start.31) | collective-permute-done | bytes 131104 | tf_op jit(solution)/shard_map/ppermute | solution.py:781
  111.0 2.6 %collective-permute-done.28.refs_3_ = bf16[128,512]{1,0:T(8,128)(2,1)S(1)} collective-permute-done((bf16[128,512]{1,0:T(8,128)(2,1)S(1)}, bf16[128,512]{1,0:T(8,128)(2,1)S(1)}, u32[]{:S(2)}, u32[]{:S(2)}) %collective-permute-start.28) | collective-permute-done | bytes 131104 | tf_op jit(solution)/shard_map/ppermute | solution.py:783
  116.0 2.2 %collective-permute-start.27 = (bf16[128,256]{1,0:T(8,128)(2,1)S(1)}, bf16[128,256]{1,0:T(8,128)(2,1)S(1)}, u32[]{:S(2)}, u32[]{:S(2)}) collective-permute-start(bf16[128,256]{1,0:T(8,128)(2,1)S(1)} %get-tuple-element.110), channel_id=1, source_target_pairs={{0,8},{1,9},{2,10},{3,11},{4,12},{5,13},{6,14},{7,15},{8,16},{9,17... | collective-permute-start | bytes 196616 | tf_op jit(solution)/shard_map/ppermute | solution.py:781
  122.1 1.9 %collective-permute-done.27.refs_2_ = bf16[128,256]{1,0:T(8,128)(2,1)S(1)} collective-permute-done((bf16[128,256]{1,0:T(8,128)(2,1)S(1)}, bf16[128,256]{1,0:T(8,128)(2,1)S(1)}, u32[]{:S(2)}, u32[]{:S(2)}) %collective-permute-start.27) | collective-permute-done | bytes 65568 | tf_op jit(solution)/shard_map/ppermute | solution.py:781
  (78 shorter events, 30.2 us)
Async XLA Ops:
  0.0 11.6 %collective-permute-start.1 = (bf16[320,2048]{1,0:T(8,128)(2,1)}, bf16[320,2048]{1,0:T(8,128)(2,1)}, u32[]{:S(2)}, u32[]{:S(2)}) collective-permute-start(bf16[320,2048]{1,0:T(8,128)(2,1)} %bitcast.17), channel_id=1, source_target_pairs={{0,1},{1,0},{2,3},{3,2},{4,5},{5,4},{6,7},{7,6},{8,9},{9,8},{10,11... | collective-permute-start | bytes 3932168 | tf_op jit(solution)/shard_map/ppermute | solution.py:642
  0.5 32.1 %collective-permute-start.4 = (bf16[320,2048]{1,0:T(8,128)(2,1)}, bf16[320,2048]{1,0:T(8,128)(2,1)S(1)}, u32[]{:S(2)}, u32[]{:S(2)}) collective-permute-start(bf16[320,2048]{1,0:T(8,128)(2,1)} %bitcast.18), channel_id=1, source_target_pairs={{0,2},{1,3},{2,0},{3,1},{4,6},{5,7},{6,4},{7,5},{8,10},{9,11},{10,... | collective-permute-start | bytes 3932168 | tf_op jit(solution)/shard_map/ppermute | solution.py:642
  3.0 8.5 %collective-permute-start = (bf16[2,128,2048]{2,1,0:T(8,128)(2,1)}, bf16[2,128,2048]{2,1,0:T(8,128)(2,1)S(1)}, u32[]{:S(2)}, u32[]{:S(2)}) collective-permute-start(bf16[2,128,2048]{2,1,0:T(8,128)(2,1)} %bitcast.8), channel_id=1, source_target_pairs={{0,1},{1,0},{2,3},{3,2},{4,5},{5,4},{6,7},{7,6},{8,9},{9,8},{10,11... | collective-permute-start | bytes 3145736 | tf_op jit(solution)/shard_map/ppermute | solution.py:642
  3.2 25.7 %collective-permute-start.2 = (bf16[2,128,2048]{2,1,0:T(8,128)(2,1)}, bf16[2,128,2048]{2,1,0:T(8,128)(2,1)}, u32[]{:S(2)}, u32[]{:S(2)}) collective-permute-start(bf16[2,128,2048]{2,1,0:T(8,128)(2,1)} %bitcast.9), channel_id=1, source_target_pairs={{0,4},{1,5},{2,6},{3,7},{4,0},{5,1},{6,2},{7,3},{8,12},{9,13},{10,... | collective-permute-start | bytes 3145736 | tf_op jit(solution)/shard_map/ppermute | solution.py:642
  32.6 6.5 %collective-permute-start.5 = (bf16[320,2048]{1,0:T(8,128)(2,1)S(1)}, bf16[320,2048]{1,0:T(8,128)(2,1)S(1)}, u32[]{:S(2)}, u32[]{:S(2)}) collective-permute-start(bf16[320,2048]{1,0:T(8,128)(2,1)S(1)} %collective-permute-done.4.w_own), channel_id=1, source_target_pairs={{0,1},{1,0},{2,3},{3,2},{4,5},{5,4},{6,7},{7,6},{8,9},{9,8},{10,11... | collective-permute-start | bytes 3932168 | tf_op jit(solution)/shard_map/ppermute | solution.py:642
  33.1 14.8 %collective-permute-start.13 = (bf16[1024,256]{1,0:T(8,128)(2,1)S(1)}, bf16[1024,256]{1,0:T(8,128)(2,1)S(1)}, u32[]{:S(2)}, u32[]{:S(2)}) collective-permute-start(bf16[1024,256]{1,0:T(8,128)(2,1)S(1)} %get-tuple-element.91), channel_id=1, source_target_pairs={{0,4},{1,5},{2,6},{3,7},{4,0},{5,1},{6,2},{7,3},{8,12},{9,13},{10,... | collective-permute-start | bytes 1572872 | tf_op jit(solution)/shard_map/ppermute | solution.py:642
  34.9 19.2 %collective-permute-start.15 = (bf16[1024,256]{1,0:T(8,128)(2,1)S(1)}, bf16[1024,256]{1,0:T(8,128)(2,1)S(1)}, u32[]{:S(2)}, u32[]{:S(2)}) collective-permute-start(bf16[1024,256]{1,0:T(8,128)(2,1)S(1)} %get-tuple-element.93.refs_10_.refs_0_), channel_id=1, source_target_pairs={{0,2},{1,3},{2,0},{3,1},{4,6},{5,7},{6,4},{7,5},{8,10},{9,11},{10,... | collective-permute-start | bytes 1572872 | tf_op jit(solution)/shard_map/ppermute | solution.py:642
  36.4 21.1 %collective-permute-start.12 = (bf16[1024,256]{1,0:T(8,128)(2,1)S(1)}, bf16[1024,256]{1,0:T(8,128)(2,1)S(1)}, u32[]{:S(2)}, u32[]{:S(2)}) collective-permute-start(bf16[1024,256]{1,0:T(8,128)(2,1)S(1)} %get-tuple-element.93.refs_10_.refs_0_), channel_id=1, source_target_pairs={{0,1},{1,0},{2,3},{3,2},{4,5},{5,4},{6,7},{7,6},{8,9},{9,8},{10,11... | collective-permute-start | bytes 1572872 | tf_op jit(solution)/shard_map/ppermute | solution.py:642
  43.2 7.6 %collective-permute-start.7 = (bf16[256,256]{1,0:T(8,128)(2,1)S(1)}, bf16[256,256]{1,0:T(8,128)(2,1)S(1)}, u32[]{:S(2)}, u32[]{:S(2)}) collective-permute-start(bf16[256,256]{1,0:T(8,128)(2,1)S(1)} %get-tuple-element.78), channel_id=1, source_target_pairs={{0,4},{1,5},{2,6},{3,7},{4,0},{5,1},{6,2},{7,3},{8,12},{9,13},{10,... | collective-permute-start | bytes 393224 | tf_op jit(solution)/shard_map/ppermute | solution.py:642
  45.0 7.6 %collective-permute-start.6 = (bf16[256,256]{1,0:T(8,128)(2,1)S(1)}, bf16[256,256]{1,0:T(8,128)(2,1)S(1)}, u32[]{:S(2)}, u32[]{:S(2)}) collective-permute-start(bf16[256,256]{1,0:T(8,128)(2,1)S(1)} %get-tuple-element.74), channel_id=1, source_target_pairs={{0,4},{1,5},{2,6},{3,7},{4,0},{5,1},{6,2},{7,3},{8,12},{9,13},{10,... | collective-permute-start | bytes 393224 | tf_op jit(solution)/shard_map/ppermute | solution.py:642
  47.9 34.4 %collective-permute-start.14 = (bf16[1024,256]{1,0:T(8,128)(2,1)S(1)}, bf16[1024,256]{1,0:T(8,128)(2,1)S(1)}, u32[]{:S(2)}, u32[]{:S(2)}) collective-permute-start(bf16[1024,256]{1,0:T(8,128)(2,1)S(1)} %collective-permute-done.13.w0_ref.refs_0_), channel_id=1, source_target_pairs={{0,1},{1,0},{2,3},{3,2},{4,5},{5,4},{6,7},{7,6},{8,9},{9,8},{10,11... | collective-permute-start | bytes 1572872 | tf_op jit(solution)/shard_map/ppermute | solution.py:642
  54.2 28.2 %collective-permute-start.16 = (bf16[1024,256]{1,0:T(8,128)(2,1)S(1)}, bf16[1024,256]{1,0:T(8,128)(2,1)S(1)}, u32[]{:S(2)}, u32[]{:S(2)}) collective-permute-start(bf16[1024,256]{1,0:T(8,128)(2,1)S(1)} %collective-permute-done.15.w2_ref.refs_0_), channel_id=1, source_target_pairs={{0,1},{1,0},{2,3},{3,2},{4,5},{5,4},{6,7},{7,6},{8,9},{9,8},{10,11... | collective-permute-start | bytes 1572872 | tf_op jit(solution)/shard_map/ppermute | solution.py:642
  54.2 31.1 %collective-permute-start.20 = (bf16[1024,256]{1,0:T(8,128)(2,1)S(1)}, bf16[1024,256]{1,0:T(8,128)(2,1)S(1)}, u32[]{:S(2)}, u32[]{:S(2)}) collective-permute-start(bf16[1024,256]{1,0:T(8,128)(2,1)S(1)} %collective-permute-done.13.w0_ref.refs_0_), channel_id=1, source_target_pairs={{0,2},{1,3},{2,0},{3,1},{4,6},{5,7},{6,4},{7,5},{8,10},{9,11},{10,... | collective-permute-start | bytes 1572872 | tf_op jit(solution)/shard_map/ppermute | solution.py:642
  57.5 14.9 %collective-permute-start.10 = (bf16[256,256]{1,0:T(8,128)(2,1)S(1)}, bf16[256,256]{1,0:T(8,128)(2,1)S(1)}, u32[]{:S(2)}, u32[]{:S(2)}) collective-permute-start(bf16[256,256]{1,0:T(8,128)(2,1)S(1)} %collective-permute-done.6.swap_a_ref.refs_3_), channel_id=1, source_target_pairs={{0,2},{1,3},{2,0},{3,1},{8,10},{9,11},{10,8},{11,9},{16,18},{17,19... | collective-permute-start | bytes 393224 | tf_op jit(solution)/shard_map/ppermute | solution.py:642
  59.6 15.7 %collective-permute-start.8 = (bf16[256,256]{1,0:T(8,128)(2,1)S(1)}, bf16[256,256]{1,0:T(8,128)(2,1)S(1)}, u32[]{:S(2)}, u32[]{:S(2)}) collective-permute-start(bf16[256,256]{1,0:T(8,128)(2,1)S(1)} %collective-permute-done.7.swap_b_ref.refs_4_), channel_id=1, source_target_pairs={{0,2},{1,3},{2,0},{3,1},{8,10},{9,11},{10,8},{11,9},{16,18},{17,19... | collective-permute-start | bytes 393224 | tf_op jit(solution)/shard_map/ppermute | solution.py:642
  72.4 6.0 %collective-permute-start.9 = (bf16[256,256]{1,0:T(8,128)(2,1)S(1)}, bf16[256,256]{1,0:T(8,128)(2,1)S(1)}, u32[]{:S(2)}, u32[]{:S(2)}) collective-permute-start(bf16[256,256]{1,0:T(8,128)(2,1)S(1)} %get-tuple-element.84.kv_b_ref.refs_6_), channel_id=1, source_target_pairs={{4,6},{5,7},{6,4},{7,5},{12,14},{13,15},{14,12},{15,13},{20,22},{2... | collective-permute-start | bytes 393224 | tf_op jit(solution)/shard_map/ppermute | solution.py:642
  75.3 8.3 %collective-permute-start.17 = (bf16[256,256]{1,0:T(8,128)(2,1)S(1)}, bf16[256,256]{1,0:T(8,128)(2,1)S(1)}, u32[]{:S(2)}, u32[]{:S(2)}) collective-permute-start(bf16[256,256]{1,0:T(8,128)(2,1)S(1)} %get-tuple-element.87), channel_id=1, source_target_pairs={{0,4},{1,5},{2,6},{3,7},{4,0},{5,1},{6,2},{7,3},{8,12},{9,13},{10,... | collective-permute-start | bytes 393224 | tf_op jit(solution)/shard_map/ppermute | solution.py:642
  78.5 6.1 %collective-permute-start.18 = (bf16[256,256]{1,0:T(8,128)(2,1)S(1)}, bf16[256,256]{1,0:T(8,128)(2,1)S(1)}, u32[]{:S(2)}, u32[]{:S(2)}) collective-permute-start(bf16[256,256]{1,0:T(8,128)(2,1)S(1)} %get-tuple-element.98), channel_id=1, source_target_pairs={{0,4},{1,5},{2,6},{3,7},{4,0},{5,1},{6,2},{7,3},{8,12},{9,13},{10,... | collective-permute-start | bytes 393224 | tf_op jit(solution)/shard_map/ppermute | solution.py:642
  85.4 12.0 %collective-permute-start.21 = (bf16[1024,256]{1,0:T(8,128)(2,1)S(1)}, bf16[1024,256]{1,0:T(8,128)(2,1)S(1)}, u32[]{:S(2)}, u32[]{:S(2)}) collective-permute-start(bf16[1024,256]{1,0:T(8,128)(2,1)S(1)} %collective-permute-done.20.refs_0_.w0_ref), channel_id=1, source_target_pairs={{0,1},{1,0},{2,3},{3,2},{4,5},{5,4},{6,7},{7,6},{8,9},{9,8},{10,11... | collective-permute-start | bytes 1572872 | tf_op jit(solution)/shard_map/ppermute | solution.py:642
  85.5 9.2 %collective-permute-start.23 = (bf16[256,512]{1,0:T(8,128)(2,1)S(1)}, bf16[256,512]{1,0:T(8,128)(2,1)S(1)}, u32[]{:S(2)}, u32[]{:S(2)}) collective-permute-start(bf16[256,512]{1,0:T(8,128)(2,1)S(1)} %get-tuple-element.104), channel_id=1, source_target_pairs={{0,4},{1,5},{2,6},{3,7},{4,0},{5,1},{6,2},{7,3},{8,12},{9,13},{10,... | collective-permute-start | bytes 786440 | tf_op jit(solution)/shard_map/ppermute | solution.py:642
  87.2 14.8 %collective-permute-start.19 = (bf16[256,512]{1,0:T(8,128)(2,1)S(1)}, bf16[256,512]{1,0:T(8,128)(2,1)S(1)}, u32[]{:S(2)}, u32[]{:S(2)}) collective-permute-start(bf16[256,512]{1,0:T(8,128)(2,1)S(1)} %get-tuple-element.95), channel_id=1, source_target_pairs={{0,4},{1,5},{2,6},{3,7},{4,0},{5,1},{6,2},{7,3},{8,12},{9,13},{10,... | collective-permute-start | bytes 786440 | tf_op jit(solution)/shard_map/ppermute | solution.py:642
  95.7 10.8 %collective-permute-start.33 = (bf16[256,512]{1,0:T(8,128)(2,1)S(1)}, bf16[256,512]{1,0:T(8,128)(2,1)S(1)}, u32[]{:S(2)}, u32[]{:S(2)}) collective-permute-start(bf16[256,512]{1,0:T(8,128)(2,1)S(1)} %shard_map.96), channel_id=1, source_target_pairs={{0,8},{1,9},{2,10},{3,11},{4,12},{5,13},{6,14},{7,15},{8,16},{9,17... | collective-permute-start | bytes 786440 | tf_op jit(solution)/shard_map/ppermute | solution.py:781
  98.3 6.3 %collective-permute-start.24 = (bf16[256,256]{1,0:T(8,128)(2,1)S(1)}, bf16[256,256]{1,0:T(8,128)(2,1)S(1)}, u32[]{:S(2)}, u32[]{:S(2)}) collective-permute-start(bf16[256,256]{1,0:T(8,128)(2,1)S(1)} %get-tuple-element.106), channel_id=1, source_target_pairs={{0,4},{1,5},{2,6},{3,7},{4,0},{5,1},{6,2},{7,3},{8,12},{9,13},{10,... | collective-permute-start | bytes 393224 | tf_op jit(solution)/shard_map/ppermute | solution.py:642
  100.4 10.1 %collective-permute-start.32 = (bf16[256,256]{1,0:T(8,128)(2,1)S(1)}, bf16[256,256]{1,0:T(8,128)(2,1)S(1)}, u32[]{:S(2)}, u32[]{:S(2)}) collective-permute-start(bf16[256,256]{1,0:T(8,128)(2,1)S(1)} %shard_map.94), channel_id=1, source_target_pairs={{0,8},{1,9},{2,10},{3,11},{4,12},{5,13},{6,14},{7,15},{8,16},{9,17... | collective-permute-start | bytes 393224 | tf_op jit(solution)/shard_map/ppermute | solution.py:781
  102.0 8.5 %collective-permute-start.31 = (bf16[256,256]{1,0:T(8,128)(2,1)S(1)}, bf16[256,256]{1,0:T(8,128)(2,1)S(1)}, u32[]{:S(2)}, u32[]{:S(2)}) collective-permute-start(bf16[256,256]{1,0:T(8,128)(2,1)S(1)} %shard_map.93), channel_id=1, source_target_pairs={{0,8},{1,9},{2,10},{3,11},{4,12},{5,13},{6,14},{7,15},{8,16},{9,17... | collective-permute-start | bytes 393224 | tf_op jit(solution)/shard_map/ppermute | solution.py:781
  106.5 9.5 %collective-permute-start.36 = (bf16[256,512]{1,0:T(8,128)(2,1)S(1)}, bf16[256,512]{1,0:T(8,128)(2,1)S(1)}, u32[]{:S(2)}, u32[]{:S(2)}) collective-permute-start(bf16[256,512]{1,0:T(8,128)(2,1)S(1)} %collective-permute-done.33.refs_2_), channel_id=1, source_target_pairs={{0,1},{1,0},{2,3},{3,2},{4,5},{5,4},{6,7},{7,6},{8,9},{9,8},{10,11... | collective-permute-start | bytes 786440 | tf_op jit(solution)/shard_map/ppermute | solution.py:642
  106.6 7.0 %collective-permute-start.28 = (bf16[128,512]{1,0:T(8,128)(2,1)S(1)}, bf16[128,512]{1,0:T(8,128)(2,1)S(1)}, u32[]{:S(2)}, u32[]{:S(2)}) collective-permute-start(bf16[128,512]{1,0:T(8,128)(2,1)S(1)} %get-tuple-element.111), channel_id=1, source_target_pairs={{0,9},{1,8},{2,11},{3,10},{4,13},{5,12},{6,15},{7,14},{8,17},{9,16... | collective-permute-start | bytes 393224 | tf_op jit(solution)/shard_map/ppermute | solution.py:783
  111.0 8.8 %collective-permute-start.22 = (bf16[128,512]{1,0:T(8,128)(2,1)S(1)}, bf16[128,512]{1,0:T(8,128)(2,1)S(1)}, u32[]{:S(2)}, u32[]{:S(2)}) collective-permute-start(bf16[128,512]{1,0:T(8,128)(2,1)S(1)} %get-tuple-element.102), channel_id=1, source_target_pairs={{0,8},{1,9},{2,10},{3,11},{4,12},{5,13},{6,14},{7,15},{8,16},{9,17... | collective-permute-start | bytes 393224 | tf_op jit(solution)/shard_map/ppermute | solution.py:781
  113.6 7.1 %collective-permute-start.25 = (bf16[128,256]{1,0:T(8,128)(2,1)S(1)}, bf16[128,256]{1,0:T(8,128)(2,1)S(1)}, u32[]{:S(2)}, u32[]{:S(2)}) collective-permute-start(bf16[128,256]{1,0:T(8,128)(2,1)S(1)} %get-tuple-element.107), channel_id=1, source_target_pairs={{0,8},{1,9},{2,10},{3,11},{4,12},{5,13},{6,14},{7,15},{8,16},{9,17... | collective-permute-start | bytes 196616 | tf_op jit(solution)/shard_map/ppermute | solution.py:781
  113.6 7.1 %collective-permute-start.29 = (bf16[128,256]{1,0:T(8,128)(2,1)S(1)}, bf16[128,256]{1,0:T(8,128)(2,1)S(1)}, u32[]{:S(2)}, u32[]{:S(2)}) collective-permute-start(bf16[128,256]{1,0:T(8,128)(2,1)S(1)} %get-tuple-element.112), channel_id=1, source_target_pairs={{0,9},{1,8},{2,11},{3,10},{4,13},{5,12},{6,15},{7,14},{8,17},{9,16... | collective-permute-start | bytes 196616 | tf_op jit(solution)/shard_map/ppermute | solution.py:783
  115.0 7.2 %collective-permute-start.30 = (bf16[128,256]{1,0:T(8,128)(2,1)S(1)}, bf16[128,256]{1,0:T(8,128)(2,1)S(1)}, u32[]{:S(2)}, u32[]{:S(2)}) collective-permute-start(bf16[128,256]{1,0:T(8,128)(2,1)S(1)} %get-tuple-element.113), channel_id=1, source_target_pairs={{0,9},{1,8},{2,11},{3,10},{4,13},{5,12},{6,15},{7,14},{8,17},{9,16... | collective-permute-start | bytes 196616 | tf_op jit(solution)/shard_map/ppermute | solution.py:783
  116.0 8.0 %collective-permute-start.27 = (bf16[128,256]{1,0:T(8,128)(2,1)S(1)}, bf16[128,256]{1,0:T(8,128)(2,1)S(1)}, u32[]{:S(2)}, u32[]{:S(2)}) collective-permute-start(bf16[128,256]{1,0:T(8,128)(2,1)S(1)} %get-tuple-element.110), channel_id=1, source_target_pairs={{0,8},{1,9},{2,10},{3,11},{4,12},{5,13},{6,14},{7,15},{8,16},{9,17... | collective-permute-start | bytes 196616 | tf_op jit(solution)/shard_map/ppermute | solution.py:781
  (13 other events, 39.5 us)

commit v5 on v4

--- a/solution.py
+++ b/solution.py
@@ -535,9 +535,9 @@
 
 
 def attend_share_kernel(part, place_ref, *refs):
-    *before, w0_ref, w1_ref, out_ref, share0_ref, share1_ref = refs
+    *before, w0_ref, w1_ref, out_ref, share_ref = refs
     attend_far_kernel(part, place_ref, *before, out_ref)
-    share_apart_kernel(place_ref, out_ref, w0_ref, w1_ref, share0_ref, share1_ref)
+    share_kernel(place_ref, out_ref, w0_ref, w1_ref, share_ref)
 
 
 def share_apart_kernel(place_ref, a_ref, w0_ref, w1_ref, share0_ref, share1_ref):
@@ -626,7 +626,7 @@
 
 
 BOTH = (0, 1)
-EARLY = ((2, (0,)), (2, (1,)), (0, BOTH))
+EARLY = ((2, BOTH), (0, BOTH))
 LATE = ((3, BOTH), (1, (0,)), (1, (1,)))
 
 
@@ -748,13 +748,13 @@
         [pltpu.VMEM((own_rows, pair), bf16)],
         attend_flops,
     )
-    far1_b = swap(after(kv_b, sums_there[1]), 2, range(4, 8))
-    far0_b = swap(after(swap_b, sums_there[1]), 2, range(4))
+    far1_b = swap(kv_b, 2, range(4, 8))
+    far0_b = swap(swap_b, 2, range(4))
     o_xy = swap(after(o_y, sums_there[1]), 2)
     o_x_c = swap(after(o_x, sums_there[1]), 1)
-    attended_there, share0, share0_c = local_kernel(
+    attended_there, share0 = local_kernel(
         functools.partial(attend_share_kernel, 1),
-        [rows_shape, half_shape, half_shape],
+        [rows_shape, chunk_shape],
         [place, *queries, far0_a, far1_a, bias, *sums_there, o_here, o_here_c],
         flops=attend_flops // 2 + chunk_flops,
     )
@@ -783,7 +783,7 @@
             arrived[1, key] = lax.ppermute(values[1], ("section", "dp"), cross)
         return values[0]
 
-    came = {(2, (0,)): swap(share0, 4), (2, (1,)): swap(share0_c, 4)}
+    came = {(2, BOTH): swap(share0, 4)}
     (attended_here,) = local_kernel(
         functools.partial(attend_kernel, 0),
         [rows_shape],
@@ -801,9 +801,7 @@
     came[0, BOTH] = swap(share2, 4)
     came[3, BOTH] = swap(share1, 4)
     attended_here = after(attended_here, share1)
-    last = finish(2, (0,), (o_y, o_y_c))
-    attended_here = after(attended_here, last)
-    last = finish(2, (1,), (o_y, o_y_c))
+    last = finish(2, BOTH, (o_y, o_y_c))
     attended_here = after(attended_here, last)
     o_xy_c = swap(after(o_xy, last), 1)
     last = finish(0, BOTH, (o_here, o_here_c))

time: 126 us -> 127 us (level)
  waiting for transfers between devices: 50.2 us -> 59.8 us
  starting transfers between devices: 41.8 us -> 34 us
    ppermute x28 -> x26, waiting for transfers between devices: 41 us -> 52.3 us  [swap(): return lax.ppermute(value, 'dp', [(i, i ^ bits) for i in among])]
    ppermute x28 -> x26, starting transfers between devices: 30.7 us -> 25.2 us  [swap(): return lax.ppermute(value, 'dp', [(i, i ^ bits) for i in among])]
    ppermute x6 -> x5, waiting for transfers between devices: 4.29 us -> 2.14 us  [finish(): arrived[0, key] = lax.ppermute(values[0], ('section', 'dp'), ring)]
    ppermute x3, starting transfers between devices: 4.03 us -> 2.39 us  [finish(): arrived[1, key] = lax.ppermute(values[1], ('section', 'dp'), cross)]
    pallas_call x18 -> x17, Pallas kernels: 25.7 us -> 25 us  [local_kernel(): pl.pallas_call(body, out_shape=tuple(outs), in_specs=[SMEM] * scalars + [...]
    ppermute x6 -> x5, starting transfers between devices: 7.02 us -> 6.39 us  [finish(): arrived[0, key] = lax.ppermute(values[0], ('section', 'dp'), ring)]
  transfers between devices with their start and end apart: 37 -> 34, of which waited for: 14 -> 17; matrix products, arithmetic and copies ran while one was open for 0% -> 0% of each run, Pallas kernels for 23% -> 22%
where the time goes in v5:
time: 127 us
  waiting for transfers between devices  59.8 us (47%)
  starting transfers between devices  34 us (27%)
  Pallas kernels  29.2 us (23%)
  local copies, waits for them, and re-layouts  3.26 us (3%)
    ppermute x26, waiting for transfers between devices, swap(): return lax.ppermute(value, 'dp', [(i, i ^ bits) for i in among])  52.3 us
    ppermute x26, starting transfers between devices, swap(): return lax.ppermute(value, 'dp', [(i, i ^ bits) for i in among])  25.2 us
    pallas_call x17, Pallas kernels, local_kernel(): pl.pallas_call(body, out_shape=tuple(outs), in_specs=[SMEM] * scalars + [...  25 us
    ppermute x5, starting transfers between devices, finish(): arrived[0, key] = lax.ppermute(values[0], ('section', 'dp'), ring)  6.39 us
    ppermute x3, waiting for transfers between devices, finish(): arrived[1, key] = lax.ppermute(values[1], ('section', 'dp'), cross)  5.36 us
    unnamed x16, local copies, waits for them, and re-layouts  3.26 us
    pallas_call x1, Pallas kernels, on_chip_grid(): pl.pallas_call(prepare_kernel, out_shape=(shape((11,), jnp.int32), shape(...  2.78 us
  transfers between devices with their start and end apart: 34, of which 17 were waited for; matrix products, arithmetic and copies ran while one was open for 0% of the time, Pallas kernels for 22%

profile of v5, /device:TPU:0, one launch (start us, length us, event | category | flops | bytes accessed | tf_op | source)
XLA Modules:
  0.0 126.7 jit_solution(12730007419642369417)
XLA Ops:
  0.5 2.5 %collective-permute-start.4 = (bf16[320,2048]{1,0:T(8,128)(2,1)}, bf16[320,2048]{1,0:T(8,128)(2,1)S(1)}, u32[]{:S(2)}, u32[]{:S(2)}) collective-permute-start(bf16[320,2048]{1,0:T(8,128)(2,1)} %bitcast.17), channel_id=1, source_target_pairs={{0,2},{1,3},{2,0},{3,1},{4,6},{5,7},{6,4},{7,5},{8,10},{9,11},{10,... | collective-permute-start | bytes 3932168 | tf_op jit(solution)/shard_map/ppermute | solution.py:642
  3.2 1.5 %collective-permute-start.2 = (bf16[2,128,2048]{2,1,0:T(8,128)(2,1)}, bf16[2,128,2048]{2,1,0:T(8,128)(2,1)}, u32[]{:S(2)}, u32[]{:S(2)}) collective-permute-start(bf16[2,128,2048]{2,1,0:T(8,128)(2,1)} %bitcast.9), channel_id=1, source_target_pairs={{0,4},{1,5},{2,6},{3,7},{4,0},{5,1},{6,2},{7,3},{8,12},{9,13},{10,... | collective-permute-start | bytes 3145736 | tf_op jit(solution)/shard_map/ppermute | solution.py:642
  7.3 2.8 %shard_map.82 = (s32[11]{0:T(128)S(1)}, f32[512,1024]{1,0:T(8,128)S(1)}, f32[512,128]{1,0:T(8,128)S(1)}, f32[512,128]{1,0:T(8,128)S(1)}, bf16[1024,256]{1,0:T(8,128)(2,1)S(1)}, /*index=5*/bf16[1024,256]{1,0:T(8,128)(2,1)S(1)}) custom-call(s32[1]{0:T(128)} %bitcast.here_ref, s32[2,8]{1,0:T(2,128)S(1)} %bitcast.21, f32[1,128]{1,0:T(1,128)S(1)} %copy-done.7, ...), custom_call_target="tpu_custom_call" | custom-call | tf_op jit(solution)/shard_map/pallas_call | solution.py:661
  11.6 2.9 %shard_map.84 = (bf16[256,640]{1,0:T(8,128)(2,1)S(1)}, bf16[256,2048]{1,0:T(8,128)(2,1)S(1)}, bf16[320,2048]{1,0:T(8,128)(2,1)S(1)}) custom-call(s32[11]{0:T(128)S(1)} %get-tuple-element.56.place_ref, bf16[128,2048]{1,0:T(8,128)(2,1)S(1)} %shard_map.83.ready_ref, bf16[2,128,2048]{2,1,0:T(8,128)(2,1)S(1)} %collective-permute-done.x_ref.x1_ref, ...), custom_call_target="tpu_custom_call" | custom-call | flops 671088640 | bytes 7414828 | tf_op jit(solution)/shard_map/pallas_call | solution.py:150
  14.5 14.4 %collective-permute-done.2.x_ref = bf16[2,128,2048]{2,1,0:T(8,128)(2,1)} collective-permute-done((bf16[2,128,2048]{2,1,0:T(8,128)(2,1)}, bf16[2,128,2048]{2,1,0:T(8,128)(2,1)}, u32[]{:S(2)}, u32[]{:S(2)}) %collective-permute-start.2) | collective-permute-done | bytes 1048608 | tf_op jit(solution)/shard_map/ppermute | solution.py:642
  30.4 2.2 %collective-permute-done.4.w_own = bf16[320,2048]{1,0:T(8,128)(2,1)S(1)} collective-permute-done((bf16[320,2048]{1,0:T(8,128)(2,1)}, bf16[320,2048]{1,0:T(8,128)(2,1)S(1)}, u32[]{:S(2)}, u32[]{:S(2)}) %collective-permute-start.4) | collective-permute-done | bytes 1310752 | tf_op jit(solution)/shard_map/ppermute | solution.py:642
  33.1 1.8 %collective-permute-start.13 = (bf16[1024,256]{1,0:T(8,128)(2,1)S(1)}, bf16[1024,256]{1,0:T(8,128)(2,1)S(1)}, u32[]{:S(2)}, u32[]{:S(2)}) collective-permute-start(bf16[1024,256]{1,0:T(8,128)(2,1)S(1)} %get-tuple-element.83), channel_id=1, source_target_pairs={{0,4},{1,5},{2,6},{3,7},{4,0},{5,1},{6,2},{7,3},{8,12},{9,13},{10,... | collective-permute-start | bytes 1572872 | tf_op jit(solution)/shard_map/ppermute | solution.py:642
  37.2 2.0 %shard_map.86 = (bf16[256,640]{1,0:T(8,128)(2,1)S(1)}, bf16[256,2048]{1,0:T(8,128)(2,1)S(1)}) custom-call(s32[11]{0:T(128)S(1)} %get-tuple-element.56.place_ref, bf16[128,2048]{1,0:T(8,128)(2,1)S(1)} %shard_map.85.ready_ref, bf16[2,128,2048]{2,1,0:T(8,128)(2,1)S(1)} %collective-permute-done.3.x_ref, f32[1,2048]{1,0:T(1,128)S(1)} %copy-done.3, ...), custom_call_target="tpu_custom_call" | custom-call | flops 671088640 | bytes 6104108 | tf_op jit(solution)/shard_map/pallas_call | solution.py:150
  39.2 1.9 %shard_map.87 = (bf16[256,1280]{1,0:T(8,128)(2,1)S(1)}, bf16[256,256]{1,0:T(8,128)(2,1)S(1)}, bf16[256,256]{1,0:T(8,128)(2,1)S(1)}) custom-call(s32[11]{0:T(128)S(1)} %get-tuple-element.56.place_ref, bf16[256,2048]{1,0:T(8,128)(2,1)S(1)} %get-tuple-element.59.normed0_ref, bf16[256,2048]{1,0:T(8,128)(2,1)S(1)} %get-tuple-element.63.normed1_ref, ...), custom_call_target="tpu_custom_call" | custom-call | flops 671088640 | bytes 6816812 | tf_op jit(solution)/shard_map/pallas_call | solution.py:150
  41.1 2.0 %shard_map.88 = (bf16[256,1280]{1,0:T(8,128)(2,1)S(1)}, bf16[256,256]{1,0:T(8,128)(2,1)S(1)}, bf16[256,256]{1,0:T(8,128)(2,1)S(1)}, bf16[256,1280]{1,0:T(8,128)(2,1)S(1)}) custom-call(s32[11]{0:T(128)S(1)} %get-tuple-element.56.place_ref, bf16[256,2048]{1,0:T(8,128)(2,1)S(1)} %get-tuple-element.59.normed0_ref, ...), custom_call_target="tpu_custom_call" | custom-call | flops 671088640 | bytes 7472172 | tf_op jit(solution)/shard_map/pallas_call | solution.py:150
  43.2 1.9 %collective-permute-start.7 = (bf16[256,256]{1,0:T(8,128)(2,1)S(1)}, bf16[256,256]{1,0:T(8,128)(2,1)S(1)}, u32[]{:S(2)}, u32[]{:S(2)}) collective-permute-start(bf16[256,256]{1,0:T(8,128)(2,1)S(1)} %get-tuple-element.73), channel_id=1, source_target_pairs={{0,4},{1,5},{2,6},{3,7},{4,0},{5,1},{6,2},{7,3},{8,12},{9,13},{10,... | collective-permute-start | bytes 393224 | tf_op jit(solution)/shard_map/ppermute | solution.py:642
  45.2 2.7 %collective-permute-done.13.w0_ref.refs_0_ = bf16[1024,256]{1,0:T(8,128)(2,1)S(1)} collective-permute-done((bf16[1024,256]{1,0:T(8,128)(2,1)S(1)}, bf16[1024,256]{1,0:T(8,128)(2,1)S(1)}, u32[]{:S(2)}, u32[]{:S(2)}) %collective-permute-start.13) | collective-permute-done | bytes 524320 | tf_op jit(solution)/shard_map/ppermute | solution.py:642
  47.9 2.8 %collective-permute-done.7.swap_b_ref.refs_4_ = bf16[256,256]{1,0:T(8,128)(2,1)S(1)} collective-permute-done((bf16[256,256]{1,0:T(8,128)(2,1)S(1)}, bf16[256,256]{1,0:T(8,128)(2,1)S(1)}, u32[]{:S(2)}, u32[]{:S(2)}) %collective-permute-start.7) | collective-permute-done | bytes 131104 | tf_op jit(solution)/shard_map/ppermute | solution.py:642
  50.7 1.9 %collective-permute-done.6.swap_a_ref.refs_3_ = bf16[256,256]{1,0:T(8,128)(2,1)S(1)} collective-permute-done((bf16[256,256]{1,0:T(8,128)(2,1)S(1)}, bf16[256,256]{1,0:T(8,128)(2,1)S(1)}, u32[]{:S(2)}, u32[]{:S(2)}) %collective-permute-start.6) | collective-permute-done | bytes 131104 | tf_op jit(solution)/shard_map/ppermute | solution.py:642
  52.6 1.5 %shard_map.89 = (f32[256,2048]{1,0:T(8,128)S(1)}, f32[256,1024]{1,0:T(8,128)S(1)}) custom-call(s32[11]{0:T(128)S(1)} %get-tuple-element.56.place_ref, bf16[256,1280]{1,0:T(8,128)(2,1)S(1)} %get-tuple-element.68.full0_ref.refs_0_, bf16[256,1280]{1,0:T(8,128)(2,1)S(1)} %get-tuple-element.71.full1_ref.refs_1_, ...), custom_call_target="tpu_custom_call" | custom-call | flops 536870912 | bytes 7733292 | tf_op jit(solution)/shard_map/pallas_call | solution.py:150
  54.9 2.6 %collective-permute-start.19 = (bf16[1024,256]{1,0:T(8,128)(2,1)S(1)}, bf16[1024,256]{1,0:T(8,128)(2,1)S(1)}, u32[]{:S(2)}, u32[]{:S(2)}) collective-permute-start(bf16[1024,256]{1,0:T(8,128)(2,1)S(1)} %collective-permute-done.13.w0_ref.refs_0_), channel_id=1, source_target_pairs={{0,2},{1,3},{2,0},{3,1},{4,6},{5,7},{6,4},{7,5},{8,10},{9,11},{10,... | collective-permute-start | bytes 1572872 | tf_op jit(solution)/shard_map/ppermute | solution.py:642
  57.5 2.1 %collective-permute-start.10 = (bf16[256,256]{1,0:T(8,128)(2,1)S(1)}, bf16[256,256]{1,0:T(8,128)(2,1)S(1)}, u32[]{:S(2)}, u32[]{:S(2)}) collective-permute-start(bf16[256,256]{1,0:T(8,128)(2,1)S(1)} %collective-permute-done.6.swap_a_ref.refs_3_), channel_id=1, source_target_pairs={{0,2},{1,3},{2,0},{3,1},{8,10},{9,11},{10,8},{11,9},{16,18},{17,19... | collective-permute-start | bytes 393224 | tf_op jit(solution)/shard_map/ppermute | solution.py:642
  60.3 12.6 %collective-permute-done.10.refs_5_ = bf16[256,256]{1,0:T(8,128)(2,1)S(1)} collective-permute-done((bf16[256,256]{1,0:T(8,128)(2,1)S(1)}, bf16[256,256]{1,0:T(8,128)(2,1)S(1)}, u32[]{:S(2)}, u32[]{:S(2)}) %collective-permute-start.10) | collective-permute-done | bytes 131104 | tf_op jit(solution)/shard_map/ppermute | solution.py:642
  72.9 3.6 %collective-permute-start.8 = (bf16[256,256]{1,0:T(8,128)(2,1)S(1)}, bf16[256,256]{1,0:T(8,128)(2,1)S(1)}, u32[]{:S(2)}, u32[]{:S(2)}) collective-permute-start(bf16[256,256]{1,0:T(8,128)(2,1)S(1)} %collective-permute-done.7.swap_b_ref.refs_4_), channel_id=1, source_target_pairs={{0,2},{1,3},{2,0},{3,1},{8,10},{9,11},{10,8},{11,9},{16,18},{17,19... | collective-permute-start | bytes 393224 | tf_op jit(solution)/shard_map/ppermute | solution.py:642
  76.5 2.3 %shard_map.90 = (bf16[256,1024]{1,0:T(8,128)(2,1)S(1)}, bf16[256,512]{1,0:T(8,128)(2,1)S(1)}) custom-call(s32[11]{0:T(128)S(1)} %get-tuple-element.56.place_ref, bf16[256,1280]{1,0:T(8,128)(2,1)S(1)} %get-tuple-element.68.full0_ref.refs_0_, bf16[256,1280]{1,0:T(8,128)(2,1)S(1)} %get-tuple-element.71.full1_ref.refs_1_, ...), custom_call_target="tpu_custom_call" | custom-call | flops 536870912 | bytes 9568300 | tf_op jit(solution)/shard_map/pallas_call | solution.py:150
  80.1 1.7 %shard_map.91.a_ref = bf16[256,1024]{1,0:T(8,128)(2,1)S(1)} custom-call(s32[11]{0:T(128)S(1)} %get-tuple-element.56.place_ref, bf16[256,1280]{1,0:T(8,128)(2,1)S(1)} %get-tuple-element.68.full0_ref.refs_0_, bf16[256,1280]{1,0:T(8,128)(2,1)S(1)} %get-tuple-element.71.full1_ref.refs_1_, bf16[256,1280]{1,0:T(8,128)(2,1)S(1)} %get-tuple-element.72.full2_ref.refs_2_, ...), custom_call_target="tpu_custom_call" | custom-call | flops 1073741824 | bytes 5373996 | tf_op jit(solution)/shard_map/pallas_call | solution.py:150
  83.1 3.4 %collective-permute-done.17.came_ref = bf16[256,512]{1,0:T(8,128)(2,1)S(1)} collective-permute-done((bf16[256,512]{1,0:T(8,128)(2,1)S(1)}, bf16[256,512]{1,0:T(8,128)(2,1)S(1)}, u32[]{:S(2)}, u32[]{:S(2)}) %collective-permute-start.17) | collective-permute-done | bytes 262176 | tf_op jit(solution)/shard_map/ppermute | solution.py:642
  87.9 1.7 %collective-permute-start.18 = (bf16[256,512]{1,0:T(8,128)(2,1)S(1)}, bf16[256,512]{1,0:T(8,128)(2,1)S(1)}, u32[]{:S(2)}, u32[]{:S(2)}) collective-permute-start(bf16[256,512]{1,0:T(8,128)(2,1)S(1)} %get-tuple-element.87), channel_id=1, source_target_pairs={{0,4},{1,5},{2,6},{3,7},{4,0},{5,1},{6,2},{7,3},{8,12},{9,13},{10,... | collective-permute-start | bytes 786440 | tf_op jit(solution)/shard_map/ppermute | solution.py:642
  90.4 6.4 %collective-permute-done.22.came_ref = bf16[256,512]{1,0:T(8,128)(2,1)S(1)} collective-permute-done((bf16[256,512]{1,0:T(8,128)(2,1)S(1)}, bf16[256,512]{1,0:T(8,128)(2,1)S(1)}, u32[]{:S(2)}, u32[]{:S(2)}) %collective-permute-start.22) | collective-permute-done | bytes 262176 | tf_op jit(solution)/shard_map/ppermute | solution.py:642
  100.0 1.7 %collective-permute-start.25 = (bf16[256,256]{1,0:T(8,128)(2,1)S(1)}, bf16[256,256]{1,0:T(8,128)(2,1)S(1)}, u32[]{:S(2)}, u32[]{:S(2)}) collective-permute-start(bf16[256,256]{1,0:T(8,128)(2,1)S(1)} %get-tuple-element.99), channel_id=1, source_target_pairs={{0,4},{1,5},{2,6},{3,7},{4,0},{5,1},{6,2},{7,3},{8,12},{9,13},{10,... | collective-permute-start | bytes 393224 | tf_op jit(solution)/shard_map/ppermute | solution.py:642
  103.4 2.6 %collective-permute-done.23.came_ref = bf16[256,256]{1,0:T(8,128)(2,1)S(1)} collective-permute-done((bf16[256,256]{1,0:T(8,128)(2,1)S(1)}, bf16[256,256]{1,0:T(8,128)(2,1)S(1)}, u32[]{:S(2)}, u32[]{:S(2)}) %collective-permute-start.23) | collective-permute-done | bytes 131104 | tf_op jit(solution)/shard_map/ppermute | solution.py:642
  110.2 1.6 %collective-permute-start.21 = (bf16[128,512]{1,0:T(8,128)(2,1)S(1)}, bf16[128,512]{1,0:T(8,128)(2,1)S(1)}, u32[]{:S(2)}, u32[]{:S(2)}) collective-permute-start(bf16[128,512]{1,0:T(8,128)(2,1)S(1)} %get-tuple-element.92), channel_id=1, source_target_pairs={{0,8},{1,9},{2,10},{3,11},{4,12},{5,13},{6,14},{7,15},{8,16},{9,17... | collective-permute-start | bytes 393224 | tf_op jit(solution)/shard_map/ppermute | solution.py:781
  111.8 1.6 %collective-permute-start.24 = (bf16[128,256]{1,0:T(8,128)(2,1)S(1)}, bf16[128,256]{1,0:T(8,128)(2,1)S(1)}, u32[]{:S(2)}, u32[]{:S(2)}) collective-permute-start(bf16[128,256]{1,0:T(8,128)(2,1)S(1)} %get-tuple-element.97), channel_id=1, source_target_pairs={{0,8},{1,9},{2,10},{3,11},{4,12},{5,13},{6,14},{7,15},{8,16},{9,17... | collective-permute-start | bytes 196616 | tf_op jit(solution)/shard_map/ppermute | solution.py:781
  113.4 2.8 %collective-permute-done.27.refs_3_ = bf16[128,512]{1,0:T(8,128)(2,1)S(1)} collective-permute-done((bf16[128,512]{1,0:T(8,128)(2,1)S(1)}, bf16[128,512]{1,0:T(8,128)(2,1)S(1)}, u32[]{:S(2)}, u32[]{:S(2)}) %collective-permute-start.27) | collective-permute-done | bytes 131104 | tf_op jit(solution)/shard_map/ppermute | solution.py:783
  117.3 1.6 %collective-permute-start.26 = (bf16[128,256]{1,0:T(8,128)(2,1)S(1)}, bf16[128,256]{1,0:T(8,128)(2,1)S(1)}, u32[]{:S(2)}, u32[]{:S(2)}) collective-permute-start(bf16[128,256]{1,0:T(8,128)(2,1)S(1)} %get-tuple-element.100), channel_id=1, source_target_pairs={{0,8},{1,9},{2,10},{3,11},{4,12},{5,13},{6,14},{7,15},{8,16},{9,17... | collective-permute-start | bytes 196616 | tf_op jit(solution)/shard_map/ppermute | solution.py:781
  118.9 1.6 %shard_map.99.refs_6_ = bf16[2,128,2048]{2,1,0:T(8,128)(2,1)} custom-call(s32[11]{0:T(128)S(1)} %get-tuple-element.56.place_ref, bf16[256,512]{1,0:T(8,128)(2,1)S(1)} %collective-permute-done.30.refs_0_, bf16[256,512]{1,0:T(8,128)(2,1)S(1)} %collective-permute-done.31.refs_1_, bf16[256,512]{1,0:T(8,128)(2,1)S(1)} %collective-permute-done.32.refs_2_, ...), custom_call_target="tpu_custom_call" | custom-call | bytes 2097196 | tf_op jit(solution)/shard_map/pallas_call | solution.py:150
  123.0 2.1 %collective-permute-done.26.refs_2_ = bf16[128,256]{1,0:T(8,128)(2,1)S(1)} collective-permute-done((bf16[128,256]{1,0:T(8,128)(2,1)S(1)}, bf16[128,256]{1,0:T(8,128)(2,1)S(1)}, u32[]{:S(2)}, u32[]{:S(2)}) %collective-permute-start.26) | collective-permute-done | bytes 65568 | tf_op jit(solution)/shard_map/ppermute | solution.py:781
  (71 shorter events, 29.3 us)
Async XLA Ops:
  0.0 11.6 %collective-permute-start.1 = (bf16[320,2048]{1,0:T(8,128)(2,1)}, bf16[320,2048]{1,0:T(8,128)(2,1)}, u32[]{:S(2)}, u32[]{:S(2)}) collective-permute-start(bf16[320,2048]{1,0:T(8,128)(2,1)} %bitcast.16), channel_id=1, source_target_pairs={{0,1},{1,0},{2,3},{3,2},{4,5},{5,4},{6,7},{7,6},{8,9},{9,8},{10,11... | collective-permute-start | bytes 3932168 | tf_op jit(solution)/shard_map/ppermute | solution.py:642
  0.5 32.1 %collective-permute-start.4 = (bf16[320,2048]{1,0:T(8,128)(2,1)}, bf16[320,2048]{1,0:T(8,128)(2,1)S(1)}, u32[]{:S(2)}, u32[]{:S(2)}) collective-permute-start(bf16[320,2048]{1,0:T(8,128)(2,1)} %bitcast.17), channel_id=1, source_target_pairs={{0,2},{1,3},{2,0},{3,1},{4,6},{5,7},{6,4},{7,5},{8,10},{9,11},{10,... | collective-permute-start | bytes 3932168 | tf_op jit(solution)/shard_map/ppermute | solution.py:642
  3.0 8.5 %collective-permute-start = (bf16[2,128,2048]{2,1,0:T(8,128)(2,1)}, bf16[2,128,2048]{2,1,0:T(8,128)(2,1)S(1)}, u32[]{:S(2)}, u32[]{:S(2)}) collective-permute-start(bf16[2,128,2048]{2,1,0:T(8,128)(2,1)} %bitcast.8), channel_id=1, source_target_pairs={{0,1},{1,0},{2,3},{3,2},{4,5},{5,4},{6,7},{7,6},{8,9},{9,8},{10,11... | collective-permute-start | bytes 3145736 | tf_op jit(solution)/shard_map/ppermute | solution.py:642
  3.2 25.7 %collective-permute-start.2 = (bf16[2,128,2048]{2,1,0:T(8,128)(2,1)}, bf16[2,128,2048]{2,1,0:T(8,128)(2,1)}, u32[]{:S(2)}, u32[]{:S(2)}) collective-permute-start(bf16[2,128,2048]{2,1,0:T(8,128)(2,1)} %bitcast.9), channel_id=1, source_target_pairs={{0,4},{1,5},{2,6},{3,7},{4,0},{5,1},{6,2},{7,3},{8,12},{9,13},{10,... | collective-permute-start | bytes 3145736 | tf_op jit(solution)/shard_map/ppermute | solution.py:642
  32.6 6.5 %collective-permute-start.5 = (bf16[320,2048]{1,0:T(8,128)(2,1)S(1)}, bf16[320,2048]{1,0:T(8,128)(2,1)S(1)}, u32[]{:S(2)}, u32[]{:S(2)}) collective-permute-start(bf16[320,2048]{1,0:T(8,128)(2,1)S(1)} %collective-permute-done.4.w_own), channel_id=1, source_target_pairs={{0,1},{1,0},{2,3},{3,2},{4,5},{5,4},{6,7},{7,6},{8,9},{9,8},{10,11... | collective-permute-start | bytes 3932168 | tf_op jit(solution)/shard_map/ppermute | solution.py:642
  33.1 14.8 %collective-permute-start.13 = (bf16[1024,256]{1,0:T(8,128)(2,1)S(1)}, bf16[1024,256]{1,0:T(8,128)(2,1)S(1)}, u32[]{:S(2)}, u32[]{:S(2)}) collective-permute-start(bf16[1024,256]{1,0:T(8,128)(2,1)S(1)} %get-tuple-element.83), channel_id=1, source_target_pairs={{0,4},{1,5},{2,6},{3,7},{4,0},{5,1},{6,2},{7,3},{8,12},{9,13},{10,... | collective-permute-start | bytes 1572872 | tf_op jit(solution)/shard_map/ppermute | solution.py:642
  34.9 19.2 %collective-permute-start.15 = (bf16[1024,256]{1,0:T(8,128)(2,1)S(1)}, bf16[1024,256]{1,0:T(8,128)(2,1)S(1)}, u32[]{:S(2)}, u32[]{:S(2)}) collective-permute-start(bf16[1024,256]{1,0:T(8,128)(2,1)S(1)} %get-tuple-element.85.refs_10_.refs_0_), channel_id=1, source_target_pairs={{0,2},{1,3},{2,0},{3,1},{4,6},{5,7},{6,4},{7,5},{8,10},{9,11},{10,... | collective-permute-start | bytes 1572872 | tf_op jit(solution)/shard_map/ppermute | solution.py:642
  36.4 21.1 %collective-permute-start.12 = (bf16[1024,256]{1,0:T(8,128)(2,1)S(1)}, bf16[1024,256]{1,0:T(8,128)(2,1)S(1)}, u32[]{:S(2)}, u32[]{:S(2)}) collective-permute-start(bf16[1024,256]{1,0:T(8,128)(2,1)S(1)} %get-tuple-element.85.refs_10_.refs_0_), channel_id=1, source_target_pairs={{0,1},{1,0},{2,3},{3,2},{4,5},{5,4},{6,7},{7,6},{8,9},{9,8},{10,11... | collective-permute-start | bytes 1572872 | tf_op jit(solution)/shard_map/ppermute | solution.py:642
  43.2 7.6 %collective-permute-start.7 = (bf16[256,256]{1,0:T(8,128)(2,1)S(1)}, bf16[256,256]{1,0:T(8,128)(2,1)S(1)}, u32[]{:S(2)}, u32[]{:S(2)}) collective-permute-start(bf16[256,256]{1,0:T(8,128)(2,1)S(1)} %get-tuple-element.73), channel_id=1, source_target_pairs={{0,4},{1,5},{2,6},{3,7},{4,0},{5,1},{6,2},{7,3},{8,12},{9,13},{10,... | collective-permute-start | bytes 393224 | tf_op jit(solution)/shard_map/ppermute | solution.py:642
  45.0 7.6 %collective-permute-start.6 = (bf16[256,256]{1,0:T(8,128)(2,1)S(1)}, bf16[256,256]{1,0:T(8,128)(2,1)S(1)}, u32[]{:S(2)}, u32[]{:S(2)}) collective-permute-start(bf16[256,256]{1,0:T(8,128)(2,1)S(1)} %get-tuple-element.69), channel_id=1, source_target_pairs={{0,4},{1,5},{2,6},{3,7},{4,0},{5,1},{6,2},{7,3},{8,12},{9,13},{10,... | collective-permute-start | bytes 393224 | tf_op jit(solution)/shard_map/ppermute | solution.py:642
  47.9 33.8 %collective-permute-start.14 = (bf16[1024,256]{1,0:T(8,128)(2,1)S(1)}, bf16[1024,256]{1,0:T(8,128)(2,1)S(1)}, u32[]{:S(2)}, u32[]{:S(2)}) collective-permute-start(bf16[1024,256]{1,0:T(8,128)(2,1)S(1)} %collective-permute-done.13.w0_ref.refs_0_), channel_id=1, source_target_pairs={{0,1},{1,0},{2,3},{3,2},{4,5},{5,4},{6,7},{7,6},{8,9},{9,8},{10,11... | collective-permute-start | bytes 1572872 | tf_op jit(solution)/shard_map/ppermute | solution.py:642
  54.2 27.6 %collective-permute-start.16 = (bf16[1024,256]{1,0:T(8,128)(2,1)S(1)}, bf16[1024,256]{1,0:T(8,128)(2,1)S(1)}, u32[]{:S(2)}, u32[]{:S(2)}) collective-permute-start(bf16[1024,256]{1,0:T(8,128)(2,1)S(1)} %collective-permute-done.15.w2_ref.refs_0_), channel_id=1, source_target_pairs={{0,1},{1,0},{2,3},{3,2},{4,5},{5,4},{6,7},{7,6},{8,9},{9,8},{10,11... | collective-permute-start | bytes 1572872 | tf_op jit(solution)/shard_map/ppermute | solution.py:642
  54.9 32.5 %collective-permute-start.19 = (bf16[1024,256]{1,0:T(8,128)(2,1)S(1)}, bf16[1024,256]{1,0:T(8,128)(2,1)S(1)}, u32[]{:S(2)}, u32[]{:S(2)}) collective-permute-start(bf16[1024,256]{1,0:T(8,128)(2,1)S(1)} %collective-permute-done.13.w0_ref.refs_0_), channel_id=1, source_target_pairs={{0,2},{1,3},{2,0},{3,1},{4,6},{5,7},{6,4},{7,5},{8,10},{9,11},{10,... | collective-permute-start | bytes 1572872 | tf_op jit(solution)/shard_map/ppermute | solution.py:642
  57.5 15.4 %collective-permute-start.10 = (bf16[256,256]{1,0:T(8,128)(2,1)S(1)}, bf16[256,256]{1,0:T(8,128)(2,1)S(1)}, u32[]{:S(2)}, u32[]{:S(2)}) collective-permute-start(bf16[256,256]{1,0:T(8,128)(2,1)S(1)} %collective-permute-done.6.swap_a_ref.refs_3_), channel_id=1, source_target_pairs={{0,2},{1,3},{2,0},{3,1},{8,10},{9,11},{10,8},{11,9},{16,18},{17,19... | collective-permute-start | bytes 393224 | tf_op jit(solution)/shard_map/ppermute | solution.py:642
  59.6 19.2 %collective-permute-start.9 = (bf16[256,256]{1,0:T(8,128)(2,1)S(1)}, bf16[256,256]{1,0:T(8,128)(2,1)S(1)}, u32[]{:S(2)}, u32[]{:S(2)}) collective-permute-start(bf16[256,256]{1,0:T(8,128)(2,1)S(1)} %get-tuple-element.75.kv_b_ref.refs_6_), channel_id=1, source_target_pairs={{4,6},{5,7},{6,4},{7,5},{12,14},{13,15},{14,12},{15,13},{20,22},{2... | collective-permute-start | bytes 393224 | tf_op jit(solution)/shard_map/ppermute | solution.py:642
  72.9 7.2 %collective-permute-start.8 = (bf16[256,256]{1,0:T(8,128)(2,1)S(1)}, bf16[256,256]{1,0:T(8,128)(2,1)S(1)}, u32[]{:S(2)}, u32[]{:S(2)}) collective-permute-start(bf16[256,256]{1,0:T(8,128)(2,1)S(1)} %collective-permute-done.7.swap_b_ref.refs_4_), channel_id=1, source_target_pairs={{0,2},{1,3},{2,0},{3,1},{8,10},{9,11},{10,8},{11,9},{16,18},{17,19... | collective-permute-start | bytes 393224 | tf_op jit(solution)/shard_map/ppermute | solution.py:642
  78.8 7.6 %collective-permute-start.17 = (bf16[256,512]{1,0:T(8,128)(2,1)S(1)}, bf16[256,512]{1,0:T(8,128)(2,1)S(1)}, u32[]{:S(2)}, u32[]{:S(2)}) collective-permute-start(bf16[256,512]{1,0:T(8,128)(2,1)S(1)} %get-tuple-element.80), channel_id=1, source_target_pairs={{0,4},{1,5},{2,6},{3,7},{4,0},{5,1},{6,2},{7,3},{8,12},{9,13},{10,... | collective-permute-start | bytes 786440 | tf_op jit(solution)/shard_map/ppermute | solution.py:642
  87.5 11.2 %collective-permute-start.20 = (bf16[1024,256]{1,0:T(8,128)(2,1)S(1)}, bf16[1024,256]{1,0:T(8,128)(2,1)S(1)}, u32[]{:S(2)}, u32[]{:S(2)}) collective-permute-start(bf16[1024,256]{1,0:T(8,128)(2,1)S(1)} %collective-permute-done.19.refs_0_.w0_ref), channel_id=1, source_target_pairs={{0,1},{1,0},{2,3},{3,2},{4,5},{5,4},{6,7},{7,6},{8,9},{9,8},{10,11... | collective-permute-start | bytes 1572872 | tf_op jit(solution)/shard_map/ppermute | solution.py:642
  87.6 9.2 %collective-permute-start.22 = (bf16[256,512]{1,0:T(8,128)(2,1)S(1)}, bf16[256,512]{1,0:T(8,128)(2,1)S(1)}, u32[]{:S(2)}, u32[]{:S(2)}) collective-permute-start(bf16[256,512]{1,0:T(8,128)(2,1)S(1)} %get-tuple-element.94), channel_id=1, source_target_pairs={{0,4},{1,5},{2,6},{3,7},{4,0},{5,1},{6,2},{7,3},{8,12},{9,13},{10,... | collective-permute-start | bytes 786440 | tf_op jit(solution)/shard_map/ppermute | solution.py:642
  87.9 14.5 %collective-permute-start.18 = (bf16[256,512]{1,0:T(8,128)(2,1)S(1)}, bf16[256,512]{1,0:T(8,128)(2,1)S(1)}, u32[]{:S(2)}, u32[]{:S(2)}) collective-permute-start(bf16[256,512]{1,0:T(8,128)(2,1)S(1)} %get-tuple-element.87), channel_id=1, source_target_pairs={{0,4},{1,5},{2,6},{3,7},{4,0},{5,1},{6,2},{7,3},{8,12},{9,13},{10,... | collective-permute-start | bytes 786440 | tf_op jit(solution)/shard_map/ppermute | solution.py:642
  89.6 18.7 %collective-permute-start.30 = (bf16[256,512]{1,0:T(8,128)(2,1)S(1)}, bf16[256,512]{1,0:T(8,128)(2,1)S(1)}, u32[]{:S(2)}, u32[]{:S(2)}) collective-permute-start(bf16[256,512]{1,0:T(8,128)(2,1)S(1)} %shard_map.93), channel_id=1, source_target_pairs={{0,8},{1,9},{2,10},{3,11},{4,12},{5,13},{6,14},{7,15},{8,16},{9,17... | collective-permute-start | bytes 786440 | tf_op jit(solution)/shard_map/ppermute | solution.py:781
  97.8 10.6 %collective-permute-start.31 = (bf16[256,512]{1,0:T(8,128)(2,1)S(1)}, bf16[256,512]{1,0:T(8,128)(2,1)S(1)}, u32[]{:S(2)}, u32[]{:S(2)}) collective-permute-start(bf16[256,512]{1,0:T(8,128)(2,1)S(1)} %shard_map.95), channel_id=1, source_target_pairs={{0,8},{1,9},{2,10},{3,11},{4,12},{5,13},{6,14},{7,15},{8,16},{9,17... | collective-permute-start | bytes 786440 | tf_op jit(solution)/shard_map/ppermute | solution.py:781
  99.6 6.4 %collective-permute-start.23 = (bf16[256,256]{1,0:T(8,128)(2,1)S(1)}, bf16[256,256]{1,0:T(8,128)(2,1)S(1)}, u32[]{:S(2)}, u32[]{:S(2)}) collective-permute-start(bf16[256,256]{1,0:T(8,128)(2,1)S(1)} %get-tuple-element.96), channel_id=1, source_target_pairs={{0,4},{1,5},{2,6},{3,7},{4,0},{5,1},{6,2},{7,3},{8,12},{9,13},{10,... | collective-permute-start | bytes 393224 | tf_op jit(solution)/shard_map/ppermute | solution.py:642
  100.0 7.5 %collective-permute-start.25 = (bf16[256,256]{1,0:T(8,128)(2,1)S(1)}, bf16[256,256]{1,0:T(8,128)(2,1)S(1)}, u32[]{:S(2)}, u32[]{:S(2)}) collective-permute-start(bf16[256,256]{1,0:T(8,128)(2,1)S(1)} %get-tuple-element.99), channel_id=1, source_target_pairs={{0,4},{1,5},{2,6},{3,7},{4,0},{5,1},{6,2},{7,3},{8,12},{9,13},{10,... | collective-permute-start | bytes 393224 | tf_op jit(solution)/shard_map/ppermute | solution.py:642
  108.4 7.8 %collective-permute-start.32 = (bf16[256,512]{1,0:T(8,128)(2,1)S(1)}, bf16[256,512]{1,0:T(8,128)(2,1)S(1)}, u32[]{:S(2)}, u32[]{:S(2)}) collective-permute-start(bf16[256,512]{1,0:T(8,128)(2,1)S(1)} %collective-permute-done.30.refs_0_), channel_id=1, source_target_pairs={{0,1},{1,0},{2,3},{3,2},{4,5},{5,4},{6,7},{7,6},{8,9},{9,8},{10,11... | collective-permute-start | bytes 786440 | tf_op jit(solution)/shard_map/ppermute | solution.py:642
  108.4 8.9 %collective-permute-start.33 = (bf16[256,512]{1,0:T(8,128)(2,1)S(1)}, bf16[256,512]{1,0:T(8,128)(2,1)S(1)}, u32[]{:S(2)}, u32[]{:S(2)}) collective-permute-start(bf16[256,512]{1,0:T(8,128)(2,1)S(1)} %collective-permute-done.31.refs_1_), channel_id=1, source_target_pairs={{0,1},{1,0},{2,3},{3,2},{4,5},{5,4},{6,7},{7,6},{8,9},{9,8},{10,11... | collective-permute-start | bytes 786440 | tf_op jit(solution)/shard_map/ppermute | solution.py:642
  108.9 7.2 %collective-permute-start.27 = (bf16[128,512]{1,0:T(8,128)(2,1)S(1)}, bf16[128,512]{1,0:T(8,128)(2,1)S(1)}, u32[]{:S(2)}, u32[]{:S(2)}) collective-permute-start(bf16[128,512]{1,0:T(8,128)(2,1)S(1)} %get-tuple-element.101), channel_id=1, source_target_pairs={{0,9},{1,8},{2,11},{3,10},{4,13},{5,12},{6,15},{7,14},{8,17},{9,16... | collective-permute-start | bytes 393224 | tf_op jit(solution)/shard_map/ppermute | solution.py:783
  110.2 10.3 %collective-permute-start.21 = (bf16[128,512]{1,0:T(8,128)(2,1)S(1)}, bf16[128,512]{1,0:T(8,128)(2,1)S(1)}, u32[]{:S(2)}, u32[]{:S(2)}) collective-permute-start(bf16[128,512]{1,0:T(8,128)(2,1)S(1)} %get-tuple-element.92), channel_id=1, source_target_pairs={{0,8},{1,9},{2,10},{3,11},{4,12},{5,13},{6,14},{7,15},{8,16},{9,17... | collective-permute-start | bytes 393224 | tf_op jit(solution)/shard_map/ppermute | solution.py:781
  111.8 9.9 %collective-permute-start.24 = (bf16[128,256]{1,0:T(8,128)(2,1)S(1)}, bf16[128,256]{1,0:T(8,128)(2,1)S(1)}, u32[]{:S(2)}, u32[]{:S(2)}) collective-permute-start(bf16[128,256]{1,0:T(8,128)(2,1)S(1)} %get-tuple-element.97), channel_id=1, source_target_pairs={{0,8},{1,9},{2,10},{3,11},{4,12},{5,13},{6,14},{7,15},{8,16},{9,17... | collective-permute-start | bytes 196616 | tf_op jit(solution)/shard_map/ppermute | solution.py:781
  116.2 5.5 %collective-permute-start.28 = (bf16[128,256]{1,0:T(8,128)(2,1)S(1)}, bf16[128,256]{1,0:T(8,128)(2,1)S(1)}, u32[]{:S(2)}, u32[]{:S(2)}) collective-permute-start(bf16[128,256]{1,0:T(8,128)(2,1)S(1)} %get-tuple-element.102), channel_id=1, source_target_pairs={{0,9},{1,8},{2,11},{3,10},{4,13},{5,12},{6,15},{7,14},{8,17},{9,16... | collective-permute-start | bytes 196616 | tf_op jit(solution)/shard_map/ppermute | solution.py:783
  116.2 6.9 %collective-permute-start.29 = (bf16[128,256]{1,0:T(8,128)(2,1)S(1)}, bf16[128,256]{1,0:T(8,128)(2,1)S(1)}, u32[]{:S(2)}, u32[]{:S(2)}) collective-permute-start(bf16[128,256]{1,0:T(8,128)(2,1)S(1)} %get-tuple-element.103), channel_id=1, source_target_pairs={{0,9},{1,8},{2,11},{3,10},{4,13},{5,12},{6,15},{7,14},{8,17},{9,16... | collective-permute-start | bytes 196616 | tf_op jit(solution)/shard_map/ppermute | solution.py:783
  117.3 7.8 %collective-permute-start.26 = (bf16[128,256]{1,0:T(8,128)(2,1)S(1)}, bf16[128,256]{1,0:T(8,128)(2,1)S(1)}, u32[]{:S(2)}, u32[]{:S(2)}) collective-permute-start(bf16[128,256]{1,0:T(8,128)(2,1)S(1)} %get-tuple-element.100), channel_id=1, source_target_pairs={{0,8},{1,9},{2,10},{3,11},{4,12},{5,13},{6,14},{7,15},{8,16},{9,17... | collective-permute-start | bytes 196616 | tf_op jit(solution)/shard_map/ppermute | solution.py:781
  (10 other events, 29.2 us)
